TPU v7x, 32 devices: a whole 2x2x4 slice. The times are simulated.
32 devices in a mesh: group: 2 (over y), region: 4 (over z), probe: 4 (over x, core).
Axes of the slice: x: 2, y: 2, z: 4, core: 2. Of those that a mesh axis runs over, the one named last changes fastest.
Arguments:
- object_slices: float32 [4, 2, 512, 256], P('group', None, 'region', 'probe'), parts along dimension 0, may hold values from -4 to 4
- probe: float32 [4, 128, 128], P('group'), parts along dimension 0, may hold values from -6 to 6
- intensity: float32 [4, 16, 256, 128], P('region', 'probe', 'group'), parts along dimension 2, may hold values from 0.5 to 4
- positions: int32 [4, 16, 4], P('region', 'probe', 'group'), parts along dimension 2, may hold values from 0 to 255, as said below
Outputs:
- gradient: float32 [4, 2, 512, 256], P('group', None, 'region', 'probe'), parts along dimension 0
There are 2 independent parts, one for each index of `group`. A program takes and returns all parts, laid end to end along the dimension named above; each array names one. Nothing has to cross between parts.
Inputs may be any that keep to these rules, and one draw needn't show every extreme that they name: `positions`: entry 0 is a row offset below 128 within the region's rows, entry 1 a column offset below 256.
All inputs are finite; a program needn't handle non-finite values.
Results may differ from a plain program's by a relative error of at most 0.00014.
Values sent between devices are 32-bit elements; how exact they have to be, the bound alone decides.
No kernel may reach another device: no remote copies, remote signals or barrier semaphores. Data moves between devices by JAX's collectives and lax.ppermute only.
A program may use at most 64 MiB of HBM per device.

v0:
```python
import math

import jax
import jax.numpy as jnp
from jax import lax
from jax.sharding import PartitionSpec as P


def from_behind(block, axis, distance):
    devices = range(lax.axis_size(axis))
    route = [((i - distance) % len(devices), i) for i in devices]
    return lax.ppermute(block, axis, route)


def propagator(window):
    indices = lax.iota(jnp.int32, window)
    frequency = (
        jnp.where(indices < window // 2, indices, indices - window).astype(jnp.float32) / window
    )
    phases = -60.0 * (frequency[:, None] ** 2 + frequency[None, :] ** 2)
    return (jnp.cos(phases), jnp.sin(phases))


def dft_tables(window):
    indices = lax.iota(jnp.int32, window)
    product = indices[:, None] * indices[None, :] % window
    angles = product.astype(jnp.float32) * (2.0 * math.pi / window)
    norm_factor = 1.0 / math.sqrt(window)
    return (jnp.cos(angles) * norm_factor, -jnp.sin(angles) * norm_factor)


def left_mul(matrix, values):
    return jnp.einsum("ab,nbc->nac", matrix, values, precision=lax.Precision.HIGHEST)


def right_mul(values, matrix):
    return jnp.einsum("nab,bc->nac", values, matrix, precision=lax.Precision.HIGHEST)


def transform(real_part, imag_part, table_re, table_im):
    left_re = left_mul(table_re, real_part) - left_mul(table_im, imag_part)
    left_im = left_mul(table_re, imag_part) + left_mul(table_im, real_part)
    out_re = right_mul(left_re, table_re) - right_mul(left_im, table_im)
    out_im = right_mul(left_re, table_im) + right_mul(left_im, table_re)
    return (out_re, out_im)


def fresnel(real_part, imag_part, table_re, table_im, kernel_re, kernel_im):
    spec_re, spec_im = transform(real_part, imag_part, table_re, table_im)
    moved_re = kernel_re * spec_re - kernel_im * spec_im
    moved_im = kernel_re * spec_im + kernel_im * spec_re
    return transform(moved_re, moved_im, table_re, -table_im)


def body(object_slices, probe, intensity, positions):
    layers = object_slices.shape[0]
    band_rows = object_slices.shape[2]
    window = probe.shape[1]
    item_count = positions.shape[1]
    lower_band = from_behind(object_slices, "region", -1)
    extended = jnp.concatenate([object_slices, lower_band], axis=2)
    whole_band = lax.all_gather(extended, "probe", axis=3, tiled=True)
    columns = whole_band.shape[3]
    padded = jnp.concatenate([whole_band, whole_band[:, :, :, :window]], axis=3)
    row_offsets = positions[0, :, 0]
    col_offsets = positions[0, :, 1]
    anchor = jnp.zeros((), jnp.int32)

    def cut_patch(row_offset, col_offset):
        return lax.dynamic_slice(
            padded, (anchor, anchor, row_offset, col_offset), (layers, 2, window, window)
        )

    patches = jax.vmap(cut_patch)(row_offsets, col_offsets)
    table_re, table_im = dft_tables(window)
    kernel_re, kernel_im = propagator(window)
    wave_re = jnp.broadcast_to(probe[0], (item_count, window, window))
    wave_im = jnp.broadcast_to(probe[1], (item_count, window, window))
    incident = []
    exit_re = wave_re
    exit_im = wave_im
    for layer in range(layers):
        incident.append((wave_re, wave_im))
        patch_re = patches[:, layer, 0]
        patch_im = patches[:, layer, 1]
        exit_re = wave_re * patch_re - wave_im * patch_im
        exit_im = wave_re * patch_im + wave_im * patch_re
        if layer < layers - 1:
            wave_re, wave_im = fresnel(exit_re, exit_im, table_re, table_im, kernel_re, kernel_im)
    far_re, far_im = transform(exit_re, exit_im, table_re, table_im)
    misfit = far_re * far_re + far_im * far_im - intensity[0]
    back_re, back_im = transform(misfit * far_re, misfit * far_im, table_re, -table_im)
    layer_grads = [None] * layers
    for layer in reversed(range(layers)):
        wave_re, wave_im = incident[layer]
        layer_grads[layer] = jnp.stack(
            [wave_re * back_re + wave_im * back_im, wave_re * back_im - wave_im * back_re], axis=1
        )
        if layer > 0:
            patch_re = patches[:, layer, 0]
            patch_im = patches[:, layer, 1]
            carried_re = patch_re * back_re + patch_im * back_im
            carried_im = patch_re * back_im - patch_im * back_re
            back_re, back_im = fresnel(
                carried_re, carried_im, table_re, table_im, kernel_re, -kernel_im
            )
    gradients = jnp.stack(layer_grads, axis=1)

    def deposit(position, accumulated):
        corner = (anchor, anchor, row_offsets[position], col_offsets[position])
        current = lax.dynamic_slice(accumulated, corner, (layers, 2, window, window))
        return lax.dynamic_update_slice(accumulated, current + gradients[position], corner)

    accumulated = lax.fori_loop(0, item_count, deposit, jnp.zeros(padded.shape, jnp.float32))
    wrapped_head = accumulated[:, :, :, :window] + accumulated[:, :, :, columns:]
    folded = jnp.concatenate([wrapped_head, accumulated[:, :, :, window:columns]], axis=3)
    upper_part = folded[:, :, :band_rows]
    spill_rows = folded[:, :, band_rows:]
    returned = from_behind(spill_rows, "region", 1)
    summed = lax.psum_scatter(upper_part + returned, "probe", scatter_dimension=3, tiled=True)
    return summed * (1.0 / (item_count * lax.axis_size("probe")))


def solution(mesh):
    placed = (
        P("group", None, "region", "probe"),
        P("group", None, None),
        P("region", "probe", "group", None),
        P("region", "probe", "group"),
    )
    return jax.shard_map(
        body,
        mesh=mesh,
        in_specs=placed,
        out_specs=P("group", None, "region", "probe"),
        check_vma=False,
    )
```

profile of v0, /device:TPU:0, one launch (start us, length us, event | category | flops | bytes accessed | tf_op | source)
XLA Modules:
  0.0 167.3 jit_solution(12580402229340034271)
XLA Ops:
  6.5 1.0 copy.66
  7.5 5.1 %collective-permute-start = (f32[2,2,128,64]{2,1,0,3:T(2,128)S(1)}, f32[2,2,128,64]{2,1,0,3:T(2,128)S(1)}, u32[]{:S(2)}, u32[]{:S(2)}) collective-permute-start(f32[2,2,128,64]{2,1,0,3:T(2,128)S(1)} %copy.66), channel_id=1, source_target_pairs={{4,0},{8,4},{12,8},{0,12},{5,1},{9,5},{13,9},{1,13},{6,2},{10,6},{... | collective-permute-start | bytes 393224 | tf_op jit(solution)/shard_map/ppermute | solution.py:12
  12.6 2.8 %collective-permute-done = f32[2,2,128,64]{2,1,0,3:T(2,128)S(1)} collective-permute-done((f32[2,2,128,64]{2,1,0,3:T(2,128)S(1)}, f32[2,2,128,64]{2,1,0,3:T(2,128)S(1)}, u32[]{:S(2)}, u32[]{:S(2)}) %collective-permute-start) | collective-permute-done | bytes 131104 | tf_op jit(solution)/shard_map/ppermute | solution.py:12
  15.4 0.8 pad_maximum_fusion.3
  16.3 0.8 compare_select_fusion.1
  17.3 0.8 slice_bitcast_fusion.2
  18.1 0.9 slice_bitcast_fusion.1
  19.3 15.7 %all-gather.2.cloned.1.call-done = f32[2,2,256,256]{2,1,0,3:T(2,128)} async-done(((f32[2,2,256,64]{2,1,0,3:T(2,128)}), f32[2,2,256,256]{2,1,0,3:T(2,128)}) %all-gather.2.cloned.1.call-update) | async-done | bytes 1048592 | tf_op jit(solution)/shard_map/all_gather | solution.py:62
  35.1 1.3 slice.77
  37.1 10.2 %while.15 = (s32[]{:T(128)}, f32[2,2,256,384]{2,1,0,3:T(2,128)S(1)}, s32[4,4]{1,0:T(4,128)S(1)}, f32[4,2,2,128,128]{4,3,0,2,1:T(8,128)S(1)}, s32[]{:T(128)}) while((s32[]{:T(128)}, f32[2,2,256,384]{2,1,0,3:T(2,128)S(1)}, s32[4,4]{1,0:T(4,128)S(1)}, f32[4,2,2,128,128]{4,3,0,2,1:T(8,128)S(1)}, s32[]{:T(128)}) %tuple.59), condition=%wide.while_cond, body=%wide.while_body.sunk | while | flops 2 | bytes 1572997 | solution.py:70
  37.8 1.6 constant_dynamic-slice_fusion.8
  40.3 1.6 constant_dynamic-slice_fusion.8
  42.8 1.6 constant_dynamic-slice_fusion.8
  45.3 1.6 constant_dynamic-slice_fusion.8
  47.3 0.8 fusion.95
  48.1 0.8 fusion.11
  48.9 0.7 fusion.50
  50.3 0.8 fusion.91
  51.1 0.8 fusion.10
  52.6 0.7 convolution_subtract_fusion.10
  53.3 0.8 fusion.84
  54.1 0.8 fusion.88
  54.9 0.8 fusion.9
  57.1 0.8 fusion.8
  58.6 0.9 fusion.15
  64.7 0.7 convolution_subtract_fusion.6
  65.4 0.8 fusion.70
  66.2 0.8 fusion.74
  67.0 0.8 fusion.5
  69.2 0.8 fusion.4
  70.7 1.2 fusion.17
  77.0 0.7 convolution_subtract_fusion.2
  77.7 0.8 fusion.56
  78.5 0.8 fusion.60
  79.3 0.8 fusion.1
  81.5 0.8 fusion
  82.3 0.9 convolution_add_fusion
  83.2 0.7 add_bitcast_fusion.1
  84.3 35.6 %while.14 = (s32[]{:T(128)}, f32[2,2,256,384]{2,3,1,0:T(8,128)S(1)}, s32[4]{0:T(128)S(1)}, s32[4]{0:T(128)S(1)}, f32[4,2,2,128,128]{4,3,0,2,1:T(8,128)S(1)}, /*index=5*/s32[]{:T(128)}, s32[]{:T(128)}, s32[]{:T(128)}, s32[]{:T(128)}) while((s32[]{:T(128)}, f32[2,2,256,384]{2,3,1,0:T(8,128)S(1)}, s32[4]{0:T(128)S(1)}, s32[4]{0:T(128)S(1)}, ...), condition=%wide.region_1.2_spmd, body=%wide.region_0.1_spmd.sunk | while | flops 65544 | bytes 2883793 | solution.py:114
  90.2 3.0 %dynamic_update_slice.8 = f32[2,2,256,384]{2,3,1,0:T(8,128)S(1)} dynamic-update-slice(f32[2,2,256,384]{2,3,1,0:T(8,128)S(1)} %get-tuple-element.251, f32[2,2,128,128]{2,3,1,0:T(8,128)S(1)} %copy.185, s32[]{:T(128)} %constant.61.clone.1..sunk, s32[]{:T(128)} %constant.61.clone.1..sunk, s32[]{:T(128)S(6)} %select_n.346, s32[]{:T(128)S(6)} %select_n.347) | dynamic-update-slice | bytes 524292 | tf_op jit(solution)/shard_map/while/body/eval_jaxpr/dynamic_update_slice | solution.py:112
  99.3 1.8 %dynamic_update_slice.8 = f32[2,2,256,384]{2,3,1,0:T(8,128)S(1)} dynamic-update-slice(f32[2,2,256,384]{2,3,1,0:T(8,128)S(1)} %get-tuple-element.251, f32[2,2,128,128]{2,3,1,0:T(8,128)S(1)} %copy.185, s32[]{:T(128)} %constant.61.clone.1..sunk, s32[]{:T(128)} %constant.61.clone.1..sunk, s32[]{:T(128)S(6)} %select_n.346, s32[]{:T(128)S(6)} %select_n.347) | dynamic-update-slice | bytes 524292 | tf_op jit(solution)/shard_map/while/body/eval_jaxpr/dynamic_update_slice | solution.py:112
  107.1 3.4 %dynamic_update_slice.8 = f32[2,2,256,384]{2,3,1,0:T(8,128)S(1)} dynamic-update-slice(f32[2,2,256,384]{2,3,1,0:T(8,128)S(1)} %get-tuple-element.251, f32[2,2,128,128]{2,3,1,0:T(8,128)S(1)} %copy.185, s32[]{:T(128)} %constant.61.clone.1..sunk, s32[]{:T(128)} %constant.61.clone.1..sunk, s32[]{:T(128)S(6)} %select_n.346, s32[]{:T(128)S(6)} %select_n.347) | dynamic-update-slice | bytes 524292 | tf_op jit(solution)/shard_map/while/body/eval_jaxpr/dynamic_update_slice | solution.py:112
  116.5 3.4 %dynamic_update_slice.8 = f32[2,2,256,384]{2,3,1,0:T(8,128)S(1)} dynamic-update-slice(f32[2,2,256,384]{2,3,1,0:T(8,128)S(1)} %get-tuple-element.251, f32[2,2,128,128]{2,3,1,0:T(8,128)S(1)} %copy.185, s32[]{:T(128)} %constant.61.clone.1..sunk, s32[]{:T(128)} %constant.61.clone.1..sunk, s32[]{:T(128)S(6)} %select_n.346, s32[]{:T(128)S(6)} %select_n.347) | dynamic-update-slice | bytes 524292 | tf_op jit(solution)/shard_map/while/body/eval_jaxpr/dynamic_update_slice | solution.py:112
  120.1 3.2 %collective-permute-start.1 = (f32[2,2,128,256]{2,3,1,0:T(8,128)S(1)}, f32[2,2,128,256]{2,3,1,0:T(8,128)S(1)}, u32[]{:S(2)}, u32[]{:S(2)}) collective-permute-start(f32[2,2,128,256]{2,3,1,0:T(8,128)S(1)} %pad_maximum_fusion.2), channel_id=1, source_target_pairs={{12,0},{0,4},{4,8},{8,12},{13,1},{1,5},{5,9},{9,13},{14,2},{2,6},{... | collective-permute-start | bytes 1572872 | tf_op jit(solution)/shard_map/ppermute | solution.py:12
  123.2 14.4 %collective-permute-done.1 = f32[2,2,128,256]{2,3,1,0:T(8,128)S(1)} collective-permute-done((f32[2,2,128,256]{2,3,1,0:T(8,128)S(1)}, f32[2,2,128,256]{2,3,1,0:T(8,128)S(1)}, u32[]{:S(2)}, u32[]{:S(2)}) %collective-permute-start.1) | collective-permute-done | bytes 524320 | tf_op jit(solution)/shard_map/ppermute | solution.py:12
  137.6 0.9 fusion.13
  138.5 20.2 %reduce-scatter.2.cloned.1.call-done = f32[2,2,128,64]{2,3,1,0:T(8,128)} async-done(((f32[2,2,128,256]{2,3,1,0:T(8,128)}), f32[2,2,128,64]{2,3,1,0:T(8,128)}) %reduce-scatter.2.cloned.1.call-update) | async-done | bytes 131088 | tf_op jit(solution)/shard_map/reduce_scatter | solution.py:120
  158.7 1.6 broadcast_multiply_fusion
  (86 shorter events, 29.7 us)
Async XLA Ops:
  6.5 28.5 %all-gather.2.cloned.1.call-start = ((), (), s32[]{:S(2)}) async-start(), calls=%async_computation.1 | async-start | bytes 1310720 | tf_op jit(solution)/shard_map/all_gather | solution.py:62
  7.5 7.9 %collective-permute-start = (f32[2,2,128,64]{2,1,0,3:T(2,128)S(1)}, f32[2,2,128,64]{2,1,0,3:T(2,128)S(1)}, u32[]{:S(2)}, u32[]{:S(2)}) collective-permute-start(f32[2,2,128,64]{2,1,0,3:T(2,128)S(1)} %copy.66), channel_id=1, source_target_pairs={{4,0},{8,4},{12,8},{0,12},{5,1},{9,5},{13,9},{1,13},{6,2},{10,6},{... | collective-permute-start | bytes 393224 | tf_op jit(solution)/shard_map/ppermute | solution.py:12
  16.3 142.4 %reduce-scatter.2.cloned.1.call-start = ((), (), s32[]{:S(2)}) async-start(), calls=%async_computation.2 | async-start | bytes 655360 | tf_op jit(solution)/shard_map/reduce_scatter | solution.py:120
  35.1 1.4 copy-start.1
  62.5 2.9 %copy-start = (f32[1,4,128,128]{3,2,1,0:T(8,128)S(1)}, f32[1,4,128,128]{3,2,1,0:T(8,128)}, u32[]{:S(2)}) copy-start(f32[1,4,128,128]{3,2,1,0:T(8,128)} %param.8) | copy-start | bytes 786436
  120.1 17.5 %collective-permute-start.1 = (f32[2,2,128,256]{2,3,1,0:T(8,128)S(1)}, f32[2,2,128,256]{2,3,1,0:T(8,128)S(1)}, u32[]{:S(2)}, u32[]{:S(2)}) collective-permute-start(f32[2,2,128,256]{2,3,1,0:T(8,128)S(1)} %pad_maximum_fusion.2), channel_id=1, source_target_pairs={{12,0},{0,4},{4,8},{8,12},{13,1},{1,5},{5,9},{9,13},{14,2},{2,6},{... | collective-permute-start | bytes 1572872 | tf_op jit(solution)/shard_map/ppermute | solution.py:12
Sparse Core Ops, SparseCore 0:
  16.4 18.6 all-gather.1
  138.6 20.0 reduce-scatter.1
where the time goes:
time: 170 us; the launch traced here: 167 us
  waiting for transfers between devices  53.1 us (31%)
  matrix products  36.3 us (21%)
  local copies, waits for them, and re-layouts  32.8 us (19%)
  loops' own time  17.2 us (10%)
  between operations  14 us (8%)
  starting transfers between devices  8.31 us (5%)
  other arithmetic  5.53 us (3%)
    reduce_scatter x1, waiting for transfers between devices, body(): lax.psum_scatter(upper_part + returned, 'probe', scatter_dimension=3, til...  20.2 us
    dot_general x24, matrix products, right_mul(): jnp.einsum('nab,bc->nac', values, matrix, precision=lax.Precision.HIGHEST)  18.2 us
    dot_general x24, matrix products, left_mul(): jnp.einsum('ab,nbc->nac', matrix, values, precision=lax.Precision.HIGHEST)  18.1 us
    ppermute x2, waiting for transfers between devices, from_behind(): return lax.ppermute(block, axis, route)  17.1 us
    another operation x1, loops' own time, body(): lax.fori_loop(0, item_count, deposit, jnp.zeros(padded.shape, jnp.float32))  16.8 us
    all_gather x1, waiting for transfers between devices, body(): whole_band = lax.all_gather(extended, 'probe', axis=3, tiled=True)  15.7 us
    dynamic_update_slice x8, local copies, waits for them, and re-layouts, deposit(): lax.dynamic_update_slice(accumulated, current + gradients[position], corner)  12.3 us
    gather x20, local copies, waits for them, and re-layouts  9.85 us
  transfers between devices with their start and end apart: 4, of which 4 were waited for; matrix products, arithmetic and copies ran while one was open for 2% of the time, Pallas kernels for 0%

commit v1 on v0

v1 whole, which is shorter than its diff:
```python
import math

import jax
import jax.numpy as jnp
import ml_dtypes
import numpy as np
from jax import lax
from jax.experimental import pallas as pl
from jax.experimental.pallas import tpu as pltpu
from jax.sharding import PartitionSpec as P

CORES = 2
HALF = 64


def split_table(table):
    high = table.astype(ml_dtypes.bfloat16)
    low = (table - high.astype(np.float64)).astype(ml_dtypes.bfloat16)
    return np.stack([high, low])


def tables(window):
    indices = np.arange(window)
    angles = 2.0 * math.pi * ((indices[:, None] * indices[None, :]) % window) / window
    real, imag = np.cos(angles) / math.sqrt(window), -np.sin(angles) / math.sqrt(window)
    direct = np.block([[real, imag], [-imag, real]])
    inverse = np.block([[real, -imag], [imag, real]])
    frequency = np.where(indices < window // 2, indices, indices - window) / window
    phases = -60.0 * (frequency[:, None] ** 2 + frequency[None, :] ** 2)
    kernel = np.stack([np.cos(phases), np.sin(phases)]).astype(np.float32)
    return split_table(direct), split_table(inverse), kernel


def split(values):
    high = values.astype(jnp.bfloat16)
    low = (values - high.astype(jnp.float32)).astype(jnp.bfloat16)
    return high, low


def times_right(values, table_ref):
    high, low = split(values)
    table = jnp.concatenate([table_ref[0], table_ref[0], table_ref[1]], axis=0)
    stacked = jnp.concatenate([high, low, high], axis=1)
    return jnp.dot(stacked, table, preferred_element_type=jnp.float32)


def times_left(table_ref, values):
    high, low = split(values)
    table = jnp.concatenate([table_ref[0], table_ref[0], table_ref[1]], axis=1)
    stacked = jnp.concatenate([high, low, high], axis=0)
    return jnp.dot(table, stacked, preferred_element_type=jnp.float32)


def to_rows(values, window):
    count = values.shape[0] // window
    return jnp.concatenate(
        [
            jnp.concatenate(
                [values[n * window : (n + 1) * window, c * window : (c + 1) * window] for n in range(count)],
                axis=1,
            )
            for c in range(2)
        ],
        axis=0,
    )


def part(values, n, c, window):
    return values[c * window : (c + 1) * window, n * window : (n + 1) * window]


def join(pairs):
    return jnp.concatenate(
        [jnp.concatenate([re for re, _ in pairs], axis=1), jnp.concatenate([im for _, im in pairs], axis=1)],
        axis=0,
    )


def lanes(pairs):
    return jnp.concatenate([jnp.concatenate([re, im], axis=1) for re, im in pairs], axis=0)


def fresnel(pairs, direct_ref, inverse_ref, kernel_ref, sign, window):
    count = len(pairs)
    half = to_rows(times_right(lanes(pairs), direct_ref), window)
    spec = times_left(inverse_ref, half)
    k_re, k_im = kernel_ref[0], kernel_ref[1]
    if sign < 0:
        k_im = -k_im
    moved = []
    for n in range(count):
        re, im = part(spec, n, 0, window), part(spec, n, 1, window)
        moved.append((k_re * re - k_im * im, k_re * im + k_im * re))
    half = to_rows(times_right(lanes(moved), inverse_ref), window)
    wave = times_left(direct_ref, half)
    return [(part(wave, n, 0, window), part(wave, n, 1, window)) for n in range(count)]


def assemble(unit_refs, field_ref, ring, rows, window):
    me = lax.axis_index("probe")
    x, core = me // CORES, me % CORES
    lane = lax.broadcasted_iota(jnp.int32, (rows, window), 1)
    at = 0
    for step in range(ring):
        tile = lax.rem(x + step, ring)
        for band in range(2):
            mine, other = unit_refs[at][...], unit_refs[at + 1][...]
            at += 2
            even = jnp.where(core == 0, mine, other)
            odd = jnp.where(core == 0, other, mine)
            where = pl.ds(band * rows, rows)
            field_ref[tile, 0, where, :] = jnp.where(lane < HALF, even, pltpu.roll(odd, HALF, 1))
            field_ref[tile, 1, where, :] = jnp.where(lane < HALF, pltpu.roll(even, HALF, 1), odd)


def cut(field_ref, position_ref, n, ring, window):
    row, column = position_ref[0, n, 0], position_ref[0, n, 1]
    tile = column // window
    after = jnp.where(tile + 1 == ring, 0, tile + 1)
    offset = column - tile * window
    back = lax.rem(window - offset, window)
    lane = lax.broadcasted_iota(jnp.int32, (window, window), 1)
    halves = []
    for c in range(2):
        first = pltpu.roll(field_ref[tile, c, pl.ds(row, window), :], back, 1)
        second = pltpu.roll(field_ref[after, c, pl.ds(row, window), :], back, 1)
        halves.append(jnp.where(lane < window - offset, first, second))
    return tuple(halves)


def deposit(total_ref, position_ref, n, pair, ring, window):
    row, column = position_ref[0, n, 0], position_ref[0, n, 1]
    tile = column // window
    after = jnp.where(tile + 1 == ring, 0, tile + 1)
    offset = column - tile * window
    lane = lax.broadcasted_iota(jnp.int32, (window, window), 1)
    rows = pl.ds(row, window)
    for c in range(2):
        turned = pltpu.roll(pair[c], offset, 1)
        total_ref[tile, c, rows, :] += jnp.where(lane >= offset, turned, 0.0)
        total_ref[after, c, rows, :] += jnp.where(lane < offset, turned, 0.0)


def hand_out(total_ref, keep_ref, send_ref, ring, rows, window):
    me = lax.axis_index("probe")
    x, core = me // CORES, me % CORES
    lane = lax.broadcasted_iota(jnp.int32, (rows, window), 1)
    for step in range(ring):
        tile = lax.rem(x + step, ring)
        for band in range(2):
            where = pl.ds(band * rows, rows)
            re, im = total_ref[tile, 0, where, :], total_ref[tile, 1, where, :]
            even = jnp.where(lane < HALF, re, pltpu.roll(im, HALF, 1))
            odd = jnp.where(lane < HALF, pltpu.roll(re, HALF, 1), im)
            keep_ref[2 * step + band] = jnp.where(core == 0, even, odd)
            send_ref[2 * step + band] = jnp.where(core == 0, odd, even)


def pack_kernel(object_ref, *out_refs):
    for layer, out_ref in enumerate(out_refs):
        out_ref[...] = jnp.concatenate([object_ref[layer, 0], object_ref[layer, 1]], axis=1)


def first_kernel(ring, rows, window, position_ref, probe_ref, direct_ref, inverse_ref, kernel_ref, *rest):
    unit_refs, wave_ref, field_ref = rest[:-2], rest[-2], rest[-1]
    count = position_ref.shape[1]
    assemble(unit_refs, field_ref, ring, rows, window)
    probe_re, probe_im = probe_ref[0], probe_ref[1]
    exits = []
    for n in range(count):
        re, im = cut(field_ref, position_ref, n, ring, window)
        exits.append((probe_re * re - probe_im * im, probe_re * im + probe_im * re))
    waves = fresnel(exits, direct_ref, inverse_ref, kernel_ref, 1, window)
    for n, (re, im) in enumerate(waves):
        wave_ref[n, 0] = re
        wave_ref[n, 1] = im


def middle_kernel(ring, rows, window, position_ref, wave_ref, intensity_ref, direct_ref, inverse_ref, *rest):
    unit_refs, (carried_ref, keep_ref, send_ref, field_ref, total_ref) = rest[:-5], rest[-5:]
    count = position_ref.shape[1]
    assemble(unit_refs, field_ref, ring, rows, window)
    total_ref[...] = jnp.zeros_like(total_ref)
    exits, patches = [], []
    for n in range(count):
        re, im = cut(field_ref, position_ref, n, ring, window)
        w_re, w_im = wave_ref[n, 0], wave_ref[n, 1]
        patches.append((re, im))
        exits.append((w_re * re - w_im * im, w_re * im + w_im * re))
    far = times_left(inverse_ref, to_rows(times_right(lanes(exits), direct_ref), window))
    scaled = []
    for n in range(count):
        re, im = part(far, n, 0, window), part(far, n, 1, window)
        misfit = re * re + im * im - intensity_ref[0, n]
        scaled.append((misfit * re, misfit * im))
    back = times_left(direct_ref, to_rows(times_right(lanes(scaled), inverse_ref), window))
    for n in range(count):
        b_re, b_im = part(back, n, 0, window), part(back, n, 1, window)
        w_re, w_im = wave_ref[n, 0], wave_ref[n, 1]
        p_re, p_im = patches[n]
        carried_ref[n, 0] = p_re * b_re + p_im * b_im
        carried_ref[n, 1] = p_re * b_im - p_im * b_re
        gradient = (w_re * b_re + w_im * b_im, w_re * b_im - w_im * b_re)
        deposit(total_ref, position_ref, n, gradient, ring, window)
    hand_out(total_ref, keep_ref, send_ref, ring, rows, window)


def last_kernel(
    ring, rows, window, position_ref, probe_ref, carried_ref, direct_ref, inverse_ref, kernel_ref, keep_ref, send_ref, total_ref
):
    count = position_ref.shape[1]
    total_ref[...] = jnp.zeros_like(total_ref)
    carried = [(carried_ref[n, 0], carried_ref[n, 1]) for n in range(count)]
    backs = fresnel(carried, direct_ref, inverse_ref, kernel_ref, -1, window)
    probe_re, probe_im = probe_ref[0], probe_ref[1]
    for n, (b_re, b_im) in enumerate(backs):
        gradient = (probe_re * b_re + probe_im * b_im, probe_re * b_im - probe_im * b_re)
        deposit(total_ref, position_ref, n, gradient, ring, window)
    hand_out(total_ref, keep_ref, send_ref, ring, rows, window)


def sum_kernel(scale, per_layer, *refs):
    out_ref = refs[-1]
    for layer in range(out_ref.shape[0]):
        terms = refs[layer * per_layer : (layer + 1) * per_layer]
        total = terms[0][...]
        for term in terms[1:]:
            total += term[...]
        total *= scale
        out_ref[layer, 0] = total[:, :HALF]
        out_ref[layer, 1] = total[:, HALF:]


VMEM = pl.BlockSpec(memory_space=pltpu.VMEM)
SMEM = pl.BlockSpec(memory_space=pltpu.SMEM)
PARAMS = pltpu.CompilerParams(vmem_limit_bytes=40 << 20)


def cost(flops, moved):
    return pl.CostEstimate(flops=flops, bytes_accessed=moved, transcendentals=0)


def body(object_slices, probe, intensity, positions):
    layers, _, rows, _ = object_slices.shape
    window = probe.shape[1]
    count = positions.shape[1]
    regions = lax.axis_size("region")
    devices = lax.axis_size("probe")
    ring = devices // CORES
    direct, inverse, kernel = (jnp.asarray(t) for t in tables(window))
    unit = jax.ShapeDtypeStruct((rows, window), jnp.float32)
    waves = jax.ShapeDtypeStruct((count, 2, window, window), jnp.float32)
    units = jax.ShapeDtypeStruct((2 * ring, rows, window), jnp.float32)
    field = pltpu.VMEM((ring, 2, 2 * rows, window), jnp.float32)
    dft_flops = count * 2 * 3 * 2 * window * (2 * window) ** 2

    def swap(value):
        return lax.ppermute(value, "probe", [(i, i ^ 1) for i in range(devices)])

    def route(step, band):
        pairs = []
        for r in range(regions):
            for d in range(devices):
                there = ((d // CORES + step) % ring) * CORES + d % CORES
                pairs.append((r * devices + d, ((r + band) % regions) * devices + there))
        return pairs

    def fetch(value, step, band):
        return lax.ppermute(value, ("region", "probe"), [(b, a) for a, b in route(step, band)])

    def give(value, step, band):
        return lax.ppermute(value, ("region", "probe"), route(step, band))

    steps = [(step, band) for step in range(ring) for band in range(2)]

    def gathered(tile):
        out = []
        for step, band in steps:
            here = tile if step == band == 0 else fetch(tile, step, band)
            out += [here, swap(here)]
        return out

    packed = pl.pallas_call(
        pack_kernel, out_shape=[unit] * layers, in_specs=[VMEM], out_specs=[VMEM] * layers, compiler_params=PARAMS
    )(object_slices)
    unit_sets = [gathered(tile) for tile in packed]
    wave = pl.pallas_call(
        lambda *refs: first_kernel(ring, rows, window, *refs),
        out_shape=waves,
        in_specs=[SMEM] + [VMEM] * (4 + 4 * ring),
        out_specs=VMEM,
        scratch_shapes=[field],
        compiler_params=PARAMS,
        cost_estimate=cost(2 * dft_flops, 1 << 20),
    )(positions, probe, direct, inverse, kernel, *unit_sets[0])
    carried, keep_1, send_1 = pl.pallas_call(
        lambda *refs: middle_kernel(ring, rows, window, *refs),
        out_shape=[waves, units, units],
        in_specs=[SMEM] + [VMEM] * (4 + 4 * ring),
        out_specs=[VMEM] * 3,
        scratch_shapes=[field, field],
        compiler_params=PARAMS,
        cost_estimate=cost(2 * dft_flops, 1 << 20),
    )(positions, wave, intensity, direct, inverse, *unit_sets[1])
    keep_0, send_0 = pl.pallas_call(
        lambda *refs: last_kernel(ring, rows, window, *refs),
        out_shape=[units, units],
        in_specs=[SMEM] + [VMEM] * 5,
        out_specs=[VMEM] * 2,
        scratch_shapes=[field],
        compiler_params=PARAMS,
        cost_estimate=cost(2 * dft_flops, 1 << 20),
    )(positions, probe, carried, direct, inverse, kernel)

    def returned(keep, send):
        other = swap(send)
        out = []
        for at, (step, band) in enumerate(steps):
            both = keep[at] + other[at]
            out.append(both if at == 0 else give(both, step, band))
        return out

    terms_1 = returned(keep_1, send_1)
    terms_0 = returned(keep_0, send_0)
    return pl.pallas_call(
        lambda *refs: sum_kernel(1.0 / (count * devices), 2 * ring, *refs),
        out_shape=jax.ShapeDtypeStruct(object_slices.shape, jnp.float32),
        in_specs=[VMEM] * (4 * ring),
        out_specs=VMEM,
        compiler_params=PARAMS,
    )(*terms_0, *terms_1)


def solution(mesh):
    placed = (
        P("group", None, "region", "probe"),
        P("group", None, None),
        P("region", "probe", "group", None),
        P("region", "probe", "group"),
    )
    return jax.shard_map(
        body,
        mesh=mesh,
        in_specs=placed,
        out_specs=P("group", None, "region", "probe"),
        check_vma=False,
    )
```

time: 170 us -> 44.9 us (0.26); the launches traced: 167 us -> 44.7 us
  waiting for transfers between devices: 53.1 us -> 9.28 us
  matrix products: 36.3 us -> 0 us
  local copies, waits for them, and re-layouts: 32.8 us -> 2.88 us
  loops' own time: 17.2 us -> 0 us
  starting transfers between devices: 8.31 us -> 23 us
  between operations: 14 us -> 0.17 us
  Pallas kernels: 0 us -> 9.33 us
  other arithmetic: 5.53 us -> 0.06 us
    dot_general x48 -> x0, matrix products: 36.3 us -> none  [the longest x24 18.2 us: right_mul(): jnp.einsum('nab,bc->nac', values, matrix, precision=lax.Precision.HIGHEST)]
    reduce_scatter x1 -> x0, waiting for transfers between devices: 20.2 us -> none  [body(): lax.psum_scatter(upper_part + returned, 'probe', scatter_dimension=3, til...]
    another operation x2 -> x0, loops' own time: 17.2 us -> none  [the longest x1 16.8 us: body(): lax.fori_loop(0, item_count, deposit, jnp.zeros(padded.shape, jnp.float32))]
    all_gather x1 -> x0, waiting for transfers between devices: 15.7 us -> none  [body(): whole_band = lax.all_gather(extended, 'probe', axis=3, tiled=True)]
    ppermute x2 -> x22, starting transfers between devices: 8.27 us -> 23 us  [the longest x6 12.5 us: fetch(): lax.ppermute(value, ('region', 'probe'), [(b, a) for a, b in route(step,...]
    dynamic_update_slice x8 -> x0, local copies, waits for them, and re-layouts: 12.3 us -> none  [deposit(): lax.dynamic_update_slice(accumulated, current + gradients[position], corner)]
    gather x20 -> x0, local copies, waits for them, and re-layouts: 9.85 us -> none
    pallas_call x0 -> x5, Pallas kernels: none -> 9.33 us  [the longest x1 3.37 us: body(): pl.pallas_call(lambda *refs: middle_kernel(ring, rows, window, *refs), ou...]
  transfers between devices with their start and end apart: 4 -> 22, of which waited for: 4 -> 7; matrix products, arithmetic and copies ran while one was open for 2% -> 0% of each run, Pallas kernels for 0% -> 6%
where the time goes in v1:
time: 44.9 us; the launch traced here: 44.7 us
  starting transfers between devices  23 us (51%)
  Pallas kernels  9.33 us (21%)
  waiting for transfers between devices  9.28 us (21%)
  local copies, waits for them, and re-layouts  2.88 us (6%)
    ppermute x6, starting transfers between devices, fetch(): lax.ppermute(value, ('region', 'probe'), [(b, a) for a, b in route(step,...  12.5 us
    ppermute x6, starting transfers between devices, give(): return lax.ppermute(value, ('region', 'probe'), route(step, band))  8.33 us
    ppermute x6, waiting for transfers between devices, give(): return lax.ppermute(value, ('region', 'probe'), route(step, band))  6.06 us
    pallas_call x1, Pallas kernels, body(): pl.pallas_call(lambda *refs: middle_kernel(ring, rows, window, *refs), ou...  3.37 us
    pallas_call x1, Pallas kernels, body(): pl.pallas_call(lambda *refs: first_kernel(ring, rows, window, *refs), out...  2.89 us
    pallas_call x1, Pallas kernels, body(): pl.pallas_call(lambda *refs: last_kernel(ring, rows, window, *refs), out_...  2.88 us
    ppermute x10, starting transfers between devices, swap(): return lax.ppermute(value, 'probe', [(i, i ^ 1) for i in range(devices)])  2.22 us
    ppermute x6, waiting for transfers between devices, fetch(): lax.ppermute(value, ('region', 'probe'), [(b, a) for a, b in route(step,...  2.12 us
  transfers between devices with their start and end apart: 22, of which 7 were waited for; matrix products, arithmetic and copies ran while one was open for 0% of the time, Pallas kernels for 6%

profile of v1, /device:TPU:0, one launch (start us, length us, event | category | flops | bytes accessed | tf_op | source)
XLA Modules:
  0.0 44.7 jit_solution(4110865810399716864)
XLA Ops:
  0.0 1.1 %copy.8.object_ref = f32[2,2,128,64]{3,2,1,0:T(8,128)S(1)} copy(f32[2,2,128,64]{2,3,1,0:T(8,128)} %param.7) | data formatting | bytes 262144 | tf_op args[0]
  1.1 0.0 copy-start.1
  1.1 0.1 shard_map.73
  1.2 0.0 copy-start.6
  1.2 6.0 %collective-permute-start.5 = (f32[128,128]{1,0:T(8,128)S(1)}, f32[128,128]{1,0:T(8,128)S(1)}, u32[]{:S(2)}, u32[]{:S(2)}) collective-permute-start(f32[128,128]{1,0:T(8,128)S(1)} %get-tuple-element.12.refs_5_), channel_id=1, source_target_pairs={{6,0},{7,1},{4,2},{5,3},{10,4},{11,5},{8,6},{9,7},{14,8},{15,9},{1... | collective-permute-start | bytes 196616 | tf_op jit(solution)/shard_map/ppermute | solution.py:269
  7.3 0.5 %collective-permute-start.3 = (f32[128,128]{1,0:T(8,128)S(1)}, f32[128,128]{1,0:T(8,128)S(1)}, u32[]{:S(2)}, u32[]{:S(2)}) collective-permute-start(f32[128,128]{1,0:T(8,128)S(1)} %get-tuple-element.12.refs_5_), channel_id=1, source_target_pairs={{2,0},{3,1},{0,2},{1,3},{6,4},{7,5},{4,6},{5,7},{10,8},{11,9},{8,1... | collective-permute-start | bytes 196616 | tf_op jit(solution)/shard_map/ppermute | solution.py:269
  7.8 0.4 %collective-permute-start.1 = (f32[128,128]{1,0:T(8,128)S(1)}, f32[128,128]{1,0:T(8,128)S(1)}, u32[]{:S(2)}, u32[]{:S(2)}) collective-permute-start(f32[128,128]{1,0:T(8,128)S(1)} %get-tuple-element.12.refs_5_), channel_id=1, source_target_pairs={{4,0},{5,1},{6,2},{7,3},{8,4},{9,5},{10,6},{11,7},{12,8},{13,9},{1... | collective-permute-start | bytes 196616 | tf_op jit(solution)/shard_map/ppermute | solution.py:269
  8.2 0.0 collective-permute-start
  8.2 1.4 %collective-permute-start.12 = (f32[128,128]{1,0:T(8,128)S(1)}, f32[128,128]{1,0:T(8,128)S(1)}, u32[]{:S(2)}, u32[]{:S(2)}) collective-permute-start(f32[128,128]{1,0:T(8,128)S(1)} %get-tuple-element.13.refs_5_), channel_id=1, source_target_pairs={{6,0},{7,1},{4,2},{5,3},{10,4},{11,5},{8,6},{9,7},{14,8},{15,9},{1... | collective-permute-start | bytes 196616 | tf_op jit(solution)/shard_map/ppermute | solution.py:269
  9.6 0.0 collective-permute-done.5.refs_11_
  9.6 0.5 %collective-permute-start.10 = (f32[128,128]{1,0:T(8,128)S(1)}, f32[128,128]{1,0:T(8,128)S(1)}, u32[]{:S(2)}, u32[]{:S(2)}) collective-permute-start(f32[128,128]{1,0:T(8,128)S(1)} %get-tuple-element.13.refs_5_), channel_id=1, source_target_pairs={{2,0},{3,1},{0,2},{1,3},{6,4},{7,5},{4,6},{5,7},{10,8},{11,9},{8,1... | collective-permute-start | bytes 196616 | tf_op jit(solution)/shard_map/ppermute | solution.py:269
  10.2 1.4 %collective-permute-done.3.refs_9_ = f32[128,128]{1,0:T(8,128)S(1)} collective-permute-done((f32[128,128]{1,0:T(8,128)S(1)}, f32[128,128]{1,0:T(8,128)S(1)}, u32[]{:S(2)}, u32[]{:S(2)}) %collective-permute-start.3) | collective-permute-done | bytes 65568 | tf_op jit(solution)/shard_map/ppermute | solution.py:269
  11.5 3.5 %collective-permute-start.8 = (f32[128,128]{1,0:T(8,128)S(1)}, f32[128,128]{1,0:T(8,128)S(1)}, u32[]{:S(2)}, u32[]{:S(2)}) collective-permute-start(f32[128,128]{1,0:T(8,128)S(1)} %get-tuple-element.13.refs_5_), channel_id=1, source_target_pairs={{4,0},{5,1},{6,2},{7,3},{8,4},{9,5},{10,6},{11,7},{12,8},{13,9},{1... | collective-permute-start | bytes 196616 | tf_op jit(solution)/shard_map/ppermute | solution.py:269
  15.1 0.0 collective-permute-done.1.refs_7_
  15.1 0.0 collective-permute-start.6
  15.1 0.5 %collective-permute-start.4 = (f32[128,128]{1,0:T(8,128)S(1)}, f32[128,128]{1,0:T(8,128)S(1)}, u32[]{:S(2)}, u32[]{:S(2)}) collective-permute-start(f32[128,128]{1,0:T(8,128)S(1)} %collective-permute-done.3.refs_9_), channel_id=1, source_target_pairs={{0,1},{1,0},{2,3},{3,2},{4,5},{5,4},{6,7},{7,6},{8,9},{9,8},{10,11... | collective-permute-start | bytes 196616 | tf_op jit(solution)/shard_map/ppermute | solution.py:258
  15.6 0.0 collective-permute-done.12.refs_11_
  15.6 0.1 collective-permute-start.2
  15.7 0.1 copy.11.refs_0_
  15.8 0.5 %collective-permute-start.7 = (f32[128,128]{1,0:T(8,128)S(1)}, f32[128,128]{1,0:T(8,128)S(1)}, u32[]{:S(2)}, u32[]{:S(2)}) collective-permute-start(f32[128,128]{1,0:T(8,128)S(1)} %get-tuple-element.13.refs_5_), channel_id=1, source_target_pairs={{0,1},{1,0},{2,3},{3,2},{4,5},{5,4},{6,7},{7,6},{8,9},{9,8},{10,11... | collective-permute-start | bytes 196616 | tf_op jit(solution)/shard_map/ppermute | solution.py:258
  16.2 0.7 %collective-permute-done.8.refs_7_ = f32[128,128]{1,0:T(8,128)S(1)} collective-permute-done((f32[128,128]{1,0:T(8,128)S(1)}, f32[128,128]{1,0:T(8,128)S(1)}, u32[]{:S(2)}, u32[]{:S(2)}) %collective-permute-start.8) | collective-permute-done | bytes 65568 | tf_op jit(solution)/shard_map/ppermute | solution.py:269
  17.0 0.5 %collective-permute-start.11 = (f32[128,128]{1,0:T(8,128)S(1)}, f32[128,128]{1,0:T(8,128)S(1)}, u32[]{:S(2)}, u32[]{:S(2)}) collective-permute-start(f32[128,128]{1,0:T(8,128)S(1)} %collective-permute-done.10.refs_9_), channel_id=1, source_target_pairs={{0,1},{1,0},{2,3},{3,2},{4,5},{5,4},{6,7},{7,6},{8,9},{9,8},{10,11... | collective-permute-start | bytes 196616 | tf_op jit(solution)/shard_map/ppermute | solution.py:258
  17.5 0.1 collective-permute-start.9
  17.6 0.0 copy-start.4
  17.6 0.9 %copy-done.4 = f32[2,128,128]{2,1,0:T(8,128)S(1)} copy-done((f32[2,128,128]{2,1,0:T(8,128)S(1)}, f32[2,128,128]{2,1,0:T(8,128)}, u32[]{:S(2)}) %copy-start.4) | copy-done | bytes 131096
  18.5 2.9 %shard_map.74.refs_1_ = f32[4,2,128,128]{3,2,1,0:T(8,128)S(1)} custom-call(s32[1,4,2]{2,1,0:T(4,128)S(1)} %copy.11.refs_0_, f32[2,128,128]{2,1,0:T(8,128)S(1)} %copy-done.1, bf16[2,256,256]{2,1,0:T(8,128)(2,1)S(1)} %copy-done.3, bf16[2,256,256]{2,1,0:T(8,128)(2,1)S(1)} %copy-done.2, f32[2,128,128]{2,1,0:T(8,128)S(1)} %copy-done.4, ...), custom_call_target="tpu_custom_call" | custom-call | flops 805306368 | bytes 1048576 | tf_op jit(solution)/shard_map/pallas_call | solution.py:287
  21.4 0.0 copy-start.5
  21.4 0.0 collective-permute-done.7.refs_6_
  21.4 0.0 collective-permute-done.9.refs_8_
  21.4 3.4 %shard_map.75 = (f32[4,2,128,128]{3,2,1,0:T(8,128)S(1)}, f32[4,128,128]{2,1,0:T(8,128)S(1)}, f32[4,128,128]{2,1,0:T(8,128)S(1)}) custom-call(s32[1,4,2]{2,1,0:T(4,128)S(1)} %copy.11.refs_0_, f32[4,2,128,128]{3,2,1,0:T(8,128)S(1)} %shard_map.74.refs_1_, f32[1,4,128,128]{3,2,1,0:T(8,128)S(1)} %copy-done, bf16[2,256,256]{2,1,0:T(8,128)(2,1)S(1)} %copy-done.3, ...), custom_call_target="tpu_custom_call" | custom-call | flops 805306368 | bytes 1048576 | tf_op jit(solution)/shard_map/pallas_call | solution.py:296
  24.8 2.9 %shard_map.76 = (f32[4,128,128]{2,1,0:T(8,128)S(1)}, f32[4,128,128]{2,1,0:T(8,128)S(1)}) custom-call(s32[1,4,2]{2,1,0:T(4,128)S(1)} %copy.11.refs_0_, f32[2,128,128]{2,1,0:T(8,128)S(1)} %copy-done.1, f32[4,2,128,128]{3,2,1,0:T(8,128)S(1)} %get-tuple-element.14.refs_2_, bf16[2,256,256]{2,1,0:T(8,128)(2,1)S(1)} %copy-done.3, ...), custom_call_target="tpu_custom_call" | custom-call | flops 805306368 | bytes 1048576 | tf_op jit(solution)/shard_map/pallas_call | solution.py:305
  27.7 0.5 %collective-permute-start.14 = (f32[4,128,128]{2,1,0:T(8,128)S(1)}, f32[4,128,128]{2,1,0:T(8,128)S(1)}, u32[]{:S(2)}, u32[]{:S(2)}) collective-permute-start(f32[4,128,128]{2,1,0:T(8,128)S(1)} %get-tuple-element.16), channel_id=1, source_target_pairs={{0,1},{1,0},{2,3},{3,2},{4,5},{5,4},{6,7},{7,6},{8,9},{9,8},{10,11... | collective-permute-start | bytes 786440 | tf_op jit(solution)/shard_map/ppermute | solution.py:258
  28.2 0.1 collective-permute-start.18
  28.3 1.1 %collective-permute-done.14 = f32[4,128,128]{2,1,0:T(8,128)S(1)} collective-permute-done((f32[4,128,128]{2,1,0:T(8,128)S(1)}, f32[4,128,128]{2,1,0:T(8,128)S(1)}, u32[]{:S(2)}, u32[]{:S(2)}) %collective-permute-start.14) | collective-permute-done | bytes 262176 | tf_op jit(solution)/shard_map/ppermute | solution.py:258
  29.4 0.3 collective-permute-start.17
  29.7 1.2 %collective-permute-start.16 = (f32[128,128]{1,0:T(8,128)S(1)}, f32[128,128]{1,0:T(8,128)S(1)}, u32[]{:S(2)}, u32[]{:S(2)}) collective-permute-start(f32[128,128]{1,0:T(8,128)S(1)} %get-tuple-element.24), channel_id=1, source_target_pairs={{0,2},{1,3},{2,0},{3,1},{4,6},{5,7},{6,4},{7,5},{8,10},{9,11},{10,... | collective-permute-start | bytes 196616 | tf_op jit(solution)/shard_map/ppermute | solution.py:272
  31.0 1.4 %collective-permute-start.15 = (f32[128,128]{1,0:T(8,128)S(1)}, f32[128,128]{1,0:T(8,128)S(1)}, u32[]{:S(2)}, u32[]{:S(2)}) collective-permute-start(f32[128,128]{1,0:T(8,128)S(1)} %get-tuple-element.25), channel_id=1, source_target_pairs={{0,4},{1,5},{2,6},{3,7},{4,8},{5,9},{6,10},{7,11},{8,12},{9,13},{1... | collective-permute-start | bytes 196616 | tf_op jit(solution)/shard_map/ppermute | solution.py:272
  32.4 0.0 collective-permute-done.18
  32.4 4.0 %collective-permute-start.21 = (f32[128,128]{1,0:T(8,128)S(1)}, f32[128,128]{1,0:T(8,128)S(1)}, u32[]{:S(2)}, u32[]{:S(2)}) collective-permute-start(f32[128,128]{1,0:T(8,128)S(1)} %get-tuple-element.19), channel_id=1, source_target_pairs={{0,6},{1,7},{2,4},{3,5},{4,10},{5,11},{6,8},{7,9},{8,14},{9,15},{1... | collective-permute-start | bytes 196616 | tf_op jit(solution)/shard_map/ppermute | solution.py:272
  36.5 1.3 %collective-permute-start.20 = (f32[128,128]{1,0:T(8,128)S(1)}, f32[128,128]{1,0:T(8,128)S(1)}, u32[]{:S(2)}, u32[]{:S(2)}) collective-permute-start(f32[128,128]{1,0:T(8,128)S(1)} %get-tuple-element.20), channel_id=1, source_target_pairs={{0,2},{1,3},{2,0},{3,1},{4,6},{5,7},{6,4},{7,5},{8,10},{9,11},{10,... | collective-permute-start | bytes 196616 | tf_op jit(solution)/shard_map/ppermute | solution.py:272
  37.8 0.0 collective-permute-start.19
  37.8 0.0 collective-permute-done.16.refs_2_
  37.8 0.2 collective-permute-done.15.refs_1_
  38.0 1.5 %collective-permute-done.21.refs_7_ = f32[128,128]{1,0:T(8,128)S(1)} collective-permute-done((f32[128,128]{1,0:T(8,128)S(1)}, f32[128,128]{1,0:T(8,128)S(1)}, u32[]{:S(2)}, u32[]{:S(2)}) %collective-permute-start.21) | collective-permute-done | bytes 65568 | tf_op jit(solution)/shard_map/ppermute | solution.py:272
  39.5 1.2 %collective-permute-done.20.refs_6_ = f32[128,128]{1,0:T(8,128)S(1)} collective-permute-done((f32[128,128]{1,0:T(8,128)S(1)}, f32[128,128]{1,0:T(8,128)S(1)}, u32[]{:S(2)}, u32[]{:S(2)}) %collective-permute-start.20) | collective-permute-done | bytes 65568 | tf_op jit(solution)/shard_map/ppermute | solution.py:272
  40.8 3.1 %collective-permute-done.19.refs_5_ = f32[128,128]{1,0:T(8,128)S(1)} collective-permute-done((f32[128,128]{1,0:T(8,128)S(1)}, f32[128,128]{1,0:T(8,128)S(1)}, u32[]{:S(2)}, u32[]{:S(2)}) %collective-permute-start.19) | collective-permute-done | bytes 65568 | tf_op jit(solution)/shard_map/ppermute | solution.py:272
  43.9 0.1 shard_map.77
  44.0 0.8 %copy.12 = f32[2,2,128,64]{2,3,1,0:T(8,128)} copy(f32[2,2,128,64]{3,2,1,0:T(8,128)S(1)} %shard_map.77) | data formatting | bytes 262144 | tf_op jit(solution)/shard_map/pallas_call | solution.py:325
  (20 shorter events, 0.1 us)
Async XLA Ops:
  0.0 17.6 %copy-start.2 = (bf16[2,256,256]{2,1,0:T(8,128)(2,1)S(1)}, bf16[2,256,256]{2,1,0:T(8,128)(2,1)}, u32[]{:S(2)}) copy-start(bf16[2,256,256]{2,1,0:T(8,128)(2,1)} %constant.7.clone.refs_3_.refs_4_) | copy-start | bytes 786436
  0.0 17.6 %copy-start.3 = (bf16[2,256,256]{2,1,0:T(8,128)(2,1)S(1)}, bf16[2,256,256]{2,1,0:T(8,128)(2,1)}, u32[]{:S(2)}) copy-start(bf16[2,256,256]{2,1,0:T(8,128)(2,1)} %constant.6.clone.refs_2_.refs_3_) | copy-start | bytes 786436
  1.1 16.5 %copy-start.1 = (f32[2,128,128]{2,1,0:T(8,128)S(1)}, f32[2,128,128]{2,1,0:T(8,128)}, u32[]{:S(2)}) copy-start(f32[2,128,128]{2,1,0:T(8,128)} %refs_1_.3) | copy-start | bytes 393220
  1.2 14.4 %copy-start.6 = (s32[1,4,2]{1,2,0:T(2,128)S(1)}, s32[1,4,2]{1,2,0:T(2,128)}, u32[]{:S(2)}) copy-start(s32[1,4,2]{1,2,0:T(2,128)} %param.10) | copy-start | bytes 100
  1.2 8.4 %collective-permute-start.5 = (f32[128,128]{1,0:T(8,128)S(1)}, f32[128,128]{1,0:T(8,128)S(1)}, u32[]{:S(2)}, u32[]{:S(2)}) collective-permute-start(f32[128,128]{1,0:T(8,128)S(1)} %get-tuple-element.12.refs_5_), channel_id=1, source_target_pairs={{6,0},{7,1},{4,2},{5,3},{10,4},{11,5},{8,6},{9,7},{14,8},{15,9},{1... | collective-permute-start | bytes 196616 | tf_op jit(solution)/shard_map/ppermute | solution.py:269
  7.3 4.3 %collective-permute-start.3 = (f32[128,128]{1,0:T(8,128)S(1)}, f32[128,128]{1,0:T(8,128)S(1)}, u32[]{:S(2)}, u32[]{:S(2)}) collective-permute-start(f32[128,128]{1,0:T(8,128)S(1)} %get-tuple-element.12.refs_5_), channel_id=1, source_target_pairs={{2,0},{3,1},{0,2},{1,3},{6,4},{7,5},{4,6},{5,7},{10,8},{11,9},{8,1... | collective-permute-start | bytes 196616 | tf_op jit(solution)/shard_map/ppermute | solution.py:269
  7.8 7.3 %collective-permute-start.1 = (f32[128,128]{1,0:T(8,128)S(1)}, f32[128,128]{1,0:T(8,128)S(1)}, u32[]{:S(2)}, u32[]{:S(2)}) collective-permute-start(f32[128,128]{1,0:T(8,128)S(1)} %get-tuple-element.12.refs_5_), channel_id=1, source_target_pairs={{4,0},{5,1},{6,2},{7,3},{8,4},{9,5},{10,6},{11,7},{12,8},{13,9},{1... | collective-permute-start | bytes 196616 | tf_op jit(solution)/shard_map/ppermute | solution.py:269
  8.2 6.8 %collective-permute-start = (f32[128,128]{1,0:T(8,128)S(1)}, f32[128,128]{1,0:T(8,128)S(1)}, u32[]{:S(2)}, u32[]{:S(2)}) collective-permute-start(f32[128,128]{1,0:T(8,128)S(1)} %get-tuple-element.12.refs_5_), channel_id=1, source_target_pairs={{0,1},{1,0},{2,3},{3,2},{4,5},{5,4},{6,7},{7,6},{8,9},{9,8},{10,11... | collective-permute-start | bytes 196616 | tf_op jit(solution)/shard_map/ppermute | solution.py:258
  8.2 7.3 %collective-permute-start.12 = (f32[128,128]{1,0:T(8,128)S(1)}, f32[128,128]{1,0:T(8,128)S(1)}, u32[]{:S(2)}, u32[]{:S(2)}) collective-permute-start(f32[128,128]{1,0:T(8,128)S(1)} %get-tuple-element.13.refs_5_), channel_id=1, source_target_pairs={{6,0},{7,1},{4,2},{5,3},{10,4},{11,5},{8,6},{9,7},{14,8},{15,9},{1... | collective-permute-start | bytes 196616 | tf_op jit(solution)/shard_map/ppermute | solution.py:269
  9.6 6.1 %collective-permute-start.10 = (f32[128,128]{1,0:T(8,128)S(1)}, f32[128,128]{1,0:T(8,128)S(1)}, u32[]{:S(2)}, u32[]{:S(2)}) collective-permute-start(f32[128,128]{1,0:T(8,128)S(1)} %get-tuple-element.13.refs_5_), channel_id=1, source_target_pairs={{2,0},{3,1},{0,2},{1,3},{6,4},{7,5},{4,6},{5,7},{10,8},{11,9},{8,1... | collective-permute-start | bytes 196616 | tf_op jit(solution)/shard_map/ppermute | solution.py:269
  11.5 5.4 %collective-permute-start.8 = (f32[128,128]{1,0:T(8,128)S(1)}, f32[128,128]{1,0:T(8,128)S(1)}, u32[]{:S(2)}, u32[]{:S(2)}) collective-permute-start(f32[128,128]{1,0:T(8,128)S(1)} %get-tuple-element.13.refs_5_), channel_id=1, source_target_pairs={{4,0},{5,1},{6,2},{7,3},{8,4},{9,5},{10,6},{11,7},{12,8},{13,9},{1... | collective-permute-start | bytes 196616 | tf_op jit(solution)/shard_map/ppermute | solution.py:269
  15.1 1.9 %collective-permute-start.6 = (f32[128,128]{1,0:T(8,128)S(1)}, f32[128,128]{1,0:T(8,128)S(1)}, u32[]{:S(2)}, u32[]{:S(2)}) collective-permute-start(f32[128,128]{1,0:T(8,128)S(1)} %collective-permute-done.5.refs_11_), channel_id=1, source_target_pairs={{0,1},{1,0},{2,3},{3,2},{4,5},{5,4},{6,7},{7,6},{8,9},{9,8},{10,11... | collective-permute-start | bytes 196616 | tf_op jit(solution)/shard_map/ppermute | solution.py:258
  15.1 2.4 %collective-permute-start.4 = (f32[128,128]{1,0:T(8,128)S(1)}, f32[128,128]{1,0:T(8,128)S(1)}, u32[]{:S(2)}, u32[]{:S(2)}) collective-permute-start(f32[128,128]{1,0:T(8,128)S(1)} %collective-permute-done.3.refs_9_), channel_id=1, source_target_pairs={{0,1},{1,0},{2,3},{3,2},{4,5},{5,4},{6,7},{7,6},{8,9},{9,8},{10,11... | collective-permute-start | bytes 196616 | tf_op jit(solution)/shard_map/ppermute | solution.py:258
  15.6 2.0 %collective-permute-start.2 = (f32[128,128]{1,0:T(8,128)S(1)}, f32[128,128]{1,0:T(8,128)S(1)}, u32[]{:S(2)}, u32[]{:S(2)}) collective-permute-start(f32[128,128]{1,0:T(8,128)S(1)} %collective-permute-done.1.refs_7_), channel_id=1, source_target_pairs={{0,1},{1,0},{2,3},{3,2},{4,5},{5,4},{6,7},{7,6},{8,9},{9,8},{10,11... | collective-permute-start | bytes 196616 | tf_op jit(solution)/shard_map/ppermute | solution.py:258
  15.7 5.7 %copy-start = (f32[1,4,128,128]{3,2,1,0:T(8,128)S(1)}, f32[1,4,128,128]{3,2,1,0:T(8,128)}, u32[]{:S(2)}) copy-start(f32[1,4,128,128]{3,2,1,0:T(8,128)} %refs_2_.2) | copy-start | bytes 786436
  15.8 5.6 %collective-permute-start.7 = (f32[128,128]{1,0:T(8,128)S(1)}, f32[128,128]{1,0:T(8,128)S(1)}, u32[]{:S(2)}, u32[]{:S(2)}) collective-permute-start(f32[128,128]{1,0:T(8,128)S(1)} %get-tuple-element.13.refs_5_), channel_id=1, source_target_pairs={{0,1},{1,0},{2,3},{3,2},{4,5},{5,4},{6,7},{7,6},{8,9},{9,8},{10,11... | collective-permute-start | bytes 196616 | tf_op jit(solution)/shard_map/ppermute | solution.py:258
  17.0 4.4 %collective-permute-start.13 = (f32[128,128]{1,0:T(8,128)S(1)}, f32[128,128]{1,0:T(8,128)S(1)}, u32[]{:S(2)}, u32[]{:S(2)}) collective-permute-start(f32[128,128]{1,0:T(8,128)S(1)} %collective-permute-done.12.refs_11_), channel_id=1, source_target_pairs={{0,1},{1,0},{2,3},{3,2},{4,5},{5,4},{6,7},{7,6},{8,9},{9,8},{10,11... | collective-permute-start | bytes 196616 | tf_op jit(solution)/shard_map/ppermute | solution.py:258
  17.0 4.4 %collective-permute-start.11 = (f32[128,128]{1,0:T(8,128)S(1)}, f32[128,128]{1,0:T(8,128)S(1)}, u32[]{:S(2)}, u32[]{:S(2)}) collective-permute-start(f32[128,128]{1,0:T(8,128)S(1)} %collective-permute-done.10.refs_9_), channel_id=1, source_target_pairs={{0,1},{1,0},{2,3},{3,2},{4,5},{5,4},{6,7},{7,6},{8,9},{9,8},{10,11... | collective-permute-start | bytes 196616 | tf_op jit(solution)/shard_map/ppermute | solution.py:258
  17.5 3.9 %collective-permute-start.9 = (f32[128,128]{1,0:T(8,128)S(1)}, f32[128,128]{1,0:T(8,128)S(1)}, u32[]{:S(2)}, u32[]{:S(2)}) collective-permute-start(f32[128,128]{1,0:T(8,128)S(1)} %collective-permute-done.8.refs_7_), channel_id=1, source_target_pairs={{0,1},{1,0},{2,3},{3,2},{4,5},{5,4},{6,7},{7,6},{8,9},{9,8},{10,11... | collective-permute-start | bytes 196616 | tf_op jit(solution)/shard_map/ppermute | solution.py:258
  17.6 0.9 %copy-start.4 = (f32[2,128,128]{2,1,0:T(8,128)S(1)}, f32[2,128,128]{2,1,0:T(8,128)}, u32[]{:S(2)}) copy-start(f32[2,128,128]{2,1,0:T(8,128)} %constant.8.clone.refs_4_.refs_5_) | copy-start | bytes 393220
  21.4 3.4 %copy-start.5 = (f32[2,128,128]{2,1,0:T(8,128)S(1)}, f32[2,128,128]{2,1,0:T(8,128)}, u32[]{:S(2)}) copy-start(f32[2,128,128]{2,1,0:T(8,128)} %constant.8.clone.refs_4_.refs_5_) | copy-start | bytes 393220
  27.7 1.7 %collective-permute-start.14 = (f32[4,128,128]{2,1,0:T(8,128)S(1)}, f32[4,128,128]{2,1,0:T(8,128)S(1)}, u32[]{:S(2)}, u32[]{:S(2)}) collective-permute-start(f32[4,128,128]{2,1,0:T(8,128)S(1)} %get-tuple-element.16), channel_id=1, source_target_pairs={{0,1},{1,0},{2,3},{3,2},{4,5},{5,4},{6,7},{7,6},{8,9},{9,8},{10,11... | collective-permute-start | bytes 786440 | tf_op jit(solution)/shard_map/ppermute | solution.py:258
  28.2 4.2 %collective-permute-start.18 = (f32[4,128,128]{2,1,0:T(8,128)S(1)}, f32[4,128,128]{2,1,0:T(8,128)S(1)}, u32[]{:S(2)}, u32[]{:S(2)}) collective-permute-start(f32[4,128,128]{2,1,0:T(8,128)S(1)} %get-tuple-element.18), channel_id=1, source_target_pairs={{0,1},{1,0},{2,3},{3,2},{4,5},{5,4},{6,7},{7,6},{8,9},{9,8},{10,11... | collective-permute-start | bytes 786440 | tf_op jit(solution)/shard_map/ppermute | solution.py:258
  29.4 8.4 %collective-permute-start.17 = (f32[128,128]{1,0:T(8,128)S(1)}, f32[128,128]{1,0:T(8,128)S(1)}, u32[]{:S(2)}, u32[]{:S(2)}) collective-permute-start(f32[128,128]{1,0:T(8,128)S(1)} %get-tuple-element.23), channel_id=1, source_target_pairs={{0,6},{1,7},{2,4},{3,5},{4,10},{5,11},{6,8},{7,9},{8,14},{9,15},{1... | collective-permute-start | bytes 196616 | tf_op jit(solution)/shard_map/ppermute | solution.py:272
  29.7 8.1 %collective-permute-start.16 = (f32[128,128]{1,0:T(8,128)S(1)}, f32[128,128]{1,0:T(8,128)S(1)}, u32[]{:S(2)}, u32[]{:S(2)}) collective-permute-start(f32[128,128]{1,0:T(8,128)S(1)} %get-tuple-element.24), channel_id=1, source_target_pairs={{0,2},{1,3},{2,0},{3,1},{4,6},{5,7},{6,4},{7,5},{8,10},{9,11},{10,... | collective-permute-start | bytes 196616 | tf_op jit(solution)/shard_map/ppermute | solution.py:272
  31.0 7.0 %collective-permute-start.15 = (f32[128,128]{1,0:T(8,128)S(1)}, f32[128,128]{1,0:T(8,128)S(1)}, u32[]{:S(2)}, u32[]{:S(2)}) collective-permute-start(f32[128,128]{1,0:T(8,128)S(1)} %get-tuple-element.25), channel_id=1, source_target_pairs={{0,4},{1,5},{2,6},{3,7},{4,8},{5,9},{6,10},{7,11},{8,12},{9,13},{1... | collective-permute-start | bytes 196616 | tf_op jit(solution)/shard_map/ppermute | solution.py:272
  32.4 7.1 %collective-permute-start.21 = (f32[128,128]{1,0:T(8,128)S(1)}, f32[128,128]{1,0:T(8,128)S(1)}, u32[]{:S(2)}, u32[]{:S(2)}) collective-permute-start(f32[128,128]{1,0:T(8,128)S(1)} %get-tuple-element.19), channel_id=1, source_target_pairs={{0,6},{1,7},{2,4},{3,5},{4,10},{5,11},{6,8},{7,9},{8,14},{9,15},{1... | collective-permute-start | bytes 196616 | tf_op jit(solution)/shard_map/ppermute | solution.py:272
  36.5 4.3 %collective-permute-start.20 = (f32[128,128]{1,0:T(8,128)S(1)}, f32[128,128]{1,0:T(8,128)S(1)}, u32[]{:S(2)}, u32[]{:S(2)}) collective-permute-start(f32[128,128]{1,0:T(8,128)S(1)} %get-tuple-element.20), channel_id=1, source_target_pairs={{0,2},{1,3},{2,0},{3,1},{4,6},{5,7},{6,4},{7,5},{8,10},{9,11},{10,... | collective-permute-start | bytes 196616 | tf_op jit(solution)/shard_map/ppermute | solution.py:272
  37.8 6.1 %collective-permute-start.19 = (f32[128,128]{1,0:T(8,128)S(1)}, f32[128,128]{1,0:T(8,128)S(1)}, u32[]{:S(2)}, u32[]{:S(2)}) collective-permute-start(f32[128,128]{1,0:T(8,128)S(1)} %get-tuple-element.21), channel_id=1, source_target_pairs={{0,4},{1,5},{2,6},{3,7},{4,8},{5,9},{6,10},{7,11},{8,12},{9,13},{1... | collective-permute-start | bytes 196616 | tf_op jit(solution)/shard_map/ppermute | solution.py:272

commit v2 on v1

v2 whole, which is shorter than its diff:
```python
import math

import jax
import jax.numpy as jnp
import ml_dtypes
import numpy as np
from jax import lax
from jax.experimental import pallas as pl
from jax.experimental.pallas import tpu as pltpu
from jax.sharding import PartitionSpec as P

CORES = 2
HALF = 64


def split_table(table):
    high = table.astype(ml_dtypes.bfloat16)
    low = (table - high.astype(np.float64)).astype(ml_dtypes.bfloat16)
    return np.stack([high, low])


def tables(window):
    indices = np.arange(window)
    angles = 2.0 * math.pi * ((indices[:, None] * indices[None, :]) % window) / window
    real, imag = np.cos(angles) / math.sqrt(window), -np.sin(angles) / math.sqrt(window)
    direct = np.block([[real, imag], [-imag, real]])
    inverse = np.block([[real, -imag], [imag, real]])
    frequency = np.where(indices < window // 2, indices, indices - window) / window
    phases = -60.0 * (frequency[:, None] ** 2 + frequency[None, :] ** 2)
    kernel = np.stack([np.cos(phases), np.sin(phases)]).astype(np.float32)
    return split_table(direct), split_table(inverse), kernel


def split(values):
    high = values.astype(jnp.bfloat16)
    low = (values - high.astype(jnp.float32)).astype(jnp.bfloat16)
    return high, low


def times_right(values, table_ref):
    high, low = split(values)
    table = jnp.concatenate([table_ref[0], table_ref[0], table_ref[1]], axis=0)
    stacked = jnp.concatenate([high, low, high], axis=1)
    return jnp.dot(stacked, table, preferred_element_type=jnp.float32)


def times_left(table_ref, values):
    high, low = split(values)
    table = jnp.concatenate([table_ref[0], table_ref[0], table_ref[1]], axis=1)
    stacked = jnp.concatenate([high, low, high], axis=0)
    return jnp.dot(table, stacked, preferred_element_type=jnp.float32)


def to_rows(values, window):
    count = values.shape[0] // window
    return jnp.concatenate(
        [
            jnp.concatenate(
                [values[n * window : (n + 1) * window, c * window : (c + 1) * window] for n in range(count)],
                axis=1,
            )
            for c in range(2)
        ],
        axis=0,
    )


def part(values, n, c, window):
    return values[c * window : (c + 1) * window, n * window : (n + 1) * window]


def join(pairs):
    return jnp.concatenate(
        [jnp.concatenate([re for re, _ in pairs], axis=1), jnp.concatenate([im for _, im in pairs], axis=1)],
        axis=0,
    )


def lanes(pairs):
    return jnp.concatenate([jnp.concatenate([re, im], axis=1) for re, im in pairs], axis=0)


def fresnel(pairs, direct_ref, inverse_ref, kernel_ref, sign, window):
    count = len(pairs)
    half = to_rows(times_right(lanes(pairs), direct_ref), window)
    spec = times_left(inverse_ref, half)
    k_re, k_im = kernel_ref[0], kernel_ref[1]
    if sign < 0:
        k_im = -k_im
    moved = []
    for n in range(count):
        re, im = part(spec, n, 0, window), part(spec, n, 1, window)
        moved.append((k_re * re - k_im * im, k_re * im + k_im * re))
    half = to_rows(times_right(lanes(moved), inverse_ref), window)
    wave = times_left(direct_ref, half)
    return [(part(wave, n, 0, window), part(wave, n, 1, window)) for n in range(count)]


def travel_order(ring):
    return [(0, 0)] + [(step, band) for band in range(2) for step in range(ring - 1, -1, -1) if step or band]


def assemble(unit_refs, field_ref, ring, window):
    me = lax.axis_index("probe")
    x, core = me // CORES, me % CORES
    layers = field_ref.shape[0]
    columns = field_ref.shape[3] - window
    at = 0
    for step, band in travel_order(ring):
        tile = lax.rem(x + step, ring)
        for owner in (core, 1 - core):
            where = pl.ds(pl.multiple_of((tile * CORES + owner) * HALF, HALF), HALF)
            for layer in range(layers):
                for c in range(2):
                    field_ref[layer, c, band, where, :] = unit_refs[at][layer, c]
            at += 1
    field_ref[:, :, :, columns:, :] = field_ref[:, :, :, :window, :]


def cut(field_ref, layer, position_ref, n, window):
    row, column = position_ref[0, n, 0], position_ref[0, n, 1]
    back = lax.rem(window - row, window)
    lane = lax.broadcasted_iota(jnp.int32, (window, window), 1)
    halves = []
    for c in range(2):
        first = pltpu.roll(field_ref[layer, c, 0, pl.ds(column, window), :], back, 1)
        second = pltpu.roll(field_ref[layer, c, 1, pl.ds(column, window), :], back, 1)
        halves.append(jnp.where(lane < window - row, first, second))
    return tuple(halves)


def deposit(total_ref, position_ref, n, pair, window):
    row, column = position_ref[0, n, 0], position_ref[0, n, 1]
    lane = lax.broadcasted_iota(jnp.int32, (window, window), 1)
    where = pl.ds(column, window)
    for c in range(2):
        turned = pltpu.roll(pair[c], row, 1)
        total_ref[c, 0, where, :] += jnp.where(lane >= row, turned, 0.0)
        total_ref[c, 1, where, :] += jnp.where(lane < row, turned, 0.0)


def hand_out(total_ref, keep_ref, send_ref, ring, window):
    me = lax.axis_index("probe")
    x, core = me // CORES, me % CORES
    columns = total_ref.shape[2] - window
    total_ref[:, :, :window, :] += total_ref[:, :, columns:, :]
    for at, (step, band) in enumerate(travel_order(ring)):
        tile = lax.rem(x + step, ring)
        for owner, ref in ((core, keep_ref), (1 - core, send_ref)):
            where = pl.ds(pl.multiple_of((tile * CORES + owner) * HALF, HALF), HALF)
            for c in range(2):
                ref[at, c] = total_ref[c, band, where, :]


def prepare_kernel(*refs):
    sources, outputs = refs[:5], refs[5:10]
    probe_ref, intensity_ref, sems = refs[10:]
    targets = (probe_ref, intensity_ref) + outputs[2:]
    copies = [pltpu.make_async_copy(a, b, sems.at[i]) for i, (a, b) in enumerate(zip(sources, targets))]
    for copy in copies:
        copy.start()
    copies[0].wait()
    for c in range(2):
        outputs[0][c] = probe_ref[c].T
    copies[1].wait()
    for n in range(intensity_ref.shape[1]):
        outputs[1][n] = intensity_ref[0, n].T
    for copy in copies[2:]:
        copy.wait()


def main_kernel(ring, window, position_ref, probe_ref, intensity_ref, direct_ref, inverse_ref, kernel_ref, *rest):
    unit_refs, (carried_ref, keep_ref, send_ref, field_ref, wave_ref, total_ref) = rest[:-6], rest[-6:]
    count = position_ref.shape[1]
    assemble(unit_refs, field_ref, ring, window)
    total_ref[...] = jnp.zeros_like(total_ref)
    probe_re, probe_im = probe_ref[0], probe_ref[1]
    exits = []
    for n in range(count):
        re, im = cut(field_ref, 0, position_ref, n, window)
        exits.append((probe_re * re - probe_im * im, probe_re * im + probe_im * re))
    waves = fresnel(exits, direct_ref, inverse_ref, kernel_ref, 1, window)
    exits, patches = [], []
    for n in range(count):
        re, im = cut(field_ref, 1, position_ref, n, window)
        w_re, w_im = waves[n]
        wave_ref[n, 0] = w_re
        wave_ref[n, 1] = w_im
        exits.append((w_re * re - w_im * im, w_re * im + w_im * re))
    far = times_left(inverse_ref, to_rows(times_right(lanes(exits), direct_ref), window))
    scaled = []
    for n in range(count):
        re, im = part(far, n, 0, window), part(far, n, 1, window)
        misfit = re * re + im * im - intensity_ref[n]
        scaled.append((misfit * re, misfit * im))
    back = times_left(direct_ref, to_rows(times_right(lanes(scaled), inverse_ref), window))
    for n in range(count):
        b_re, b_im = part(back, n, 0, window), part(back, n, 1, window)
        w_re, w_im = wave_ref[n, 0], wave_ref[n, 1]
        p_re, p_im = cut(field_ref, 1, position_ref, n, window)
        carried_ref[n, 0] = p_re * b_re + p_im * b_im
        carried_ref[n, 1] = p_re * b_im - p_im * b_re
        gradient = (w_re * b_re + w_im * b_im, w_re * b_im - w_im * b_re)
        deposit(total_ref, position_ref, n, gradient, window)
    hand_out(total_ref, keep_ref, send_ref, ring, window)


def last_kernel(
    ring, window, position_ref, probe_ref, carried_ref, direct_ref, inverse_ref, kernel_ref, keep_ref, send_ref, total_ref
):
    count = position_ref.shape[1]
    total_ref[...] = jnp.zeros_like(total_ref)
    carried = [(carried_ref[n, 0], carried_ref[n, 1]) for n in range(count)]
    backs = fresnel(carried, direct_ref, inverse_ref, kernel_ref, -1, window)
    probe_re, probe_im = probe_ref[0], probe_ref[1]
    for n, (b_re, b_im) in enumerate(backs):
        gradient = (probe_re * b_re + probe_im * b_im, probe_re * b_im - probe_im * b_re)
        deposit(total_ref, position_ref, n, gradient, window)
    hand_out(total_ref, keep_ref, send_ref, ring, window)


def pair_kernel(layers, *refs):
    inputs, outputs = refs[: 2 * layers], refs[2 * layers :]
    for layer in range(layers):
        for at, out_ref in enumerate(outputs):
            out_ref[layer] = inputs[2 * layer][at] + inputs[2 * layer + 1][at]


def sum_kernel(scale, *refs):
    total = refs[0][...]
    for ref in refs[1:-1]:
        total += ref[...]
    refs[-1][...] = total * scale


VMEM = pl.BlockSpec(memory_space=pltpu.VMEM)
HBM = pl.BlockSpec(memory_space=pltpu.HBM)
SMEM = pl.BlockSpec(memory_space=pltpu.SMEM)
PARAMS = pltpu.CompilerParams(vmem_limit_bytes=40 << 20)


def cost(flops, moved):
    return pl.CostEstimate(flops=flops, bytes_accessed=moved, transcendentals=0)


def body(object_slices, probe, intensity, positions):
    layers, _, rows, width = object_slices.shape
    window = probe.shape[1]
    count = positions.shape[1]
    regions = lax.axis_size("region")
    devices = lax.axis_size("probe")
    ring = devices // CORES
    columns = devices * width
    direct, inverse, kernel = (jnp.asarray(t) for t in tables(window))
    unit = jax.ShapeDtypeStruct((layers, 2, width, rows), jnp.float32)
    waves = jax.ShapeDtypeStruct((count, 2, window, window), jnp.float32)
    units = jax.ShapeDtypeStruct((2 * ring, 2, width, rows), jnp.float32)
    field = pltpu.VMEM((layers, 2, 2, columns + window, rows), jnp.float32)
    total = pltpu.VMEM((2, 2, columns + window, rows), jnp.float32)
    wave_scratch = pltpu.VMEM(waves.shape, jnp.float32)
    dft_flops = count * 2 * 3 * 2 * window * (2 * window) ** 2

    def swap(value):
        return lax.ppermute(value, "probe", [(i, i ^ 1) for i in range(devices)])

    def route(step, band):
        pairs = []
        for r in range(regions):
            for d in range(devices):
                there = ((d // CORES + step) % ring) * CORES + d % CORES
                pairs.append((r * devices + d, ((r + band) % regions) * devices + there))
        return pairs

    def fetch(value, step, band):
        return lax.ppermute(value, ("region", "probe"), [(b, a) for a, b in route(step, band)])

    def give(value, step, band):
        return lax.ppermute(value, ("region", "probe"), route(step, band))

    steps = travel_order(ring)
    tile = jnp.swapaxes(object_slices, 2, 3)
    probe_t, intensity_t, direct, inverse, kernel = pl.pallas_call(
        prepare_kernel,
        out_shape=[
            jax.ShapeDtypeStruct(probe.shape, jnp.float32),
            jax.ShapeDtypeStruct(intensity.shape[1:], jnp.float32),
            jax.ShapeDtypeStruct(direct.shape, direct.dtype),
            jax.ShapeDtypeStruct(inverse.shape, inverse.dtype),
            jax.ShapeDtypeStruct(kernel.shape, kernel.dtype),
        ],
        in_specs=[HBM] * 5,
        out_specs=[VMEM] * 5,
        scratch_shapes=[
            pltpu.VMEM(probe.shape, jnp.float32),
            pltpu.VMEM(intensity.shape, jnp.float32),
            pltpu.SemaphoreType.DMA((5,)),
        ],
        compiler_params=PARAMS,
        cost_estimate=cost(dft_flops, 16 << 20),
    )(probe, intensity, direct, inverse, kernel)
    arrived = [tile] + [fetch(tile, *step) for step in steps[1:]]
    *arrived[1:], probe_t = lax.optimization_barrier((*arrived[1:], probe_t))
    gathered = []
    for value in arrived:
        gathered += [value, swap(value)]
    carried, keep_1, send_1 = pl.pallas_call(
        lambda *refs: main_kernel(ring, window, *refs),
        out_shape=[waves, units, units],
        in_specs=[SMEM] + [VMEM] * (5 + 4 * ring),
        out_specs=[VMEM] * 3,
        scratch_shapes=[field, wave_scratch, total],
        compiler_params=PARAMS,
        cost_estimate=cost(4 * dft_flops, 1 << 20),
    )(positions, probe_t, intensity_t, direct, inverse, kernel, *gathered)
    other_1 = swap(send_1)
    keep_0, send_0 = pl.pallas_call(
        lambda *refs: last_kernel(ring, window, *refs),
        out_shape=[units, units],
        in_specs=[SMEM] + [VMEM] * 5,
        out_specs=[VMEM] * 2,
        scratch_shapes=[total],
        compiler_params=PARAMS,
        cost_estimate=cost(2 * dft_flops, 1 << 20),
    )(positions, probe_t, carried, direct, inverse, kernel)
    other_1, send_0 = lax.optimization_barrier((other_1, send_0))
    other_0 = swap(send_0)
    both = pl.pallas_call(
        lambda *refs: pair_kernel(layers, *refs),
        out_shape=[unit] * len(steps),
        in_specs=[VMEM] * 4,
        out_specs=[VMEM] * len(steps),
        compiler_params=PARAMS,
    )(keep_0, other_0, keep_1, other_1)
    terms = [give(both[at], *steps[at]) for at in range(len(steps) - 1, 0, -1)] + [both[0]]
    gradient = pl.pallas_call(
        lambda *refs: sum_kernel(1.0 / (count * devices), *refs),
        out_shape=unit,
        in_specs=[VMEM] * len(steps),
        out_specs=VMEM,
        compiler_params=PARAMS,
    )(*terms)
    return jnp.swapaxes(gradient, 2, 3)


def solution(mesh):
    placed = (
        P("group", None, "region", "probe"),
        P("group", None, None),
        P("region", "probe", "group", None),
        P("region", "probe", "group"),
    )
    return jax.shard_map(
        body,
        mesh=mesh,
        in_specs=placed,
        out_specs=P("group", None, "region", "probe"),
        check_vma=False,
    )
```

time: 44.9 us -> 36.9 us (0.82)
  starting transfers between devices: 23 us -> 10.6 us
  waiting for transfers between devices: 9.28 us -> 12.2 us
  local copies, waits for them, and re-layouts: 2.88 us -> 4.76 us
    ppermute x6 -> x3, starting transfers between devices: 8.33 us -> 2.43 us  [give(): return lax.ppermute(value, ('region', 'probe'), route(step, band))]
    ppermute x6 -> x3, starting transfers between devices: 12.5 us -> 6.96 us  [fetch(): lax.ppermute(value, ('region', 'probe'), [(b, a) for a, b in route(step,...]
    unnamed x16 -> x15, local copies, waits for them, and re-layouts: 2.11 us -> 4.76 us
    ppermute x6 -> x3, waiting for transfers between devices: 6.06 us -> 8.11 us  [give(): return lax.ppermute(value, ('region', 'probe'), route(step, band))]
    ppermute x10 -> x6, waiting for transfers between devices: 1.11 us -> 2.45 us  [swap(): return lax.ppermute(value, 'probe', [(i, i ^ 1) for i in range(devices)])]
    ppermute x10 -> x6, starting transfers between devices: 2.22 us -> 1.17 us  [swap(): return lax.ppermute(value, 'probe', [(i, i ^ 1) for i in range(devices)])]
    pallas_call x1 -> x0, local copies, waits for them, and re-layouts: 0.77 us -> none  [body(): pl.pallas_call(lambda *refs: sum_kernel(1.0 / (count * devices), 2 * ring...]
    ppermute x6 -> x3, waiting for transfers between devices: 2.12 us -> 1.61 us  [fetch(): lax.ppermute(value, ('region', 'probe'), [(b, a) for a, b in route(step,...]
  transfers between devices with their start and end apart: 22 -> 12, of which waited for: 7 -> 7; matrix products, arithmetic and copies ran while one was open for 0% -> 0% of each run, Pallas kernels for 6% -> 9%
where the time goes in v2:
time: 36.9 us; the launch traced here: 36.7 us
  waiting for transfers between devices  12.2 us (33%)
  starting transfers between devices  10.6 us (29%)
  Pallas kernels  9.12 us (25%)
  local copies, waits for them, and re-layouts  4.76 us (13%)
    ppermute x3, waiting for transfers between devices, give(): return lax.ppermute(value, ('region', 'probe'), route(step, band))  8.11 us
    ppermute x3, starting transfers between devices, fetch(): lax.ppermute(value, ('region', 'probe'), [(b, a) for a, b in route(step,...  6.96 us
    pallas_call x1, Pallas kernels, body(): pl.pallas_call(lambda *refs: main_kernel(ring, window, *refs), out_shape=...  5 us
    unnamed x15, local copies, waits for them, and re-layouts  4.76 us
    pallas_call x1, Pallas kernels, body(): pl.pallas_call(lambda *refs: last_kernel(ring, window, *refs), out_shape=...  2.73 us
    ppermute x6, waiting for transfers between devices, swap(): return lax.ppermute(value, 'probe', [(i, i ^ 1) for i in range(devices)])  2.45 us
    ppermute x3, starting transfers between devices, give(): return lax.ppermute(value, ('region', 'probe'), route(step, band))  2.43 us
    ppermute x3, waiting for transfers between devices, fetch(): lax.ppermute(value, ('region', 'probe'), [(b, a) for a, b in route(step,...  1.61 us
  transfers between devices with their start and end apart: 12, of which 7 were waited for; matrix products, arithmetic and copies ran while one was open for 0% of the time, Pallas kernels for 9%

profile of v2, /device:TPU:0, one launch (start us, length us, event | category | flops | bytes accessed | tf_op | source)
XLA Modules:
  0.0 36.7 jit_solution(17586574073981750545)
XLA Ops:
  0.0 5.0 %collective-permute-start.2 = (f32[2,2,64,128]{3,2,1,0:T(8,128)}, f32[2,2,64,128]{3,2,1,0:T(8,128)S(1)}, u32[]{:S(2)}, u32[]{:S(2)}) collective-permute-start(f32[2,2,64,128]{3,2,1,0:T(8,128)} %bitcast.2), channel_id=1, source_target_pairs={{4,0},{5,1},{6,2},{7,3},{8,4},{9,5},{10,6},{11,7},{12,8},{13,9},{1... | collective-permute-start | bytes 393224 | tf_op jit(solution)/shard_map/ppermute | solution.py:275
  5.0 1.4 %collective-permute-start.1 = (f32[2,2,64,128]{3,2,1,0:T(8,128)}, f32[2,2,64,128]{3,2,1,0:T(8,128)S(1)}, u32[]{:S(2)}, u32[]{:S(2)}) collective-permute-start(f32[2,2,64,128]{3,2,1,0:T(8,128)} %bitcast.3), channel_id=1, source_target_pairs={{6,0},{7,1},{4,2},{5,3},{10,4},{11,5},{8,6},{9,7},{14,8},{15,9},{1... | collective-permute-start | bytes 393224 | tf_op jit(solution)/shard_map/ppermute | solution.py:275
  6.4 0.5 %collective-permute-start = (f32[2,2,64,128]{3,2,1,0:T(8,128)}, f32[2,2,64,128]{3,2,1,0:T(8,128)S(1)}, u32[]{:S(2)}, u32[]{:S(2)}) collective-permute-start(f32[2,2,64,128]{3,2,1,0:T(8,128)} %bitcast.4), channel_id=1, source_target_pairs={{2,0},{3,1},{0,2},{1,3},{6,4},{7,5},{4,6},{5,7},{10,8},{11,9},{8,1... | collective-permute-start | bytes 393224 | tf_op jit(solution)/shard_map/ppermute | solution.py:275
  7.0 0.0 collective-permute-start.3
  7.0 0.0 copy-start
  7.0 0.9 %copy-done = f32[1,4,128,128]{3,2,1,0:T(8,128)S(1)} copy-done((f32[1,4,128,128]{3,2,1,0:T(8,128)S(1)}, f32[1,4,128,128]{3,2,1,0:T(8,128)}, u32[]{:S(2)}) %copy-start) | copy-done | bytes 262168
  7.9 0.0 copy-start.1
  7.9 0.9 %copy-done.1 = f32[2,128,128]{2,1,0:T(8,128)S(1)} copy-done((f32[2,128,128]{2,1,0:T(8,128)S(1)}, f32[2,128,128]{2,1,0:T(8,128)}, u32[]{:S(2)}) %copy-start.1) | copy-done | bytes 131096
  8.8 0.0 copy-start.3
  8.8 0.9 %copy-done.3 = bf16[2,256,256]{2,1,0:T(8,128)(2,1)S(1)} copy-done((bf16[2,256,256]{2,1,0:T(8,128)(2,1)S(1)}, bf16[2,256,256]{2,1,0:T(8,128)(2,1)}, u32[]{:S(2)}) %copy-start.3) | copy-done | bytes 262168
  9.8 0.0 copy-start.4
  9.8 0.9 %copy-done.4 = bf16[2,256,256]{2,1,0:T(8,128)(2,1)S(1)} copy-done((bf16[2,256,256]{2,1,0:T(8,128)(2,1)S(1)}, bf16[2,256,256]{2,1,0:T(8,128)(2,1)}, u32[]{:S(2)}) %copy-start.4) | copy-done | bytes 262168
  10.7 0.0 copy-start.5
  10.7 0.9 %copy-done.5 = f32[2,128,128]{2,1,0:T(8,128)S(1)} copy-done((f32[2,128,128]{2,1,0:T(8,128)S(1)}, f32[2,128,128]{2,1,0:T(8,128)}, u32[]{:S(2)}) %copy-start.5) | copy-done | bytes 131096
  11.6 0.0 copy-start.2
  11.6 0.7 %shard_map.73 = (f32[2,128,128]{2,1,0:T(8,128)S(1)}, f32[4,128,128]{2,1,0:T(8,128)S(1)}, bf16[2,256,256]{2,1,0:T(8,128)(2,1)S(1)}, bf16[2,256,256]{2,1,0:T(8,128)(2,1)S(1)}, f32[2,128,128]{2,1,0:T(8,128)S(1)}) custom-call(f32[2,128,128]{2,1,0:T(8,128)S(1)} %copy-done.1, f32[1,4,128,128]{3,2,1,0:T(8,128)S(1)} %copy-done, bf16[2,256,256]{2,1,0:T(8,128)(2,1)S(1)} %copy-done.4, ...), custom_call_target="tpu_custom_call" | custom-call | flops 402653184 | bytes 16777216 | tf_op jit(solution)/shard_map/pallas_call | solution.py:282
  12.3 0.0 copy-start.6
  12.3 0.0 collective-permute-done.2.refs_12_
  12.3 0.0 collective-permute-done.1.refs_10_
  12.3 1.6 %collective-permute-done.refs_8_ = f32[2,2,64,128]{3,2,1,0:T(8,128)S(1)} collective-permute-done((f32[2,2,64,128]{3,2,1,0:T(8,128)}, f32[2,2,64,128]{3,2,1,0:T(8,128)S(1)}, u32[]{:S(2)}, u32[]{:S(2)}) %collective-permute-start) | collective-permute-done | bytes 131104 | tf_op jit(solution)/shard_map/ppermute | solution.py:275
  13.9 0.0 collective-permute-start.4
  13.9 0.5 %collective-permute-start.5 = (f32[2,2,64,128]{3,2,1,0:T(8,128)S(1)}, f32[2,2,64,128]{3,2,1,0:T(8,128)S(1)}, u32[]{:S(2)}, u32[]{:S(2)}) collective-permute-start(f32[2,2,64,128]{3,2,1,0:T(8,128)S(1)} %collective-permute-done.1.refs_10_), channel_id=1, source_target_pairs={{0,1},{1,0},{2,3},{3,2},{4,5},{5,4},{6,7},{7,6},{8,9},{9,8},{10,11... | collective-permute-start | bytes 393224 | tf_op jit(solution)/shard_map/ppermute | solution.py:264
  14.4 0.0 collective-permute-start.6
  14.5 0.0 copy-done.6
  14.5 0.1 copy.9.refs_0_
  14.5 0.0 collective-permute-done.3.refs_7_
  14.6 0.7 %collective-permute-done.4.refs_9_ = f32[2,2,64,128]{3,2,1,0:T(8,128)S(1)} collective-permute-done((f32[2,2,64,128]{3,2,1,0:T(8,128)S(1)}, f32[2,2,64,128]{3,2,1,0:T(8,128)S(1)}, u32[]{:S(2)}, u32[]{:S(2)}) %collective-permute-start.4) | collective-permute-done | bytes 131104 | tf_op jit(solution)/shard_map/ppermute | solution.py:264
  15.3 0.2 collective-permute-done.5.refs_11_
  15.5 0.3 collective-permute-done.6.refs_13_
  15.8 0.0 copy-done.2
  15.8 5.0 %shard_map.74 = (f32[4,2,128,128]{3,2,1,0:T(8,128)S(1)}, f32[4,2,64,128]{3,2,1,0:T(8,128)S(1)}, f32[4,2,64,128]{3,2,1,0:T(8,128)S(1)}) custom-call(s32[1,4,2]{2,1,0:T(4,128)S(1)} %copy.9.refs_0_, f32[2,128,128]{2,1,0:T(8,128)S(1)} %get-tuple-element.26.refs_1_, f32[4,128,128]{2,1,0:T(8,128)S(1)} %get-tuple-element.27.refs_2_, ...), custom_call_target="tpu_custom_call" | custom-call | flops 1610612736 | bytes 1048576 | tf_op jit(solution)/shard_map/pallas_call | solution.py:306
  20.8 0.3 collective-permute-start.7
  21.0 2.7 %shard_map.75 = (f32[4,2,64,128]{3,2,1,0:T(8,128)S(1)}, f32[4,2,64,128]{3,2,1,0:T(8,128)S(1)}) custom-call(s32[1,4,2]{2,1,0:T(4,128)S(1)} %copy.9.refs_0_, f32[2,128,128]{2,1,0:T(8,128)S(1)} %get-tuple-element.26.refs_1_, f32[4,2,128,128]{3,2,1,0:T(8,128)S(1)} %get-tuple-element.34.refs_2_, bf16[2,256,256]{2,1,0:T(8,128)(2,1)S(1)} %get-tuple-element.28.refs_3_, ...), custom_call_target="tpu_custom_call" | custom-call | flops 805306368 | bytes 1048576 | tf_op jit(solution)/shard_map/pallas_call | solution.py:316
  23.8 0.0 collective-permute-done.7.refs_3_
  23.8 0.4 %collective-permute-start.8 = (f32[4,2,64,128]{3,2,1,0:T(8,128)S(1)}, f32[4,2,64,128]{3,2,1,0:T(8,128)S(1)}, u32[]{:S(2)}, u32[]{:S(2)}) collective-permute-start(f32[4,2,64,128]{3,2,1,0:T(8,128)S(1)} %get-tuple-element.38), channel_id=1, source_target_pairs={{0,1},{1,0},{2,3},{3,2},{4,5},{5,4},{6,7},{7,6},{8,9},{9,8},{10,11... | collective-permute-start | bytes 786440 | tf_op jit(solution)/shard_map/ppermute | solution.py:264
  24.2 1.2 %collective-permute-done.8.refs_1_ = f32[4,2,64,128]{3,2,1,0:T(8,128)S(1)} collective-permute-done((f32[4,2,64,128]{3,2,1,0:T(8,128)S(1)}, f32[4,2,64,128]{3,2,1,0:T(8,128)S(1)}, u32[]{:S(2)}, u32[]{:S(2)}) %collective-permute-start.8) | collective-permute-done | bytes 262176 | tf_op jit(solution)/shard_map/ppermute | solution.py:264
  25.4 0.1 shard_map.76
  25.5 0.9 %collective-permute-start.9 = (f32[2,2,64,128]{3,2,1,0:T(8,128)S(1)}, f32[2,2,64,128]{3,2,1,0:T(8,128)S(1)}, u32[]{:S(2)}, u32[]{:S(2)}) collective-permute-start(f32[2,2,64,128]{3,2,1,0:T(8,128)S(1)} %get-tuple-element.41), channel_id=1, source_target_pairs={{0,4},{1,5},{2,6},{3,7},{4,8},{5,9},{6,10},{7,11},{8,12},{9,13},{1... | collective-permute-start | bytes 393224 | tf_op jit(solution)/shard_map/ppermute | solution.py:278
  26.4 0.5 %collective-permute-start.10 = (f32[2,2,64,128]{3,2,1,0:T(8,128)S(1)}, f32[2,2,64,128]{3,2,1,0:T(8,128)S(1)}, u32[]{:S(2)}, u32[]{:S(2)}) collective-permute-start(f32[2,2,64,128]{3,2,1,0:T(8,128)S(1)} %get-tuple-element.42), channel_id=1, source_target_pairs={{0,6},{1,7},{2,4},{3,5},{4,10},{5,11},{6,8},{7,9},{8,14},{9,15},{1... | collective-permute-start | bytes 393224 | tf_op jit(solution)/shard_map/ppermute | solution.py:278
  26.9 1.0 %collective-permute-start.11 = (f32[2,2,64,128]{3,2,1,0:T(8,128)S(1)}, f32[2,2,64,128]{3,2,1,0:T(8,128)S(1)}, u32[]{:S(2)}, u32[]{:S(2)}) collective-permute-start(f32[2,2,64,128]{3,2,1,0:T(8,128)S(1)} %get-tuple-element.43), channel_id=1, source_target_pairs={{0,2},{1,3},{2,0},{3,1},{4,6},{5,7},{6,4},{7,5},{8,10},{9,11},{10,... | collective-permute-start | bytes 393224 | tf_op jit(solution)/shard_map/ppermute | solution.py:278
  27.9 5.7 %collective-permute-done.9.refs_0_ = f32[2,2,64,128]{3,2,1,0:T(8,128)S(1)} collective-permute-done((f32[2,2,64,128]{3,2,1,0:T(8,128)S(1)}, f32[2,2,64,128]{3,2,1,0:T(8,128)S(1)}, u32[]{:S(2)}, u32[]{:S(2)}) %collective-permute-start.9) | collective-permute-done | bytes 131104 | tf_op jit(solution)/shard_map/ppermute | solution.py:278
  33.6 2.4 %collective-permute-done.10.refs_1_ = f32[2,2,64,128]{3,2,1,0:T(8,128)S(1)} collective-permute-done((f32[2,2,64,128]{3,2,1,0:T(8,128)S(1)}, f32[2,2,64,128]{3,2,1,0:T(8,128)S(1)}, u32[]{:S(2)}, u32[]{:S(2)}) %collective-permute-start.10) | collective-permute-done | bytes 131104 | tf_op jit(solution)/shard_map/ppermute | solution.py:278
  36.0 0.0 collective-permute-done.11.refs_2_
  36.0 0.7 %shard_map.77 = f32[2,2,64,128]{3,2,1,0:T(8,128)} custom-call(f32[2,2,64,128]{3,2,1,0:T(8,128)S(1)} %collective-permute-done.9.refs_0_, f32[2,2,64,128]{3,2,1,0:T(8,128)S(1)} %collective-permute-done.10.refs_1_, f32[2,2,64,128]{3,2,1,0:T(8,128)S(1)} %collective-permute-done.11.refs_2_, f32[2,2,64,128]{3,2,1,0:T(8,128)S(1)} %get-tuple-element.44.refs_3_), custom_call_target="tpu_custom_call" | custom-call | tf_op jit(solution)/shard_map/pallas_call | solution.py:335
Async XLA Ops:
  0.0 12.3 %collective-permute-start.2 = (f32[2,2,64,128]{3,2,1,0:T(8,128)}, f32[2,2,64,128]{3,2,1,0:T(8,128)S(1)}, u32[]{:S(2)}, u32[]{:S(2)}) collective-permute-start(f32[2,2,64,128]{3,2,1,0:T(8,128)} %bitcast.2), channel_id=1, source_target_pairs={{4,0},{5,1},{6,2},{7,3},{8,4},{9,5},{10,6},{11,7},{12,8},{13,9},{1... | collective-permute-start | bytes 393224 | tf_op jit(solution)/shard_map/ppermute | solution.py:275
  5.0 7.3 %collective-permute-start.1 = (f32[2,2,64,128]{3,2,1,0:T(8,128)}, f32[2,2,64,128]{3,2,1,0:T(8,128)S(1)}, u32[]{:S(2)}, u32[]{:S(2)}) collective-permute-start(f32[2,2,64,128]{3,2,1,0:T(8,128)} %bitcast.3), channel_id=1, source_target_pairs={{6,0},{7,1},{4,2},{5,3},{10,4},{11,5},{8,6},{9,7},{14,8},{15,9},{1... | collective-permute-start | bytes 393224 | tf_op jit(solution)/shard_map/ppermute | solution.py:275
  6.4 7.5 %collective-permute-start = (f32[2,2,64,128]{3,2,1,0:T(8,128)}, f32[2,2,64,128]{3,2,1,0:T(8,128)S(1)}, u32[]{:S(2)}, u32[]{:S(2)}) collective-permute-start(f32[2,2,64,128]{3,2,1,0:T(8,128)} %bitcast.4), channel_id=1, source_target_pairs={{2,0},{3,1},{0,2},{1,3},{6,4},{7,5},{4,6},{5,7},{10,8},{11,9},{8,1... | collective-permute-start | bytes 393224 | tf_op jit(solution)/shard_map/ppermute | solution.py:275
  7.0 7.6 %collective-permute-start.3 = (f32[2,2,64,128]{3,2,1,0:T(8,128)}, f32[2,2,64,128]{3,2,1,0:T(8,128)S(1)}, u32[]{:S(2)}, u32[]{:S(2)}) collective-permute-start(f32[2,2,64,128]{3,2,1,0:T(8,128)} %bitcast.5), channel_id=1, source_target_pairs={{0,1},{1,0},{2,3},{3,2},{4,5},{5,4},{6,7},{7,6},{8,9},{9,8},{10,11... | collective-permute-start | bytes 393224 | tf_op jit(solution)/shard_map/ppermute | solution.py:264
  7.0 1.0 %copy-start = (f32[1,4,128,128]{3,2,1,0:T(8,128)S(1)}, f32[1,4,128,128]{3,2,1,0:T(8,128)}, u32[]{:S(2)}) copy-start(f32[1,4,128,128]{3,2,1,0:T(8,128)} %refs_1_.1) | copy-start | bytes 786436
  7.9 0.9 %copy-start.1 = (f32[2,128,128]{2,1,0:T(8,128)S(1)}, f32[2,128,128]{2,1,0:T(8,128)}, u32[]{:S(2)}) copy-start(f32[2,128,128]{2,1,0:T(8,128)} %refs_0_.3) | copy-start | bytes 393220
  8.8 0.9 %copy-start.3 = (bf16[2,256,256]{2,1,0:T(8,128)(2,1)S(1)}, bf16[2,256,256]{2,1,0:T(8,128)(2,1)}, u32[]{:S(2)}) copy-start(bf16[2,256,256]{2,1,0:T(8,128)(2,1)} %constant.7.clone.refs_3_) | copy-start | bytes 786436
  9.8 0.9 %copy-start.4 = (bf16[2,256,256]{2,1,0:T(8,128)(2,1)S(1)}, bf16[2,256,256]{2,1,0:T(8,128)(2,1)}, u32[]{:S(2)}) copy-start(bf16[2,256,256]{2,1,0:T(8,128)(2,1)} %constant.6.clone.refs_2_) | copy-start | bytes 786436
  10.7 0.9 %copy-start.5 = (f32[2,128,128]{2,1,0:T(8,128)S(1)}, f32[2,128,128]{2,1,0:T(8,128)}, u32[]{:S(2)}) copy-start(f32[2,128,128]{2,1,0:T(8,128)} %constant.8.clone.refs_4_) | copy-start | bytes 393220
  11.6 4.2 %copy-start.2 = (f32[2,2,128,64]{2,3,1,0:T(8,128)S(1)}, f32[2,2,128,64]{2,3,1,0:T(8,128)}, u32[]{:S(2)}) copy-start(f32[2,2,128,64]{2,3,1,0:T(8,128)} %param.7) | copy-start | bytes 393220
  12.3 2.2 %copy-start.6 = (s32[1,4,2]{1,2,0:T(2,128)S(1)}, s32[1,4,2]{1,2,0:T(2,128)}, u32[]{:S(2)}) copy-start(s32[1,4,2]{1,2,0:T(2,128)} %param.10) | copy-start | bytes 100
  13.9 1.3 %collective-permute-start.4 = (f32[2,2,64,128]{3,2,1,0:T(8,128)S(1)}, f32[2,2,64,128]{3,2,1,0:T(8,128)S(1)}, u32[]{:S(2)}, u32[]{:S(2)}) collective-permute-start(f32[2,2,64,128]{3,2,1,0:T(8,128)S(1)} %collective-permute-done.refs_8_), channel_id=1, source_target_pairs={{0,1},{1,0},{2,3},{3,2},{4,5},{5,4},{6,7},{7,6},{8,9},{9,8},{10,11... | collective-permute-start | bytes 393224 | tf_op jit(solution)/shard_map/ppermute | solution.py:264
  13.9 1.5 %collective-permute-start.5 = (f32[2,2,64,128]{3,2,1,0:T(8,128)S(1)}, f32[2,2,64,128]{3,2,1,0:T(8,128)S(1)}, u32[]{:S(2)}, u32[]{:S(2)}) collective-permute-start(f32[2,2,64,128]{3,2,1,0:T(8,128)S(1)} %collective-permute-done.1.refs_10_), channel_id=1, source_target_pairs={{0,1},{1,0},{2,3},{3,2},{4,5},{5,4},{6,7},{7,6},{8,9},{9,8},{10,11... | collective-permute-start | bytes 393224 | tf_op jit(solution)/shard_map/ppermute | solution.py:264
  14.4 1.3 %collective-permute-start.6 = (f32[2,2,64,128]{3,2,1,0:T(8,128)S(1)}, f32[2,2,64,128]{3,2,1,0:T(8,128)S(1)}, u32[]{:S(2)}, u32[]{:S(2)}) collective-permute-start(f32[2,2,64,128]{3,2,1,0:T(8,128)S(1)} %collective-permute-done.2.refs_12_), channel_id=1, source_target_pairs={{0,1},{1,0},{2,3},{3,2},{4,5},{5,4},{6,7},{7,6},{8,9},{9,8},{10,11... | collective-permute-start | bytes 393224 | tf_op jit(solution)/shard_map/ppermute | solution.py:264
  20.8 3.0 %collective-permute-start.7 = (f32[4,2,64,128]{3,2,1,0:T(8,128)S(1)}, f32[4,2,64,128]{3,2,1,0:T(8,128)S(1)}, u32[]{:S(2)}, u32[]{:S(2)}) collective-permute-start(f32[4,2,64,128]{3,2,1,0:T(8,128)S(1)} %get-tuple-element.36), channel_id=1, source_target_pairs={{0,1},{1,0},{2,3},{3,2},{4,5},{5,4},{6,7},{7,6},{8,9},{9,8},{10,11... | collective-permute-start | bytes 786440 | tf_op jit(solution)/shard_map/ppermute | solution.py:264
  23.8 1.6 %collective-permute-start.8 = (f32[4,2,64,128]{3,2,1,0:T(8,128)S(1)}, f32[4,2,64,128]{3,2,1,0:T(8,128)S(1)}, u32[]{:S(2)}, u32[]{:S(2)}) collective-permute-start(f32[4,2,64,128]{3,2,1,0:T(8,128)S(1)} %get-tuple-element.38), channel_id=1, source_target_pairs={{0,1},{1,0},{2,3},{3,2},{4,5},{5,4},{6,7},{7,6},{8,9},{9,8},{10,11... | collective-permute-start | bytes 786440 | tf_op jit(solution)/shard_map/ppermute | solution.py:264
  25.5 8.2 %collective-permute-start.9 = (f32[2,2,64,128]{3,2,1,0:T(8,128)S(1)}, f32[2,2,64,128]{3,2,1,0:T(8,128)S(1)}, u32[]{:S(2)}, u32[]{:S(2)}) collective-permute-start(f32[2,2,64,128]{3,2,1,0:T(8,128)S(1)} %get-tuple-element.41), channel_id=1, source_target_pairs={{0,4},{1,5},{2,6},{3,7},{4,8},{5,9},{6,10},{7,11},{8,12},{9,13},{1... | collective-permute-start | bytes 393224 | tf_op jit(solution)/shard_map/ppermute | solution.py:278
  26.4 9.6 %collective-permute-start.10 = (f32[2,2,64,128]{3,2,1,0:T(8,128)S(1)}, f32[2,2,64,128]{3,2,1,0:T(8,128)S(1)}, u32[]{:S(2)}, u32[]{:S(2)}) collective-permute-start(f32[2,2,64,128]{3,2,1,0:T(8,128)S(1)} %get-tuple-element.42), channel_id=1, source_target_pairs={{0,6},{1,7},{2,4},{3,5},{4,10},{5,11},{6,8},{7,9},{8,14},{9,15},{1... | collective-permute-start | bytes 393224 | tf_op jit(solution)/shard_map/ppermute | solution.py:278
  26.9 9.1 %collective-permute-start.11 = (f32[2,2,64,128]{3,2,1,0:T(8,128)S(1)}, f32[2,2,64,128]{3,2,1,0:T(8,128)S(1)}, u32[]{:S(2)}, u32[]{:S(2)}) collective-permute-start(f32[2,2,64,128]{3,2,1,0:T(8,128)S(1)} %get-tuple-element.43), channel_id=1, source_target_pairs={{0,2},{1,3},{2,0},{3,1},{4,6},{5,7},{6,4},{7,5},{8,10},{9,11},{10,... | collective-permute-start | bytes 393224 | tf_op jit(solution)/shard_map/ppermute | solution.py:278

commit v3 on v2

--- a/solution.py
+++ b/solution.py
@@ -10,6 +10,7 @@
 from jax.sharding import PartitionSpec as P
 
 CORES = 2
+PAIRED = 2
 HALF = 64
 
 
@@ -39,9 +40,9 @@
 
 def times_right(values, table_ref):
     high, low = split(values)
-    table = jnp.concatenate([table_ref[0], table_ref[0], table_ref[1]], axis=0)
-    stacked = jnp.concatenate([high, low, high], axis=1)
-    return jnp.dot(stacked, table, preferred_element_type=jnp.float32)
+    rows = values.shape[0]
+    both = jnp.dot(jnp.concatenate([high, low], axis=0), table_ref[0], preferred_element_type=jnp.float32)
+    return both[:rows] + both[rows:] + jnp.dot(high, table_ref[1], preferred_element_type=jnp.float32)
 
 
 def times_left(table_ref, values):
@@ -65,35 +66,32 @@
     )
 
 
-def part(values, n, c, window):
-    return values[c * window : (c + 1) * window, n * window : (n + 1) * window]
-
-
-def join(pairs):
-    return jnp.concatenate(
-        [jnp.concatenate([re for re, _ in pairs], axis=1), jnp.concatenate([im for _, im in pairs], axis=1)],
-        axis=0,
-    )
-
-
 def lanes(pairs):
     return jnp.concatenate([jnp.concatenate([re, im], axis=1) for re, im in pairs], axis=0)
 
 
+def transform(pairs, right_ref, left_ref, window):
+    halves = [times_right(jnp.concatenate(pair, axis=1), right_ref) for pair in pairs]
+    out = []
+    for at in range(0, len(pairs), PAIRED):
+        group = halves[at : at + PAIRED]
+        rows = [jnp.concatenate([half[:, c * window : (c + 1) * window] for half in group], axis=1) for c in range(2)]
+        whole = times_left(left_ref, jnp.concatenate(rows, axis=0))
+        for n in range(len(group)):
+            columns = slice(n * window, (n + 1) * window)
+            out.append((whole[:window, columns], whole[window:, columns]))
+    return out
+
+
 def fresnel(pairs, direct_ref, inverse_ref, kernel_ref, sign, window):
-    count = len(pairs)
-    half = to_rows(times_right(lanes(pairs), direct_ref), window)
-    spec = times_left(inverse_ref, half)
     k_re, k_im = kernel_ref[0], kernel_ref[1]
     if sign < 0:
         k_im = -k_im
-    moved = []
-    for n in range(count):
-        re, im = part(spec, n, 0, window), part(spec, n, 1, window)
-        moved.append((k_re * re - k_im * im, k_re * im + k_im * re))
-    half = to_rows(times_right(lanes(moved), inverse_ref), window)
-    wave = times_left(direct_ref, half)
-    return [(part(wave, n, 0, window), part(wave, n, 1, window)) for n in range(count)]
+    moved = [
+        (k_re * re - k_im * im, k_re * im + k_im * re)
+        for re, im in transform(pairs, direct_ref, inverse_ref, window)
+    ]
+    return transform(moved, inverse_ref, direct_ref, window)
 
 
 def travel_order(ring):
@@ -180,22 +178,18 @@
         re, im = cut(field_ref, 0, position_ref, n, window)
         exits.append((probe_re * re - probe_im * im, probe_re * im + probe_im * re))
     waves = fresnel(exits, direct_ref, inverse_ref, kernel_ref, 1, window)
-    exits, patches = [], []
+    exits = []
     for n in range(count):
         re, im = cut(field_ref, 1, position_ref, n, window)
         w_re, w_im = waves[n]
         wave_ref[n, 0] = w_re
         wave_ref[n, 1] = w_im
         exits.append((w_re * re - w_im * im, w_re * im + w_im * re))
-    far = times_left(inverse_ref, to_rows(times_right(lanes(exits), direct_ref), window))
     scaled = []
-    for n in range(count):
-        re, im = part(far, n, 0, window), part(far, n, 1, window)
+    for n, (re, im) in enumerate(transform(exits, direct_ref, inverse_ref, window)):
         misfit = re * re + im * im - intensity_ref[n]
         scaled.append((misfit * re, misfit * im))
-    back = times_left(direct_ref, to_rows(times_right(lanes(scaled), inverse_ref), window))
-    for n in range(count):
-        b_re, b_im = part(back, n, 0, window), part(back, n, 1, window)
+    for n, (b_re, b_im) in enumerate(transform(scaled, inverse_ref, direct_ref, window)):
         w_re, w_im = wave_ref[n, 0], wave_ref[n, 1]
         p_re, p_im = cut(field_ref, 1, position_ref, n, window)
         carried_ref[n, 0] = p_re * b_re + p_im * b_im

time: 36.9 us -> 35.1 us (0.951)
  Pallas kernels: 9.12 us -> 7.21 us
    pallas_call x1, Pallas kernels: 5 us -> 3.72 us  [body(): pl.pallas_call(lambda *refs: main_kernel(ring, window, *refs), out_shape=...]
    pallas_call x1, Pallas kernels: 2.73 us -> 2.1 us  [body(): pl.pallas_call(lambda *refs: last_kernel(ring, window, *refs), out_shape=...]
  transfers between devices with their start and end apart: 12 -> 12, of which waited for: 7 -> 7; matrix products, arithmetic and copies ran while one was open for 0% -> 0% of each run, Pallas kernels for 9% -> 8%
where the time goes in v3:
time: 35.1 us; the launch traced here: 34.8 us
  waiting for transfers between devices  12.2 us (35%)
  starting transfers between devices  10.6 us (30%)
  Pallas kernels  7.21 us (21%)
  local copies, waits for them, and re-layouts  4.76 us (14%)
    ppermute x3, waiting for transfers between devices, give(): return lax.ppermute(value, ('region', 'probe'), route(step, band))  8.14 us
    ppermute x3, starting transfers between devices, fetch(): lax.ppermute(value, ('region', 'probe'), [(b, a) for a, b in route(step,...  6.96 us
    unnamed x15, local copies, waits for them, and re-layouts  4.76 us
    pallas_call x1, Pallas kernels, body(): pl.pallas_call(lambda *refs: main_kernel(ring, window, *refs), out_shape=...  3.72 us
    ppermute x6, waiting for transfers between devices, swap(): return lax.ppermute(value, 'probe', [(i, i ^ 1) for i in range(devices)])  2.46 us
    ppermute x3, starting transfers between devices, give(): return lax.ppermute(value, ('region', 'probe'), route(step, band))  2.45 us
    pallas_call x1, Pallas kernels, body(): pl.pallas_call(lambda *refs: last_kernel(ring, window, *refs), out_shape=...  2.1 us
    ppermute x3, waiting for transfers between devices, fetch(): lax.ppermute(value, ('region', 'probe'), [(b, a) for a, b in route(step,...  1.61 us
  transfers between devices with their start and end apart: 12, of which 7 were waited for; matrix products, arithmetic and copies ran while one was open for 0% of the time, Pallas kernels for 8%

profile of v3, /device:TPU:0, one launch (start us, length us, event | category | flops | bytes accessed | tf_op | source)
XLA Modules:
  0.0 34.8 jit_solution(16078415593507762977)
XLA Ops:
  0.0 5.0 %collective-permute-start.2 = (f32[2,2,64,128]{3,2,1,0:T(8,128)}, f32[2,2,64,128]{3,2,1,0:T(8,128)S(1)}, u32[]{:S(2)}, u32[]{:S(2)}) collective-permute-start(f32[2,2,64,128]{3,2,1,0:T(8,128)} %bitcast.2), channel_id=1, source_target_pairs={{4,0},{5,1},{6,2},{7,3},{8,4},{9,5},{10,6},{11,7},{12,8},{13,9},{1... | collective-permute-start | bytes 393224 | tf_op jit(solution)/shard_map/ppermute | solution.py:269
  5.0 1.4 %collective-permute-start.1 = (f32[2,2,64,128]{3,2,1,0:T(8,128)}, f32[2,2,64,128]{3,2,1,0:T(8,128)S(1)}, u32[]{:S(2)}, u32[]{:S(2)}) collective-permute-start(f32[2,2,64,128]{3,2,1,0:T(8,128)} %bitcast.3), channel_id=1, source_target_pairs={{6,0},{7,1},{4,2},{5,3},{10,4},{11,5},{8,6},{9,7},{14,8},{15,9},{1... | collective-permute-start | bytes 393224 | tf_op jit(solution)/shard_map/ppermute | solution.py:269
  6.4 0.5 %collective-permute-start = (f32[2,2,64,128]{3,2,1,0:T(8,128)}, f32[2,2,64,128]{3,2,1,0:T(8,128)S(1)}, u32[]{:S(2)}, u32[]{:S(2)}) collective-permute-start(f32[2,2,64,128]{3,2,1,0:T(8,128)} %bitcast.4), channel_id=1, source_target_pairs={{2,0},{3,1},{0,2},{1,3},{6,4},{7,5},{4,6},{5,7},{10,8},{11,9},{8,1... | collective-permute-start | bytes 393224 | tf_op jit(solution)/shard_map/ppermute | solution.py:269
  7.0 0.0 collective-permute-start.3
  7.0 0.0 copy-start
  7.0 0.9 %copy-done = f32[1,4,128,128]{3,2,1,0:T(8,128)S(1)} copy-done((f32[1,4,128,128]{3,2,1,0:T(8,128)S(1)}, f32[1,4,128,128]{3,2,1,0:T(8,128)}, u32[]{:S(2)}) %copy-start) | copy-done | bytes 262168
  7.9 0.0 copy-start.1
  7.9 0.9 %copy-done.1 = f32[2,128,128]{2,1,0:T(8,128)S(1)} copy-done((f32[2,128,128]{2,1,0:T(8,128)S(1)}, f32[2,128,128]{2,1,0:T(8,128)}, u32[]{:S(2)}) %copy-start.1) | copy-done | bytes 131096
  8.8 0.0 copy-start.3
  8.8 0.9 %copy-done.3 = bf16[2,256,256]{2,1,0:T(8,128)(2,1)S(1)} copy-done((bf16[2,256,256]{2,1,0:T(8,128)(2,1)S(1)}, bf16[2,256,256]{2,1,0:T(8,128)(2,1)}, u32[]{:S(2)}) %copy-start.3) | copy-done | bytes 262168
  9.8 0.0 copy-start.4
  9.8 0.9 %copy-done.4 = bf16[2,256,256]{2,1,0:T(8,128)(2,1)S(1)} copy-done((bf16[2,256,256]{2,1,0:T(8,128)(2,1)S(1)}, bf16[2,256,256]{2,1,0:T(8,128)(2,1)}, u32[]{:S(2)}) %copy-start.4) | copy-done | bytes 262168
  10.7 0.0 copy-start.5
  10.7 0.9 %copy-done.5 = f32[2,128,128]{2,1,0:T(8,128)S(1)} copy-done((f32[2,128,128]{2,1,0:T(8,128)S(1)}, f32[2,128,128]{2,1,0:T(8,128)}, u32[]{:S(2)}) %copy-start.5) | copy-done | bytes 131096
  11.6 0.0 copy-start.2
  11.6 0.7 %shard_map.73 = (f32[2,128,128]{2,1,0:T(8,128)S(1)}, f32[4,128,128]{2,1,0:T(8,128)S(1)}, bf16[2,256,256]{2,1,0:T(8,128)(2,1)S(1)}, bf16[2,256,256]{2,1,0:T(8,128)(2,1)S(1)}, f32[2,128,128]{2,1,0:T(8,128)S(1)}) custom-call(f32[2,128,128]{2,1,0:T(8,128)S(1)} %copy-done.1, f32[1,4,128,128]{3,2,1,0:T(8,128)S(1)} %copy-done, bf16[2,256,256]{2,1,0:T(8,128)(2,1)S(1)} %copy-done.4, ...), custom_call_target="tpu_custom_call" | custom-call | flops 402653184 | bytes 16777216 | tf_op jit(solution)/shard_map/pallas_call | solution.py:276
  12.3 0.0 copy-start.6
  12.3 0.0 collective-permute-done.2.refs_12_
  12.3 0.0 collective-permute-done.1.refs_10_
  12.3 1.6 %collective-permute-done.refs_8_ = f32[2,2,64,128]{3,2,1,0:T(8,128)S(1)} collective-permute-done((f32[2,2,64,128]{3,2,1,0:T(8,128)}, f32[2,2,64,128]{3,2,1,0:T(8,128)S(1)}, u32[]{:S(2)}, u32[]{:S(2)}) %collective-permute-start) | collective-permute-done | bytes 131104 | tf_op jit(solution)/shard_map/ppermute | solution.py:269
  13.9 0.0 collective-permute-start.4
  13.9 0.5 %collective-permute-start.5 = (f32[2,2,64,128]{3,2,1,0:T(8,128)S(1)}, f32[2,2,64,128]{3,2,1,0:T(8,128)S(1)}, u32[]{:S(2)}, u32[]{:S(2)}) collective-permute-start(f32[2,2,64,128]{3,2,1,0:T(8,128)S(1)} %collective-permute-done.1.refs_10_), channel_id=1, source_target_pairs={{0,1},{1,0},{2,3},{3,2},{4,5},{5,4},{6,7},{7,6},{8,9},{9,8},{10,11... | collective-permute-start | bytes 393224 | tf_op jit(solution)/shard_map/ppermute | solution.py:258
  14.4 0.0 collective-permute-start.6
  14.5 0.0 copy-done.6
  14.5 0.1 copy.9.refs_0_
  14.5 0.0 collective-permute-done.3.refs_7_
  14.6 0.7 %collective-permute-done.4.refs_9_ = f32[2,2,64,128]{3,2,1,0:T(8,128)S(1)} collective-permute-done((f32[2,2,64,128]{3,2,1,0:T(8,128)S(1)}, f32[2,2,64,128]{3,2,1,0:T(8,128)S(1)}, u32[]{:S(2)}, u32[]{:S(2)}) %collective-permute-start.4) | collective-permute-done | bytes 131104 | tf_op jit(solution)/shard_map/ppermute | solution.py:258
  15.3 0.2 collective-permute-done.5.refs_11_
  15.5 0.3 collective-permute-done.6.refs_13_
  15.8 0.0 copy-done.2
  15.8 3.7 %shard_map.74 = (f32[4,2,128,128]{3,2,1,0:T(8,128)S(1)}, f32[4,2,64,128]{3,2,1,0:T(8,128)S(1)}, f32[4,2,64,128]{3,2,1,0:T(8,128)S(1)}) custom-call(s32[1,4,2]{2,1,0:T(4,128)S(1)} %copy.9.refs_0_, f32[2,128,128]{2,1,0:T(8,128)S(1)} %get-tuple-element.26.refs_1_, f32[4,128,128]{2,1,0:T(8,128)S(1)} %get-tuple-element.27.refs_2_, ...), custom_call_target="tpu_custom_call" | custom-call | flops 1610612736 | bytes 1048576 | tf_op jit(solution)/shard_map/pallas_call | solution.py:300
  19.5 0.3 collective-permute-start.7
  19.8 2.1 %shard_map.75 = (f32[4,2,64,128]{3,2,1,0:T(8,128)S(1)}, f32[4,2,64,128]{3,2,1,0:T(8,128)S(1)}) custom-call(s32[1,4,2]{2,1,0:T(4,128)S(1)} %copy.9.refs_0_, f32[2,128,128]{2,1,0:T(8,128)S(1)} %get-tuple-element.26.refs_1_, f32[4,2,128,128]{3,2,1,0:T(8,128)S(1)} %get-tuple-element.34.refs_2_, bf16[2,256,256]{2,1,0:T(8,128)(2,1)S(1)} %get-tuple-element.28.refs_3_, ...), custom_call_target="tpu_custom_call" | custom-call | flops 805306368 | bytes 1048576 | tf_op jit(solution)/shard_map/pallas_call | solution.py:310
  21.9 0.0 collective-permute-done.7.refs_3_
  21.9 0.4 %collective-permute-start.8 = (f32[4,2,64,128]{3,2,1,0:T(8,128)S(1)}, f32[4,2,64,128]{3,2,1,0:T(8,128)S(1)}, u32[]{:S(2)}, u32[]{:S(2)}) collective-permute-start(f32[4,2,64,128]{3,2,1,0:T(8,128)S(1)} %get-tuple-element.38), channel_id=1, source_target_pairs={{0,1},{1,0},{2,3},{3,2},{4,5},{5,4},{6,7},{7,6},{8,9},{9,8},{10,11... | collective-permute-start | bytes 786440 | tf_op jit(solution)/shard_map/ppermute | solution.py:258
  22.3 1.2 %collective-permute-done.8.refs_1_ = f32[4,2,64,128]{3,2,1,0:T(8,128)S(1)} collective-permute-done((f32[4,2,64,128]{3,2,1,0:T(8,128)S(1)}, f32[4,2,64,128]{3,2,1,0:T(8,128)S(1)}, u32[]{:S(2)}, u32[]{:S(2)}) %collective-permute-start.8) | collective-permute-done | bytes 262176 | tf_op jit(solution)/shard_map/ppermute | solution.py:258
  23.5 0.1 shard_map.76
  23.6 0.9 %collective-permute-start.9 = (f32[2,2,64,128]{3,2,1,0:T(8,128)S(1)}, f32[2,2,64,128]{3,2,1,0:T(8,128)S(1)}, u32[]{:S(2)}, u32[]{:S(2)}) collective-permute-start(f32[2,2,64,128]{3,2,1,0:T(8,128)S(1)} %get-tuple-element.41), channel_id=1, source_target_pairs={{0,4},{1,5},{2,6},{3,7},{4,8},{5,9},{6,10},{7,11},{8,12},{9,13},{1... | collective-permute-start | bytes 393224 | tf_op jit(solution)/shard_map/ppermute | solution.py:272
  24.5 0.5 %collective-permute-start.10 = (f32[2,2,64,128]{3,2,1,0:T(8,128)S(1)}, f32[2,2,64,128]{3,2,1,0:T(8,128)S(1)}, u32[]{:S(2)}, u32[]{:S(2)}) collective-permute-start(f32[2,2,64,128]{3,2,1,0:T(8,128)S(1)} %get-tuple-element.42), channel_id=1, source_target_pairs={{0,6},{1,7},{2,4},{3,5},{4,10},{5,11},{6,8},{7,9},{8,14},{9,15},{1... | collective-permute-start | bytes 393224 | tf_op jit(solution)/shard_map/ppermute | solution.py:272
  25.0 1.0 %collective-permute-start.11 = (f32[2,2,64,128]{3,2,1,0:T(8,128)S(1)}, f32[2,2,64,128]{3,2,1,0:T(8,128)S(1)}, u32[]{:S(2)}, u32[]{:S(2)}) collective-permute-start(f32[2,2,64,128]{3,2,1,0:T(8,128)S(1)} %get-tuple-element.43), channel_id=1, source_target_pairs={{0,2},{1,3},{2,0},{3,1},{4,6},{5,7},{6,4},{7,5},{8,10},{9,11},{10,... | collective-permute-start | bytes 393224 | tf_op jit(solution)/shard_map/ppermute | solution.py:272
  26.0 5.7 %collective-permute-done.9.refs_0_ = f32[2,2,64,128]{3,2,1,0:T(8,128)S(1)} collective-permute-done((f32[2,2,64,128]{3,2,1,0:T(8,128)S(1)}, f32[2,2,64,128]{3,2,1,0:T(8,128)S(1)}, u32[]{:S(2)}, u32[]{:S(2)}) %collective-permute-start.9) | collective-permute-done | bytes 131104 | tf_op jit(solution)/shard_map/ppermute | solution.py:272
  31.7 2.4 %collective-permute-done.10.refs_1_ = f32[2,2,64,128]{3,2,1,0:T(8,128)S(1)} collective-permute-done((f32[2,2,64,128]{3,2,1,0:T(8,128)S(1)}, f32[2,2,64,128]{3,2,1,0:T(8,128)S(1)}, u32[]{:S(2)}, u32[]{:S(2)}) %collective-permute-start.10) | collective-permute-done | bytes 131104 | tf_op jit(solution)/shard_map/ppermute | solution.py:272
  34.1 0.0 collective-permute-done.11.refs_2_
  34.2 0.7 %shard_map.77 = f32[2,2,64,128]{3,2,1,0:T(8,128)} custom-call(f32[2,2,64,128]{3,2,1,0:T(8,128)S(1)} %collective-permute-done.9.refs_0_, f32[2,2,64,128]{3,2,1,0:T(8,128)S(1)} %collective-permute-done.10.refs_1_, f32[2,2,64,128]{3,2,1,0:T(8,128)S(1)} %collective-permute-done.11.refs_2_, f32[2,2,64,128]{3,2,1,0:T(8,128)S(1)} %get-tuple-element.44.refs_3_), custom_call_target="tpu_custom_call" | custom-call | tf_op jit(solution)/shard_map/pallas_call | solution.py:329
Async XLA Ops:
  0.0 12.3 %collective-permute-start.2 = (f32[2,2,64,128]{3,2,1,0:T(8,128)}, f32[2,2,64,128]{3,2,1,0:T(8,128)S(1)}, u32[]{:S(2)}, u32[]{:S(2)}) collective-permute-start(f32[2,2,64,128]{3,2,1,0:T(8,128)} %bitcast.2), channel_id=1, source_target_pairs={{4,0},{5,1},{6,2},{7,3},{8,4},{9,5},{10,6},{11,7},{12,8},{13,9},{1... | collective-permute-start | bytes 393224 | tf_op jit(solution)/shard_map/ppermute | solution.py:269
  5.0 7.3 %collective-permute-start.1 = (f32[2,2,64,128]{3,2,1,0:T(8,128)}, f32[2,2,64,128]{3,2,1,0:T(8,128)S(1)}, u32[]{:S(2)}, u32[]{:S(2)}) collective-permute-start(f32[2,2,64,128]{3,2,1,0:T(8,128)} %bitcast.3), channel_id=1, source_target_pairs={{6,0},{7,1},{4,2},{5,3},{10,4},{11,5},{8,6},{9,7},{14,8},{15,9},{1... | collective-permute-start | bytes 393224 | tf_op jit(solution)/shard_map/ppermute | solution.py:269
  6.4 7.5 %collective-permute-start = (f32[2,2,64,128]{3,2,1,0:T(8,128)}, f32[2,2,64,128]{3,2,1,0:T(8,128)S(1)}, u32[]{:S(2)}, u32[]{:S(2)}) collective-permute-start(f32[2,2,64,128]{3,2,1,0:T(8,128)} %bitcast.4), channel_id=1, source_target_pairs={{2,0},{3,1},{0,2},{1,3},{6,4},{7,5},{4,6},{5,7},{10,8},{11,9},{8,1... | collective-permute-start | bytes 393224 | tf_op jit(solution)/shard_map/ppermute | solution.py:269
  7.0 7.6 %collective-permute-start.3 = (f32[2,2,64,128]{3,2,1,0:T(8,128)}, f32[2,2,64,128]{3,2,1,0:T(8,128)S(1)}, u32[]{:S(2)}, u32[]{:S(2)}) collective-permute-start(f32[2,2,64,128]{3,2,1,0:T(8,128)} %bitcast.5), channel_id=1, source_target_pairs={{0,1},{1,0},{2,3},{3,2},{4,5},{5,4},{6,7},{7,6},{8,9},{9,8},{10,11... | collective-permute-start | bytes 393224 | tf_op jit(solution)/shard_map/ppermute | solution.py:258
  7.0 1.0 %copy-start = (f32[1,4,128,128]{3,2,1,0:T(8,128)S(1)}, f32[1,4,128,128]{3,2,1,0:T(8,128)}, u32[]{:S(2)}) copy-start(f32[1,4,128,128]{3,2,1,0:T(8,128)} %refs_1_.1) | copy-start | bytes 786436
  7.9 0.9 %copy-start.1 = (f32[2,128,128]{2,1,0:T(8,128)S(1)}, f32[2,128,128]{2,1,0:T(8,128)}, u32[]{:S(2)}) copy-start(f32[2,128,128]{2,1,0:T(8,128)} %refs_0_.3) | copy-start | bytes 393220
  8.8 0.9 %copy-start.3 = (bf16[2,256,256]{2,1,0:T(8,128)(2,1)S(1)}, bf16[2,256,256]{2,1,0:T(8,128)(2,1)}, u32[]{:S(2)}) copy-start(bf16[2,256,256]{2,1,0:T(8,128)(2,1)} %constant.7.clone.refs_3_) | copy-start | bytes 786436
  9.8 0.9 %copy-start.4 = (bf16[2,256,256]{2,1,0:T(8,128)(2,1)S(1)}, bf16[2,256,256]{2,1,0:T(8,128)(2,1)}, u32[]{:S(2)}) copy-start(bf16[2,256,256]{2,1,0:T(8,128)(2,1)} %constant.6.clone.refs_2_) | copy-start | bytes 786436
  10.7 0.9 %copy-start.5 = (f32[2,128,128]{2,1,0:T(8,128)S(1)}, f32[2,128,128]{2,1,0:T(8,128)}, u32[]{:S(2)}) copy-start(f32[2,128,128]{2,1,0:T(8,128)} %constant.8.clone.refs_4_) | copy-start | bytes 393220
  11.6 4.2 %copy-start.2 = (f32[2,2,128,64]{2,3,1,0:T(8,128)S(1)}, f32[2,2,128,64]{2,3,1,0:T(8,128)}, u32[]{:S(2)}) copy-start(f32[2,2,128,64]{2,3,1,0:T(8,128)} %param.7) | copy-start | bytes 393220
  12.3 2.2 %copy-start.6 = (s32[1,4,2]{1,2,0:T(2,128)S(1)}, s32[1,4,2]{1,2,0:T(2,128)}, u32[]{:S(2)}) copy-start(s32[1,4,2]{1,2,0:T(2,128)} %param.10) | copy-start | bytes 100
  13.9 1.3 %collective-permute-start.4 = (f32[2,2,64,128]{3,2,1,0:T(8,128)S(1)}, f32[2,2,64,128]{3,2,1,0:T(8,128)S(1)}, u32[]{:S(2)}, u32[]{:S(2)}) collective-permute-start(f32[2,2,64,128]{3,2,1,0:T(8,128)S(1)} %collective-permute-done.refs_8_), channel_id=1, source_target_pairs={{0,1},{1,0},{2,3},{3,2},{4,5},{5,4},{6,7},{7,6},{8,9},{9,8},{10,11... | collective-permute-start | bytes 393224 | tf_op jit(solution)/shard_map/ppermute | solution.py:258
  13.9 1.5 %collective-permute-start.5 = (f32[2,2,64,128]{3,2,1,0:T(8,128)S(1)}, f32[2,2,64,128]{3,2,1,0:T(8,128)S(1)}, u32[]{:S(2)}, u32[]{:S(2)}) collective-permute-start(f32[2,2,64,128]{3,2,1,0:T(8,128)S(1)} %collective-permute-done.1.refs_10_), channel_id=1, source_target_pairs={{0,1},{1,0},{2,3},{3,2},{4,5},{5,4},{6,7},{7,6},{8,9},{9,8},{10,11... | collective-permute-start | bytes 393224 | tf_op jit(solution)/shard_map/ppermute | solution.py:258
  14.4 1.3 %collective-permute-start.6 = (f32[2,2,64,128]{3,2,1,0:T(8,128)S(1)}, f32[2,2,64,128]{3,2,1,0:T(8,128)S(1)}, u32[]{:S(2)}, u32[]{:S(2)}) collective-permute-start(f32[2,2,64,128]{3,2,1,0:T(8,128)S(1)} %collective-permute-done.2.refs_12_), channel_id=1, source_target_pairs={{0,1},{1,0},{2,3},{3,2},{4,5},{5,4},{6,7},{7,6},{8,9},{9,8},{10,11... | collective-permute-start | bytes 393224 | tf_op jit(solution)/shard_map/ppermute | solution.py:258
  19.5 2.4 %collective-permute-start.7 = (f32[4,2,64,128]{3,2,1,0:T(8,128)S(1)}, f32[4,2,64,128]{3,2,1,0:T(8,128)S(1)}, u32[]{:S(2)}, u32[]{:S(2)}) collective-permute-start(f32[4,2,64,128]{3,2,1,0:T(8,128)S(1)} %get-tuple-element.36), channel_id=1, source_target_pairs={{0,1},{1,0},{2,3},{3,2},{4,5},{5,4},{6,7},{7,6},{8,9},{9,8},{10,11... | collective-permute-start | bytes 786440 | tf_op jit(solution)/shard_map/ppermute | solution.py:258
  21.9 1.6 %collective-permute-start.8 = (f32[4,2,64,128]{3,2,1,0:T(8,128)S(1)}, f32[4,2,64,128]{3,2,1,0:T(8,128)S(1)}, u32[]{:S(2)}, u32[]{:S(2)}) collective-permute-start(f32[4,2,64,128]{3,2,1,0:T(8,128)S(1)} %get-tuple-element.38), channel_id=1, source_target_pairs={{0,1},{1,0},{2,3},{3,2},{4,5},{5,4},{6,7},{7,6},{8,9},{9,8},{10,11... | collective-permute-start | bytes 786440 | tf_op jit(solution)/shard_map/ppermute | solution.py:258
  23.6 8.2 %collective-permute-start.9 = (f32[2,2,64,128]{3,2,1,0:T(8,128)S(1)}, f32[2,2,64,128]{3,2,1,0:T(8,128)S(1)}, u32[]{:S(2)}, u32[]{:S(2)}) collective-permute-start(f32[2,2,64,128]{3,2,1,0:T(8,128)S(1)} %get-tuple-element.41), channel_id=1, source_target_pairs={{0,4},{1,5},{2,6},{3,7},{4,8},{5,9},{6,10},{7,11},{8,12},{9,13},{1... | collective-permute-start | bytes 393224 | tf_op jit(solution)/shard_map/ppermute | solution.py:272
  24.5 9.7 %collective-permute-start.10 = (f32[2,2,64,128]{3,2,1,0:T(8,128)S(1)}, f32[2,2,64,128]{3,2,1,0:T(8,128)S(1)}, u32[]{:S(2)}, u32[]{:S(2)}) collective-permute-start(f32[2,2,64,128]{3,2,1,0:T(8,128)S(1)} %get-tuple-element.42), channel_id=1, source_target_pairs={{0,6},{1,7},{2,4},{3,5},{4,10},{5,11},{6,8},{7,9},{8,14},{9,15},{1... | collective-permute-start | bytes 393224 | tf_op jit(solution)/shard_map/ppermute | solution.py:272
  25.0 9.2 %collective-permute-start.11 = (f32[2,2,64,128]{3,2,1,0:T(8,128)S(1)}, f32[2,2,64,128]{3,2,1,0:T(8,128)S(1)}, u32[]{:S(2)}, u32[]{:S(2)}) collective-permute-start(f32[2,2,64,128]{3,2,1,0:T(8,128)S(1)} %get-tuple-element.43), channel_id=1, source_target_pairs={{0,2},{1,3},{2,0},{3,1},{4,6},{5,7},{6,4},{7,5},{8,10},{9,11},{10,... | collective-permute-start | bytes 393224 | tf_op jit(solution)/shard_map/ppermute | solution.py:272

commit v4 on v3

--- a/solution.py
+++ b/solution.py
@@ -95,7 +95,7 @@
 
 
 def travel_order(ring):
-    return [(0, 0)] + [(step, band) for band in range(2) for step in range(ring - 1, -1, -1) if step or band]
+    return [(0, 0), (0, 1)] + [(step, band) for band in range(2) for step in range(1, ring)]
 
 
 def assemble(unit_refs, field_ref, ring, window):
@@ -137,17 +137,17 @@
         total_ref[c, 1, where, :] += jnp.where(lane < row, turned, 0.0)
 
 
-def hand_out(total_ref, keep_ref, send_ref, ring, window):
+def hand_out(total_ref, layer, keep_refs, send_refs, ring, window):
     me = lax.axis_index("probe")
     x, core = me // CORES, me % CORES
     columns = total_ref.shape[2] - window
     total_ref[:, :, :window, :] += total_ref[:, :, columns:, :]
     for at, (step, band) in enumerate(travel_order(ring)):
         tile = lax.rem(x + step, ring)
-        for owner, ref in ((core, keep_ref), (1 - core, send_ref)):
+        for owner, ref in ((core, keep_refs[at]), (1 - core, send_refs[at])):
             where = pl.ds(pl.multiple_of((tile * CORES + owner) * HALF, HALF), HALF)
             for c in range(2):
-                ref[at, c] = total_ref[c, band, where, :]
+                ref[layer, c] = total_ref[c, band, where, :]
 
 
 def prepare_kernel(*refs):
@@ -168,10 +168,12 @@
 
 
 def main_kernel(ring, window, position_ref, probe_ref, intensity_ref, direct_ref, inverse_ref, kernel_ref, *rest):
-    unit_refs, (carried_ref, keep_ref, send_ref, field_ref, wave_ref, total_ref) = rest[:-6], rest[-6:]
+    unit_refs, rest = rest[: 4 * ring], rest[4 * ring :]
+    keep_refs, send_refs, (field_ref, wave_ref, total_ref, first_total_ref) = rest[: 2 * ring], rest[2 * ring : -4], rest[-4:]
     count = position_ref.shape[1]
     assemble(unit_refs, field_ref, ring, window)
     total_ref[...] = jnp.zeros_like(total_ref)
+    first_total_ref[...] = jnp.zeros_like(first_total_ref)
     probe_re, probe_im = probe_ref[0], probe_ref[1]
     exits = []
     for n in range(count):
@@ -189,35 +191,17 @@
     for n, (re, im) in enumerate(transform(exits, direct_ref, inverse_ref, window)):
         misfit = re * re + im * im - intensity_ref[n]
         scaled.append((misfit * re, misfit * im))
+    carried, gradients = [], []
     for n, (b_re, b_im) in enumerate(transform(scaled, inverse_ref, direct_ref, window)):
         w_re, w_im = wave_ref[n, 0], wave_ref[n, 1]
         p_re, p_im = cut(field_ref, 1, position_ref, n, window)
-        carried_ref[n, 0] = p_re * b_re + p_im * b_im
-        carried_ref[n, 1] = p_re * b_im - p_im * b_re
-        gradient = (w_re * b_re + w_im * b_im, w_re * b_im - w_im * b_re)
-        deposit(total_ref, position_ref, n, gradient, window)
-    hand_out(total_ref, keep_ref, send_ref, ring, window)
-
-
-def last_kernel(
-    ring, window, position_ref, probe_ref, carried_ref, direct_ref, inverse_ref, kernel_ref, keep_ref, send_ref, total_ref
-):
-    count = position_ref.shape[1]
-    total_ref[...] = jnp.zeros_like(total_ref)
-    carried = [(carried_ref[n, 0], carried_ref[n, 1]) for n in range(count)]
-    backs = fresnel(carried, direct_ref, inverse_ref, kernel_ref, -1, window)
-    probe_re, probe_im = probe_ref[0], probe_ref[1]
-    for n, (b_re, b_im) in enumerate(backs):
+        carried.append((p_re * b_re + p_im * b_im, p_re * b_im - p_im * b_re))
+        deposit(total_ref, position_ref, n, (w_re * b_re + w_im * b_im, w_re * b_im - w_im * b_re), window)
+    hand_out(total_ref, 1, keep_refs, send_refs, ring, window)
+    for n, (b_re, b_im) in enumerate(fresnel(carried, direct_ref, inverse_ref, kernel_ref, -1, window)):
         gradient = (probe_re * b_re + probe_im * b_im, probe_re * b_im - probe_im * b_re)
-        deposit(total_ref, position_ref, n, gradient, window)
-    hand_out(total_ref, keep_ref, send_ref, ring, window)
-
-
-def pair_kernel(layers, *refs):
-    inputs, outputs = refs[: 2 * layers], refs[2 * layers :]
-    for layer in range(layers):
-        for at, out_ref in enumerate(outputs):
-            out_ref[layer] = inputs[2 * layer][at] + inputs[2 * layer + 1][at]
+        deposit(first_total_ref, position_ref, n, gradient, window)
+    hand_out(first_total_ref, 0, keep_refs, send_refs, ring, window)
 
 
 def sum_kernel(scale, *refs):
@@ -247,11 +231,9 @@
     columns = devices * width
     direct, inverse, kernel = (jnp.asarray(t) for t in tables(window))
     unit = jax.ShapeDtypeStruct((layers, 2, width, rows), jnp.float32)
-    waves = jax.ShapeDtypeStruct((count, 2, window, window), jnp.float32)
-    units = jax.ShapeDtypeStruct((2 * ring, 2, width, rows), jnp.float32)
     field = pltpu.VMEM((layers, 2, 2, columns + window, rows), jnp.float32)
     total = pltpu.VMEM((2, 2, columns + window, rows), jnp.float32)
-    wave_scratch = pltpu.VMEM(waves.shape, jnp.float32)
+    wave_scratch = pltpu.VMEM((count, 2, window, window), jnp.float32)
     dft_flops = count * 2 * 3 * 2 * window * (2 * window) ** 2
 
     def swap(value):
@@ -290,49 +272,41 @@
             pltpu.SemaphoreType.DMA((5,)),
         ],
         compiler_params=PARAMS,
-        cost_estimate=cost(dft_flops, 16 << 20),
-    )(probe, intensity, direct, inverse, kernel)
+        cost_estimate=cost(1, 1),
+    )(*(pltpu.with_memory_space_constraint(value, pltpu.HBM) for value in (probe, intensity, direct, inverse, kernel)))
     arrived = [tile] + [fetch(tile, *step) for step in steps[1:]]
-    *arrived[1:], probe_t = lax.optimization_barrier((*arrived[1:], probe_t))
-    gathered = []
-    for value in arrived:
-        gathered += [value, swap(value)]
-    carried, keep_1, send_1 = pl.pallas_call(
+    early = [at for at, step in enumerate(steps) if at and not all(step)]
+    late = [at for at, step in enumerate(steps) if all(step)]
+    *values, probe_t = lax.optimization_barrier((*(arrived[at] for at in early), probe_t))
+    arrived = {0: tile, **dict(zip(early, values)), **{at: arrived[at] for at in late}}
+    swapped = {at: swap(arrived[at]) for at in [0] + early}
+    values = lax.optimization_barrier(([arrived[at] for at in late], [swapped[at] for at in early]))
+    arrived.update(zip(late, values[0]))
+    swapped.update(zip(early, values[1]))
+    swapped.update({at: swap(arrived[at]) for at in late})
+    gathered = [value for at in range(len(steps)) for value in (arrived[at], swapped[at])]
+    outputs = pl.pallas_call(
         lambda *refs: main_kernel(ring, window, *refs),
-        out_shape=[waves, units, units],
+        out_shape=[unit] * (2 * len(steps)),
         in_specs=[SMEM] + [VMEM] * (5 + 4 * ring),
-        out_specs=[VMEM] * 3,
-        scratch_shapes=[field, wave_scratch, total],
+        out_specs=[VMEM] * (2 * len(steps)),
+        scratch_shapes=[field, wave_scratch, total, total],
         compiler_params=PARAMS,
-        cost_estimate=cost(4 * dft_flops, 1 << 20),
+        cost_estimate=cost(6 * dft_flops, 8 << 20),
     )(positions, probe_t, intensity_t, direct, inverse, kernel, *gathered)
-    other_1 = swap(send_1)
-    keep_0, send_0 = pl.pallas_call(
-        lambda *refs: last_kernel(ring, window, *refs),
-        out_shape=[units, units],
-        in_specs=[SMEM] + [VMEM] * 5,
-        out_specs=[VMEM] * 2,
-        scratch_shapes=[total],
-        compiler_params=PARAMS,
-        cost_estimate=cost(2 * dft_flops, 1 << 20),
-    )(positions, probe_t, carried, direct, inverse, kernel)
-    other_1, send_0 = lax.optimization_barrier((other_1, send_0))
-    other_0 = swap(send_0)
-    both = pl.pallas_call(
-        lambda *refs: pair_kernel(layers, *refs),
-        out_shape=[unit] * len(steps),
-        in_specs=[VMEM] * 4,
-        out_specs=[VMEM] * len(steps),
-        compiler_params=PARAMS,
-    )(keep_0, other_0, keep_1, other_1)
-    terms = [give(both[at], *steps[at]) for at in range(len(steps) - 1, 0, -1)] + [both[0]]
+    keep, send = outputs[: len(steps)], outputs[len(steps) :]
+    order = late + early
+    other = {at: swap(send[at]) for at in order}
+    own, other[order[0]] = lax.optimization_barrier((send[0], other[order[0]]))
+    terms = [give(keep[at] + other[at], *steps[at]) for at in order]
+    other_own = swap(own)
     gradient = pl.pallas_call(
         lambda *refs: sum_kernel(1.0 / (count * devices), *refs),
         out_shape=unit,
-        in_specs=[VMEM] * len(steps),
+        in_specs=[VMEM] * (len(steps) + 1),
         out_specs=VMEM,
         compiler_params=PARAMS,
-    )(*terms)
+    )(keep[0], other_own, *terms)
     return jnp.swapaxes(gradient, 2, 3)
 
 

time: 35.1 us -> 32.3 us (0.920)
  local copies, waits for them, and re-layouts: 4.76 us -> 0.1 us
  waiting for transfers between devices: 12.2 us -> 13.5 us
  starting transfers between devices: 10.6 us -> 11.5 us
    unnamed x15 -> x5, local copies, waits for them, and re-layouts: 4.76 us -> 0.1 us
    ppermute x3, waiting for transfers between devices: 1.61 us -> 3.86 us  [fetch(): lax.ppermute(value, ('region', 'probe'), [(b, a) for a, b in route(step,...]
    pallas_call x2 -> x0, Pallas kernels: 2.16 us -> none  [the longest x1 2.1 us: body(): pl.pallas_call(lambda *refs: last_kernel(ring, window, *refs), out_shape=...]
    pallas_call x1, Pallas kernels: 3.72 us -> 5.05 us  [body(): pl.pallas_call(lambda *refs: main_kernel(ring, window, *refs), out_shape=...]
    ppermute x3, starting transfers between devices: 2.45 us -> 3.27 us  [give(): return lax.ppermute(value, ('region', 'probe'), route(step, band))]
    pallas_call x1, Pallas kernels: 0.65 us -> 1.25 us  [body(): pl.pallas_call(prepare_kernel, out_shape=[jax.ShapeDtypeStruct(probe.shap...]
    ppermute x6 -> x8, waiting for transfers between devices: 2.46 us -> 1.93 us  [swap(): return lax.ppermute(value, 'probe', [(i, i ^ 1) for i in range(devices)])]
    ppermute x3, waiting for transfers between devices: 8.14 us -> 7.71 us  [give(): return lax.ppermute(value, ('region', 'probe'), route(step, band))]
  transfers between devices with their start and end apart: 12 -> 14, of which waited for: 7 -> 7; matrix products, arithmetic and copies ran while one was open for 0% -> 0% of each run, Pallas kernels for 8% -> 4%
where the time goes in v4:
time: 32.3 us; the launch traced here: 32.2 us
  waiting for transfers between devices  13.5 us (42%)
  starting transfers between devices  11.5 us (36%)
  Pallas kernels  6.99 us (22%)
    ppermute x3, waiting for transfers between devices, give(): return lax.ppermute(value, ('region', 'probe'), route(step, band))  7.71 us
    ppermute x3, starting transfers between devices, fetch(): lax.ppermute(value, ('region', 'probe'), [(b, a) for a, b in route(step,...  6.96 us
    pallas_call x1, Pallas kernels, body(): pl.pallas_call(lambda *refs: main_kernel(ring, window, *refs), out_shape=...  5.05 us
    ppermute x3, waiting for transfers between devices, fetch(): lax.ppermute(value, ('region', 'probe'), [(b, a) for a, b in route(step,...  3.86 us
    ppermute x3, starting transfers between devices, give(): return lax.ppermute(value, ('region', 'probe'), route(step, band))  3.27 us
    ppermute x8, waiting for transfers between devices, swap(): return lax.ppermute(value, 'probe', [(i, i ^ 1) for i in range(devices)])  1.93 us
    pallas_call x1, Pallas kernels, body(): pl.pallas_call(prepare_kernel, out_shape=[jax.ShapeDtypeStruct(probe.shap...  1.25 us
    ppermute x8, starting transfers between devices, swap(): return lax.ppermute(value, 'probe', [(i, i ^ 1) for i in range(devices)])  1.25 us
  transfers between devices with their start and end apart: 14, of which 7 were waited for; matrix products, arithmetic and copies ran while one was open for 0% of the time, Pallas kernels for 4%

profile of v4, /device:TPU:0, one launch (start us, length us, event | category | flops | bytes accessed | tf_op | source)
XLA Modules:
  0.0 32.2 jit_solution(5071671277541763036)
XLA Ops:
  0.0 0.0 copy-start
  0.0 2.9 %collective-permute-start.1 = (f32[2,2,64,128]{3,2,1,0:T(8,128)}, f32[2,2,64,128]{3,2,1,0:T(8,128)S(1)}, u32[]{:S(2)}, u32[]{:S(2)}) collective-permute-start(f32[2,2,64,128]{3,2,1,0:T(8,128)} %bitcast.2), channel_id=1, source_target_pairs={{2,0},{3,1},{0,2},{1,3},{6,4},{7,5},{4,6},{5,7},{10,8},{11,9},{8,1... | collective-permute-start | bytes 393224 | tf_op jit(solution)/shard_map/ppermute | solution.py:251
  2.9 3.6 %collective-permute-start = (f32[2,2,64,128]{3,2,1,0:T(8,128)}, f32[2,2,64,128]{3,2,1,0:T(8,128)S(1)}, u32[]{:S(2)}, u32[]{:S(2)}) collective-permute-start(f32[2,2,64,128]{3,2,1,0:T(8,128)} %bitcast.3), channel_id=1, source_target_pairs={{4,0},{5,1},{6,2},{7,3},{8,4},{9,5},{10,6},{11,7},{12,8},{13,9},{1... | collective-permute-start | bytes 393224 | tf_op jit(solution)/shard_map/ppermute | solution.py:251
  6.5 0.4 %collective-permute-start.3 = (f32[2,2,64,128]{3,2,1,0:T(8,128)}, f32[2,2,64,128]{3,2,1,0:T(8,128)S(1)}, u32[]{:S(2)}, u32[]{:S(2)}) collective-permute-start(f32[2,2,64,128]{3,2,1,0:T(8,128)} %bitcast.4), channel_id=1, source_target_pairs={{6,0},{7,1},{4,2},{5,3},{10,4},{11,5},{8,6},{9,7},{14,8},{15,9},{1... | collective-permute-start | bytes 393224 | tf_op jit(solution)/shard_map/ppermute | solution.py:251
  7.0 1.3 %shard_map.73 = (f32[2,128,128]{2,1,0:T(8,128)S(1)}, f32[4,128,128]{2,1,0:T(8,128)S(1)}, bf16[2,256,256]{2,1,0:T(8,128)(2,1)S(1)}, bf16[2,256,256]{2,1,0:T(8,128)(2,1)S(1)}, f32[2,128,128]{2,1,0:T(8,128)S(1)}) custom-call(f32[2,128,128]{2,1,0:T(8,128)} %refs_0_.2, f32[1,4,128,128]{3,2,1,0:T(8,128)} %refs_1_.1, bf16[2,256,256]{2,1,0:T(8,128)(2,1)} %constant.6.clone.refs_2_, ...), custom_call_target="tpu_custom_call" | custom-call | flops 1 | bytes 1 | tf_op jit(solution)/shard_map/pallas_call | solution.py:258
  8.2 0.0 copy-start.1
  8.2 0.0 collective-permute-done.1.refs_10_
  8.2 2.5 %collective-permute-done.refs_8_ = f32[2,2,64,128]{3,2,1,0:T(8,128)S(1)} collective-permute-done((f32[2,2,64,128]{3,2,1,0:T(8,128)}, f32[2,2,64,128]{3,2,1,0:T(8,128)S(1)}, u32[]{:S(2)}, u32[]{:S(2)}) %collective-permute-start) | collective-permute-done | bytes 131104 | tf_op jit(solution)/shard_map/ppermute | solution.py:251
  10.7 0.0 collective-permute-start.4
  10.7 0.5 %collective-permute-start.5 = (f32[2,2,64,128]{3,2,1,0:T(8,128)S(1)}, f32[2,2,64,128]{3,2,1,0:T(8,128)S(1)}, u32[]{:S(2)}, u32[]{:S(2)}) collective-permute-start(f32[2,2,64,128]{3,2,1,0:T(8,128)S(1)} %collective-permute-done.1.refs_10_), channel_id=1, source_target_pairs={{0,1},{1,0},{2,3},{3,2},{4,5},{5,4},{6,7},{7,6},{8,9},{9,8},{10,11... | collective-permute-start | bytes 393224 | tf_op jit(solution)/shard_map/ppermute | solution.py:240
  11.3 0.0 copy-done
  11.3 0.0 collective-permute-start.2
  11.3 1.4 %collective-permute-done.3.refs_12_ = f32[2,2,64,128]{3,2,1,0:T(8,128)S(1)} collective-permute-done((f32[2,2,64,128]{3,2,1,0:T(8,128)}, f32[2,2,64,128]{3,2,1,0:T(8,128)S(1)}, u32[]{:S(2)}, u32[]{:S(2)}) %collective-permute-start.3) | collective-permute-done | bytes 131104 | tf_op jit(solution)/shard_map/ppermute | solution.py:251
  12.6 0.0 collective-permute-done.4.refs_9_
  12.6 0.0 collective-permute-done.5.refs_11_
  12.6 0.0 collective-permute-start.6
  12.6 0.0 copy-done.1
  12.6 0.1 copy.8.refs_0_
  12.7 0.0 collective-permute-done.2.refs_7_
  12.7 1.2 %collective-permute-done.6.refs_13_ = f32[2,2,64,128]{3,2,1,0:T(8,128)S(1)} collective-permute-done((f32[2,2,64,128]{3,2,1,0:T(8,128)S(1)}, f32[2,2,64,128]{3,2,1,0:T(8,128)S(1)}, u32[]{:S(2)}, u32[]{:S(2)}) %collective-permute-start.6) | collective-permute-done | bytes 131104 | tf_op jit(solution)/shard_map/ppermute | solution.py:240
  14.0 5.1 %shard_map.74 = (f32[2,2,64,128]{3,2,1,0:T(8,128)S(1)}, f32[2,2,64,128]{3,2,1,0:T(8,128)S(1)}, f32[2,2,64,128]{3,2,1,0:T(8,128)S(1)}, f32[2,2,64,128]{3,2,1,0:T(...) custom-call(s32[1,4,2]{2,1,0:T(4,128)S(1)} %copy.8.refs_0_, ...), custom_call_target="tpu_custom_call" | custom-call | flops 2415919104 | bytes 8388608 | tf_op jit(solution)/shard_map/pallas_call | solution.py:288
  19.0 0.2 collective-permute-start.7
  19.3 0.4 %collective-permute-start.10 = (f32[2,2,64,128]{3,2,1,0:T(8,128)S(1)}, f32[2,2,64,128]{3,2,1,0:T(8,128)S(1)}, u32[]{:S(2)}, u32[]{:S(2)}) collective-permute-start(f32[2,2,64,128]{3,2,1,0:T(8,128)S(1)} %get-tuple-element.44), channel_id=1, source_target_pairs={{0,1},{1,0},{2,3},{3,2},{4,5},{5,4},{6,7},{7,6},{8,9},{9,8},{10,11... | collective-permute-start | bytes 393224 | tf_op jit(solution)/shard_map/ppermute | solution.py:240
  19.6 0.2 collective-permute-start.12
  19.8 0.7 %collective-permute-done.7 = f32[2,2,64,128]{3,2,1,0:T(8,128)S(1)} collective-permute-done((f32[2,2,64,128]{3,2,1,0:T(8,128)S(1)}, f32[2,2,64,128]{3,2,1,0:T(8,128)S(1)}, u32[]{:S(2)}, u32[]{:S(2)}) %collective-permute-start.7) | collective-permute-done | bytes 131104 | tf_op jit(solution)/shard_map/ppermute | solution.py:240
  20.5 0.8 %collective-permute-start.9 = (f32[2,2,64,128]{3,2,1,0:T(8,128)S(1)}, f32[2,2,64,128]{3,2,1,0:T(8,128)S(1)}, u32[]{:S(2)}, u32[]{:S(2)}) collective-permute-start(f32[2,2,64,128]{3,2,1,0:T(8,128)S(1)} %add.9), channel_id=1, source_target_pairs={{0,6},{1,7},{2,4},{3,5},{4,10},{5,11},{6,8},{7,9},{8,14},{9,15},{1... | collective-permute-start | bytes 393224 | tf_op jit(solution)/shard_map/ppermute | solution.py:254
  21.3 0.0 collective-permute-start.8
  21.3 0.0 collective-permute-done.10
  21.3 1.7 %collective-permute-start.11 = (f32[2,2,64,128]{3,2,1,0:T(8,128)S(1)}, f32[2,2,64,128]{3,2,1,0:T(8,128)S(1)}, u32[]{:S(2)}, u32[]{:S(2)}) collective-permute-start(f32[2,2,64,128]{3,2,1,0:T(8,128)S(1)} %add.10), channel_id=1, source_target_pairs={{0,4},{1,5},{2,6},{3,7},{4,8},{5,9},{6,10},{7,11},{8,12},{9,13},{1... | collective-permute-start | bytes 393224 | tf_op jit(solution)/shard_map/ppermute | solution.py:254
  23.0 0.0 collective-permute-done.12
  23.0 0.8 %collective-permute-start.13 = (f32[2,2,64,128]{3,2,1,0:T(8,128)S(1)}, f32[2,2,64,128]{3,2,1,0:T(8,128)S(1)}, u32[]{:S(2)}, u32[]{:S(2)}) collective-permute-start(f32[2,2,64,128]{3,2,1,0:T(8,128)S(1)} %add.11), channel_id=1, source_target_pairs={{0,2},{1,3},{2,0},{3,1},{4,6},{5,7},{6,4},{7,5},{8,10},{9,11},{10,... | collective-permute-start | bytes 393224 | tf_op jit(solution)/shard_map/ppermute | solution.py:254
  23.8 5.8 %collective-permute-done.9.refs_2_ = f32[2,2,64,128]{3,2,1,0:T(8,128)S(1)} collective-permute-done((f32[2,2,64,128]{3,2,1,0:T(8,128)S(1)}, f32[2,2,64,128]{3,2,1,0:T(8,128)S(1)}, u32[]{:S(2)}, u32[]{:S(2)}) %collective-permute-start.9) | collective-permute-done | bytes 131104 | tf_op jit(solution)/shard_map/ppermute | solution.py:254
  29.6 0.0 collective-permute-done.8.refs_1_
  29.6 1.6 %collective-permute-done.11.refs_3_ = f32[2,2,64,128]{3,2,1,0:T(8,128)S(1)} collective-permute-done((f32[2,2,64,128]{3,2,1,0:T(8,128)S(1)}, f32[2,2,64,128]{3,2,1,0:T(8,128)S(1)}, u32[]{:S(2)}, u32[]{:S(2)}) %collective-permute-start.11) | collective-permute-done | bytes 131104 | tf_op jit(solution)/shard_map/ppermute | solution.py:254
  31.2 0.3 collective-permute-done.13.refs_4_
  31.5 0.7 %shard_map.75 = f32[2,2,64,128]{3,2,1,0:T(8,128)} custom-call(f32[2,2,64,128]{3,2,1,0:T(8,128)S(1)} %get-tuple-element.37.refs_0_, f32[2,2,64,128]{3,2,1,0:T(8,128)S(1)} %collective-permute-done.8.refs_1_, f32[2,2,64,128]{3,2,1,0:T(8,128)S(1)} %collective-permute-done.9.refs_2_, f32[2,2,64,128]{3,2,1,0:T(8,128)S(1)} %collective-permute-done.11.refs_3_, ...), custom_call_target="tpu_custom_call" | custom-call | tf_op jit(solution)/shard_map/pallas_call | solution.py:303
  (3 shorter events, 0.0 us)
Async XLA Ops:
  0.0 11.3 %copy-start = (f32[2,2,128,64]{2,3,1,0:T(8,128)S(1)}, f32[2,2,128,64]{2,3,1,0:T(8,128)}, u32[]{:S(2)}) copy-start(f32[2,2,128,64]{2,3,1,0:T(8,128)} %param.7) | copy-start | bytes 393220
  0.0 8.2 %collective-permute-start.1 = (f32[2,2,64,128]{3,2,1,0:T(8,128)}, f32[2,2,64,128]{3,2,1,0:T(8,128)S(1)}, u32[]{:S(2)}, u32[]{:S(2)}) collective-permute-start(f32[2,2,64,128]{3,2,1,0:T(8,128)} %bitcast.2), channel_id=1, source_target_pairs={{2,0},{3,1},{0,2},{1,3},{6,4},{7,5},{4,6},{5,7},{10,8},{11,9},{8,1... | collective-permute-start | bytes 393224 | tf_op jit(solution)/shard_map/ppermute | solution.py:251
  2.9 7.8 %collective-permute-start = (f32[2,2,64,128]{3,2,1,0:T(8,128)}, f32[2,2,64,128]{3,2,1,0:T(8,128)S(1)}, u32[]{:S(2)}, u32[]{:S(2)}) collective-permute-start(f32[2,2,64,128]{3,2,1,0:T(8,128)} %bitcast.3), channel_id=1, source_target_pairs={{4,0},{5,1},{6,2},{7,3},{8,4},{9,5},{10,6},{11,7},{12,8},{13,9},{1... | collective-permute-start | bytes 393224 | tf_op jit(solution)/shard_map/ppermute | solution.py:251
  6.5 6.1 %collective-permute-start.3 = (f32[2,2,64,128]{3,2,1,0:T(8,128)}, f32[2,2,64,128]{3,2,1,0:T(8,128)S(1)}, u32[]{:S(2)}, u32[]{:S(2)}) collective-permute-start(f32[2,2,64,128]{3,2,1,0:T(8,128)} %bitcast.4), channel_id=1, source_target_pairs={{6,0},{7,1},{4,2},{5,3},{10,4},{11,5},{8,6},{9,7},{14,8},{15,9},{1... | collective-permute-start | bytes 393224 | tf_op jit(solution)/shard_map/ppermute | solution.py:251
  8.2 4.4 %copy-start.1 = (s32[1,4,2]{1,2,0:T(2,128)S(1)}, s32[1,4,2]{1,2,0:T(2,128)}, u32[]{:S(2)}) copy-start(s32[1,4,2]{1,2,0:T(2,128)} %param.10) | copy-start | bytes 100
  10.7 1.9 %collective-permute-start.4 = (f32[2,2,64,128]{3,2,1,0:T(8,128)S(1)}, f32[2,2,64,128]{3,2,1,0:T(8,128)S(1)}, u32[]{:S(2)}, u32[]{:S(2)}) collective-permute-start(f32[2,2,64,128]{3,2,1,0:T(8,128)S(1)} %collective-permute-done.refs_8_), channel_id=1, source_target_pairs={{0,1},{1,0},{2,3},{3,2},{4,5},{5,4},{6,7},{7,6},{8,9},{9,8},{10,11... | collective-permute-start | bytes 393224 | tf_op jit(solution)/shard_map/ppermute | solution.py:240
  10.7 1.9 %collective-permute-start.5 = (f32[2,2,64,128]{3,2,1,0:T(8,128)S(1)}, f32[2,2,64,128]{3,2,1,0:T(8,128)S(1)}, u32[]{:S(2)}, u32[]{:S(2)}) collective-permute-start(f32[2,2,64,128]{3,2,1,0:T(8,128)S(1)} %collective-permute-done.1.refs_10_), channel_id=1, source_target_pairs={{0,1},{1,0},{2,3},{3,2},{4,5},{5,4},{6,7},{7,6},{8,9},{9,8},{10,11... | collective-permute-start | bytes 393224 | tf_op jit(solution)/shard_map/ppermute | solution.py:240
  11.3 1.5 %collective-permute-start.2 = (f32[2,2,64,128]{3,2,1,0:T(8,128)S(1)}, f32[2,2,64,128]{3,2,1,0:T(8,128)S(1)}, u32[]{:S(2)}, u32[]{:S(2)}) collective-permute-start(f32[2,2,64,128]{3,2,1,0:T(8,128)S(1)} %bitcast.5), channel_id=1, source_target_pairs={{0,1},{1,0},{2,3},{3,2},{4,5},{5,4},{6,7},{7,6},{8,9},{9,8},{10,11... | collective-permute-start | bytes 393224 | tf_op jit(solution)/shard_map/ppermute | solution.py:240
  12.6 1.4 %collective-permute-start.6 = (f32[2,2,64,128]{3,2,1,0:T(8,128)S(1)}, f32[2,2,64,128]{3,2,1,0:T(8,128)S(1)}, u32[]{:S(2)}, u32[]{:S(2)}) collective-permute-start(f32[2,2,64,128]{3,2,1,0:T(8,128)S(1)} %collective-permute-done.3.refs_12_), channel_id=1, source_target_pairs={{0,1},{1,0},{2,3},{3,2},{4,5},{5,4},{6,7},{7,6},{8,9},{9,8},{10,11... | collective-permute-start | bytes 393224 | tf_op jit(solution)/shard_map/ppermute | solution.py:240
  19.0 1.4 %collective-permute-start.7 = (f32[2,2,64,128]{3,2,1,0:T(8,128)S(1)}, f32[2,2,64,128]{3,2,1,0:T(8,128)S(1)}, u32[]{:S(2)}, u32[]{:S(2)}) collective-permute-start(f32[2,2,64,128]{3,2,1,0:T(8,128)S(1)} %get-tuple-element.39), channel_id=1, source_target_pairs={{0,1},{1,0},{2,3},{3,2},{4,5},{5,4},{6,7},{7,6},{8,9},{9,8},{10,11... | collective-permute-start | bytes 393224 | tf_op jit(solution)/shard_map/ppermute | solution.py:240
  19.3 2.0 %collective-permute-start.10 = (f32[2,2,64,128]{3,2,1,0:T(8,128)S(1)}, f32[2,2,64,128]{3,2,1,0:T(8,128)S(1)}, u32[]{:S(2)}, u32[]{:S(2)}) collective-permute-start(f32[2,2,64,128]{3,2,1,0:T(8,128)S(1)} %get-tuple-element.44), channel_id=1, source_target_pairs={{0,1},{1,0},{2,3},{3,2},{4,5},{5,4},{6,7},{7,6},{8,9},{9,8},{10,11... | collective-permute-start | bytes 393224 | tf_op jit(solution)/shard_map/ppermute | solution.py:240
  19.6 3.4 %collective-permute-start.12 = (f32[2,2,64,128]{3,2,1,0:T(8,128)S(1)}, f32[2,2,64,128]{3,2,1,0:T(8,128)S(1)}, u32[]{:S(2)}, u32[]{:S(2)}) collective-permute-start(f32[2,2,64,128]{3,2,1,0:T(8,128)S(1)} %get-tuple-element.46), channel_id=1, source_target_pairs={{0,1},{1,0},{2,3},{3,2},{4,5},{5,4},{6,7},{7,6},{8,9},{9,8},{10,11... | collective-permute-start | bytes 393224 | tf_op jit(solution)/shard_map/ppermute | solution.py:240
  20.5 9.1 %collective-permute-start.9 = (f32[2,2,64,128]{3,2,1,0:T(8,128)S(1)}, f32[2,2,64,128]{3,2,1,0:T(8,128)S(1)}, u32[]{:S(2)}, u32[]{:S(2)}) collective-permute-start(f32[2,2,64,128]{3,2,1,0:T(8,128)S(1)} %add.9), channel_id=1, source_target_pairs={{0,6},{1,7},{2,4},{3,5},{4,10},{5,11},{6,8},{7,9},{8,14},{9,15},{1... | collective-permute-start | bytes 393224 | tf_op jit(solution)/shard_map/ppermute | solution.py:254
  21.3 8.3 %collective-permute-start.8 = (f32[2,2,64,128]{3,2,1,0:T(8,128)S(1)}, f32[2,2,64,128]{3,2,1,0:T(8,128)S(1)}, u32[]{:S(2)}, u32[]{:S(2)}) collective-permute-start(f32[2,2,64,128]{3,2,1,0:T(8,128)S(1)} %get-tuple-element.40), channel_id=1, source_target_pairs={{0,1},{1,0},{2,3},{3,2},{4,5},{5,4},{6,7},{7,6},{8,9},{9,8},{10,11... | collective-permute-start | bytes 393224 | tf_op jit(solution)/shard_map/ppermute | solution.py:240
  21.3 9.9 %collective-permute-start.11 = (f32[2,2,64,128]{3,2,1,0:T(8,128)S(1)}, f32[2,2,64,128]{3,2,1,0:T(8,128)S(1)}, u32[]{:S(2)}, u32[]{:S(2)}) collective-permute-start(f32[2,2,64,128]{3,2,1,0:T(8,128)S(1)} %add.10), channel_id=1, source_target_pairs={{0,4},{1,5},{2,6},{3,7},{4,8},{5,9},{6,10},{7,11},{8,12},{9,13},{1... | collective-permute-start | bytes 393224 | tf_op jit(solution)/shard_map/ppermute | solution.py:254
  23.0 8.5 %collective-permute-start.13 = (f32[2,2,64,128]{3,2,1,0:T(8,128)S(1)}, f32[2,2,64,128]{3,2,1,0:T(8,128)S(1)}, u32[]{:S(2)}, u32[]{:S(2)}) collective-permute-start(f32[2,2,64,128]{3,2,1,0:T(8,128)S(1)} %add.11), channel_id=1, source_target_pairs={{0,2},{1,3},{2,0},{3,1},{4,6},{5,7},{6,4},{7,5},{8,10},{9,11},{10,... | collective-permute-start | bytes 393224 | tf_op jit(solution)/shard_map/ppermute | solution.py:254

commit v5 on v4

--- a/solution.py
+++ b/solution.py
@@ -20,16 +20,18 @@
     return np.stack([high, low])
 
 
+def as_real(table):
+    return np.block([[table.real, table.imag], [-table.imag, table.real]])
+
+
 def tables(window):
     indices = np.arange(window)
     angles = 2.0 * math.pi * ((indices[:, None] * indices[None, :]) % window) / window
-    real, imag = np.cos(angles) / math.sqrt(window), -np.sin(angles) / math.sqrt(window)
-    direct = np.block([[real, imag], [-imag, real]])
-    inverse = np.block([[real, -imag], [imag, real]])
+    transform = np.exp(-1j * angles) / math.sqrt(window)
     frequency = np.where(indices < window // 2, indices, indices - window) / window
-    phases = -60.0 * (frequency[:, None] ** 2 + frequency[None, :] ** 2)
-    kernel = np.stack([np.cos(phases), np.sin(phases)]).astype(np.float32)
-    return split_table(direct), split_table(inverse), kernel
+    step = (transform.conj() * np.exp(-60j * frequency**2)) @ transform
+    step = (step + step.T) / 2
+    return np.stack([split_table(as_real(m)) for m in (transform, transform.conj(), step, step.conj())])
 
 
 def split(values):
@@ -50,24 +52,6 @@
     table = jnp.concatenate([table_ref[0], table_ref[0], table_ref[1]], axis=1)
     stacked = jnp.concatenate([high, low, high], axis=0)
     return jnp.dot(table, stacked, preferred_element_type=jnp.float32)
-
-
-def to_rows(values, window):
-    count = values.shape[0] // window
-    return jnp.concatenate(
-        [
-            jnp.concatenate(
-                [values[n * window : (n + 1) * window, c * window : (c + 1) * window] for n in range(count)],
-                axis=1,
-            )
-            for c in range(2)
-        ],
-        axis=0,
-    )
-
-
-def lanes(pairs):
-    return jnp.concatenate([jnp.concatenate([re, im], axis=1) for re, im in pairs], axis=0)
 
 
 def transform(pairs, right_ref, left_ref, window):
@@ -81,17 +65,6 @@
             columns = slice(n * window, (n + 1) * window)
             out.append((whole[:window, columns], whole[window:, columns]))
     return out
-
-
-def fresnel(pairs, direct_ref, inverse_ref, kernel_ref, sign, window):
-    k_re, k_im = kernel_ref[0], kernel_ref[1]
-    if sign < 0:
-        k_im = -k_im
-    moved = [
-        (k_re * re - k_im * im, k_re * im + k_im * re)
-        for re, im in transform(pairs, direct_ref, inverse_ref, window)
-    ]
-    return transform(moved, inverse_ref, direct_ref, window)
 
 
 def travel_order(ring):
@@ -151,8 +124,8 @@
 
 
 def prepare_kernel(*refs):
-    sources, outputs = refs[:5], refs[5:10]
-    probe_ref, intensity_ref, sems = refs[10:]
+    sources, outputs = refs[:3], refs[3:6]
+    probe_ref, intensity_ref, sems = refs[6:]
     targets = (probe_ref, intensity_ref) + outputs[2:]
     copies = [pltpu.make_async_copy(a, b, sems.at[i]) for i, (a, b) in enumerate(zip(sources, targets))]
     for copy in copies:
@@ -167,7 +140,8 @@
         copy.wait()
 
 
-def main_kernel(ring, window, position_ref, probe_ref, intensity_ref, direct_ref, inverse_ref, kernel_ref, *rest):
+def main_kernel(ring, window, position_ref, probe_ref, intensity_ref, table_ref, *rest):
+    direct_ref, inverse_ref, forth_ref, back_ref = (table_ref.at[i] for i in range(4))
     unit_refs, rest = rest[: 4 * ring], rest[4 * ring :]
     keep_refs, send_refs, (field_ref, wave_ref, total_ref, first_total_ref) = rest[: 2 * ring], rest[2 * ring : -4], rest[-4:]
     count = position_ref.shape[1]
@@ -179,7 +153,7 @@
     for n in range(count):
         re, im = cut(field_ref, 0, position_ref, n, window)
         exits.append((probe_re * re - probe_im * im, probe_re * im + probe_im * re))
-    waves = fresnel(exits, direct_ref, inverse_ref, kernel_ref, 1, window)
+    waves = transform(exits, forth_ref, back_ref, window)
     exits = []
     for n in range(count):
         re, im = cut(field_ref, 1, position_ref, n, window)
@@ -198,7 +172,7 @@
         carried.append((p_re * b_re + p_im * b_im, p_re * b_im - p_im * b_re))
         deposit(total_ref, position_ref, n, (w_re * b_re + w_im * b_im, w_re * b_im - w_im * b_re), window)
     hand_out(total_ref, 1, keep_refs, send_refs, ring, window)
-    for n, (b_re, b_im) in enumerate(fresnel(carried, direct_ref, inverse_ref, kernel_ref, -1, window)):
+    for n, (b_re, b_im) in enumerate(transform(carried, back_ref, forth_ref, window)):
         gradient = (probe_re * b_re + probe_im * b_im, probe_re * b_im - probe_im * b_re)
         deposit(first_total_ref, position_ref, n, gradient, window)
     hand_out(first_total_ref, 0, keep_refs, send_refs, ring, window)
@@ -229,7 +203,7 @@
     devices = lax.axis_size("probe")
     ring = devices // CORES
     columns = devices * width
-    direct, inverse, kernel = (jnp.asarray(t) for t in tables(window))
+    table = jnp.asarray(tables(window))
     unit = jax.ShapeDtypeStruct((layers, 2, width, rows), jnp.float32)
     field = pltpu.VMEM((layers, 2, 2, columns + window, rows), jnp.float32)
     total = pltpu.VMEM((2, 2, columns + window, rows), jnp.float32)
@@ -255,25 +229,23 @@
 
     steps = travel_order(ring)
     tile = jnp.swapaxes(object_slices, 2, 3)
-    probe_t, intensity_t, direct, inverse, kernel = pl.pallas_call(
+    probe_t, intensity_t, table = pl.pallas_call(
         prepare_kernel,
         out_shape=[
             jax.ShapeDtypeStruct(probe.shape, jnp.float32),
             jax.ShapeDtypeStruct(intensity.shape[1:], jnp.float32),
-            jax.ShapeDtypeStruct(direct.shape, direct.dtype),
-            jax.ShapeDtypeStruct(inverse.shape, inverse.dtype),
-            jax.ShapeDtypeStruct(kernel.shape, kernel.dtype),
+            jax.ShapeDtypeStruct(table.shape, table.dtype),
         ],
-        in_specs=[HBM] * 5,
-        out_specs=[VMEM] * 5,
+        in_specs=[HBM] * 3,
+        out_specs=[VMEM] * 3,
         scratch_shapes=[
             pltpu.VMEM(probe.shape, jnp.float32),
             pltpu.VMEM(intensity.shape, jnp.float32),
-            pltpu.SemaphoreType.DMA((5,)),
+            pltpu.SemaphoreType.DMA((3,)),
         ],
         compiler_params=PARAMS,
         cost_estimate=cost(1, 1),
-    )(*(pltpu.with_memory_space_constraint(value, pltpu.HBM) for value in (probe, intensity, direct, inverse, kernel)))
+    )(*(pltpu.with_memory_space_constraint(value, pltpu.HBM) for value in (probe, intensity, table)))
     arrived = [tile] + [fetch(tile, *step) for step in steps[1:]]
     early = [at for at, step in enumerate(steps) if at and not all(step)]
     late = [at for at, step in enumerate(steps) if all(step)]
@@ -288,14 +260,14 @@
     outputs = pl.pallas_call(
         lambda *refs: main_kernel(ring, window, *refs),
         out_shape=[unit] * (2 * len(steps)),
-        in_specs=[SMEM] + [VMEM] * (5 + 4 * ring),
+        in_specs=[SMEM] + [VMEM] * (3 + 4 * ring),
         out_specs=[VMEM] * (2 * len(steps)),
         scratch_shapes=[field, wave_scratch, total, total],
         compiler_params=PARAMS,
-        cost_estimate=cost(6 * dft_flops, 8 << 20),
-    )(positions, probe_t, intensity_t, direct, inverse, kernel, *gathered)
+        cost_estimate=cost(4 * dft_flops, 8 << 20),
+    )(positions, probe_t, intensity_t, table, *gathered)
     keep, send = outputs[: len(steps)], outputs[len(steps) :]
-    order = late + early
+    order = late + early[::-1]
     other = {at: swap(send[at]) for at in order}
     own, other[order[0]] = lax.optimization_barrier((send[0], other[order[0]]))
     terms = [give(keep[at] + other[at], *steps[at]) for at in order]

time: 32.3 us -> 30.9 us (0.957)
  Pallas kernels: 6.99 us -> 5.95 us
  waiting for transfers between devices: 13.5 us -> 13 us
    pallas_call x1, Pallas kernels: 5.05 us -> 3.85 us  [body(): pl.pallas_call(lambda *refs: main_kernel(ring, window, *refs), out_shape=...]
  transfers between devices with their start and end apart: 14 -> 14, of which waited for: 7 -> 7; matrix products, arithmetic and copies ran while one was open for 0% -> 0% of each run, Pallas kernels for 4% -> 5%
where the time goes in v5:
time: 30.9 us; the launch traced here: 30.7 us
  waiting for transfers between devices  13 us (42%)
  starting transfers between devices  11.5 us (37%)
  Pallas kernels  5.95 us (19%)
    ppermute x3, waiting for transfers between devices, give(): return lax.ppermute(value, ('region', 'probe'), route(step, band))  7.4 us
    ppermute x3, starting transfers between devices, fetch(): lax.ppermute(value, ('region', 'probe'), [(b, a) for a, b in route(step,...  6.96 us
    pallas_call x1, Pallas kernels, body(): pl.pallas_call(lambda *refs: main_kernel(ring, window, *refs), out_shape=...  3.85 us
    ppermute x3, waiting for transfers between devices, fetch(): lax.ppermute(value, ('region', 'probe'), [(b, a) for a, b in route(step,...  3.7 us
    ppermute x3, starting transfers between devices, give(): return lax.ppermute(value, ('region', 'probe'), route(step, band))  3.29 us
    ppermute x8, waiting for transfers between devices, swap(): return lax.ppermute(value, 'probe', [(i, i ^ 1) for i in range(devices)])  1.91 us
    pallas_call x1, Pallas kernels, body(): pl.pallas_call(prepare_kernel, out_shape=[jax.ShapeDtypeStruct(probe.shap...  1.41 us
    ppermute x8, starting transfers between devices, swap(): return lax.ppermute(value, 'probe', [(i, i ^ 1) for i in range(devices)])  1.27 us
  transfers between devices with their start and end apart: 14, of which 7 were waited for; matrix products, arithmetic and copies ran while one was open for 0% of the time, Pallas kernels for 5%

profile of v5, /device:TPU:0, one launch (start us, length us, event | category | flops | bytes accessed | tf_op | source)
XLA Modules:
  0.0 30.7 jit_solution(17224248650559757889)
XLA Ops:
  0.0 0.0 copy-start
  0.0 2.9 %collective-permute-start.1 = (f32[2,2,64,128]{3,2,1,0:T(8,128)}, f32[2,2,64,128]{3,2,1,0:T(8,128)S(1)}, u32[]{:S(2)}, u32[]{:S(2)}) collective-permute-start(f32[2,2,64,128]{3,2,1,0:T(8,128)} %bitcast.2), channel_id=1, source_target_pairs={{2,0},{3,1},{0,2},{1,3},{6,4},{7,5},{4,6},{5,7},{10,8},{11,9},{8,1... | collective-permute-start | bytes 393224 | tf_op jit(solution)/shard_map/ppermute | solution.py:225
  2.9 3.6 %collective-permute-start = (f32[2,2,64,128]{3,2,1,0:T(8,128)}, f32[2,2,64,128]{3,2,1,0:T(8,128)S(1)}, u32[]{:S(2)}, u32[]{:S(2)}) collective-permute-start(f32[2,2,64,128]{3,2,1,0:T(8,128)} %bitcast.3), channel_id=1, source_target_pairs={{4,0},{5,1},{6,2},{7,3},{8,4},{9,5},{10,6},{11,7},{12,8},{13,9},{1... | collective-permute-start | bytes 393224 | tf_op jit(solution)/shard_map/ppermute | solution.py:225
  6.5 0.4 %collective-permute-start.3 = (f32[2,2,64,128]{3,2,1,0:T(8,128)}, f32[2,2,64,128]{3,2,1,0:T(8,128)S(1)}, u32[]{:S(2)}, u32[]{:S(2)}) collective-permute-start(f32[2,2,64,128]{3,2,1,0:T(8,128)} %bitcast.4), channel_id=1, source_target_pairs={{6,0},{7,1},{4,2},{5,3},{10,4},{11,5},{8,6},{9,7},{14,8},{15,9},{1... | collective-permute-start | bytes 393224 | tf_op jit(solution)/shard_map/ppermute | solution.py:225
  7.0 1.4 %shard_map.55 = (f32[2,128,128]{2,1,0:T(8,128)S(1)}, f32[4,128,128]{2,1,0:T(8,128)S(1)}, bf16[4,2,256,256]{3,2,1,0:T(8,128)(2,1)S(1)}) custom-call(f32[2,128,128]{2,1,0:T(8,128)} %refs_0_.2, f32[1,4,128,128]{3,2,1,0:T(8,128)} %refs_1_.1, bf16[4,2,256,256]{3,2,1,0:T(8,128)(2,1)} %constant.2.clone.refs_2_), custom_call_target="tpu_custom_call" | custom-call | flops 1 | bytes 1 | tf_op jit(solution)/shard_map/pallas_call | solution.py:232
  8.4 0.0 copy-start.1
  8.4 0.0 collective-permute-done.1.refs_8_
  8.4 2.3 %collective-permute-done.refs_6_ = f32[2,2,64,128]{3,2,1,0:T(8,128)S(1)} collective-permute-done((f32[2,2,64,128]{3,2,1,0:T(8,128)}, f32[2,2,64,128]{3,2,1,0:T(8,128)S(1)}, u32[]{:S(2)}, u32[]{:S(2)}) %collective-permute-start) | collective-permute-done | bytes 131104 | tf_op jit(solution)/shard_map/ppermute | solution.py:225
  10.7 0.0 collective-permute-start.4
  10.7 0.5 %collective-permute-start.5 = (f32[2,2,64,128]{3,2,1,0:T(8,128)S(1)}, f32[2,2,64,128]{3,2,1,0:T(8,128)S(1)}, u32[]{:S(2)}, u32[]{:S(2)}) collective-permute-start(f32[2,2,64,128]{3,2,1,0:T(8,128)S(1)} %collective-permute-done.1.refs_8_), channel_id=1, source_target_pairs={{0,1},{1,0},{2,3},{3,2},{4,5},{5,4},{6,7},{7,6},{8,9},{9,8},{10,11... | collective-permute-start | bytes 393224 | tf_op jit(solution)/shard_map/ppermute | solution.py:214
  11.3 0.0 copy-done
  11.3 0.0 collective-permute-start.2
  11.3 1.4 %collective-permute-done.3.refs_10_ = f32[2,2,64,128]{3,2,1,0:T(8,128)S(1)} collective-permute-done((f32[2,2,64,128]{3,2,1,0:T(8,128)}, f32[2,2,64,128]{3,2,1,0:T(8,128)S(1)}, u32[]{:S(2)}, u32[]{:S(2)}) %collective-permute-start.3) | collective-permute-done | bytes 131104 | tf_op jit(solution)/shard_map/ppermute | solution.py:225
  12.6 0.0 collective-permute-done.4.refs_7_
  12.6 0.0 collective-permute-done.5.refs_9_
  12.6 0.0 collective-permute-start.6
  12.6 0.0 copy-done.1
  12.6 0.1 copy.6.refs_0_
  12.7 0.0 collective-permute-done.2.refs_5_
  12.7 1.2 %collective-permute-done.6.refs_11_ = f32[2,2,64,128]{3,2,1,0:T(8,128)S(1)} collective-permute-done((f32[2,2,64,128]{3,2,1,0:T(8,128)S(1)}, f32[2,2,64,128]{3,2,1,0:T(8,128)S(1)}, u32[]{:S(2)}, u32[]{:S(2)}) %collective-permute-start.6) | collective-permute-done | bytes 131104 | tf_op jit(solution)/shard_map/ppermute | solution.py:214
  14.0 3.9 %shard_map.56 = (f32[2,2,64,128]{3,2,1,0:T(8,128)S(1)}, f32[2,2,64,128]{3,2,1,0:T(8,128)S(1)}, f32[2,2,64,128]{3,2,1,0:T(8,128)S(1)}, f32[2,2,64,128]{3,2,1,0:T(...) custom-call(s32[1,4,2]{2,1,0:T(4,128)S(1)} %copy.6.refs_0_, ...), custom_call_target="tpu_custom_call" | custom-call | flops 1610612736 | bytes 8388608 | tf_op jit(solution)/shard_map/pallas_call | solution.py:260
  17.8 0.2 collective-permute-start.7
  18.1 0.3 %collective-permute-start.10 = (f32[2,2,64,128]{3,2,1,0:T(8,128)S(1)}, f32[2,2,64,128]{3,2,1,0:T(8,128)S(1)}, u32[]{:S(2)}, u32[]{:S(2)}) collective-permute-start(f32[2,2,64,128]{3,2,1,0:T(8,128)S(1)} %get-tuple-element.40), channel_id=1, source_target_pairs={{0,1},{1,0},{2,3},{3,2},{4,5},{5,4},{6,7},{7,6},{8,9},{9,8},{10,11... | collective-permute-start | bytes 393224 | tf_op jit(solution)/shard_map/ppermute | solution.py:214
  18.4 0.2 collective-permute-start.12
  18.6 0.7 %collective-permute-done.7 = f32[2,2,64,128]{3,2,1,0:T(8,128)S(1)} collective-permute-done((f32[2,2,64,128]{3,2,1,0:T(8,128)S(1)}, f32[2,2,64,128]{3,2,1,0:T(8,128)S(1)}, u32[]{:S(2)}, u32[]{:S(2)}) %collective-permute-start.7) | collective-permute-done | bytes 131104 | tf_op jit(solution)/shard_map/ppermute | solution.py:214
  19.3 0.9 %collective-permute-start.9 = (f32[2,2,64,128]{3,2,1,0:T(8,128)S(1)}, f32[2,2,64,128]{3,2,1,0:T(8,128)S(1)}, u32[]{:S(2)}, u32[]{:S(2)}) collective-permute-start(f32[2,2,64,128]{3,2,1,0:T(8,128)S(1)} %add.9), channel_id=1, source_target_pairs={{0,6},{1,7},{2,4},{3,5},{4,10},{5,11},{6,8},{7,9},{8,14},{9,15},{1... | collective-permute-start | bytes 393224 | tf_op jit(solution)/shard_map/ppermute | solution.py:228
  20.1 0.0 collective-permute-start.8
  20.1 0.0 collective-permute-done.10
  20.2 0.8 %collective-permute-start.11 = (f32[2,2,64,128]{3,2,1,0:T(8,128)S(1)}, f32[2,2,64,128]{3,2,1,0:T(8,128)S(1)}, u32[]{:S(2)}, u32[]{:S(2)}) collective-permute-start(f32[2,2,64,128]{3,2,1,0:T(8,128)S(1)} %add.10), channel_id=1, source_target_pairs={{0,2},{1,3},{2,0},{3,1},{4,6},{5,7},{6,4},{7,5},{8,10},{9,11},{10,... | collective-permute-start | bytes 393224 | tf_op jit(solution)/shard_map/ppermute | solution.py:228
  20.9 0.0 collective-permute-done.12
  21.0 1.7 %collective-permute-start.13 = (f32[2,2,64,128]{3,2,1,0:T(8,128)S(1)}, f32[2,2,64,128]{3,2,1,0:T(8,128)S(1)}, u32[]{:S(2)}, u32[]{:S(2)}) collective-permute-start(f32[2,2,64,128]{3,2,1,0:T(8,128)S(1)} %add.11), channel_id=1, source_target_pairs={{0,4},{1,5},{2,6},{3,7},{4,8},{5,9},{6,10},{7,11},{8,12},{9,13},{1... | collective-permute-start | bytes 393224 | tf_op jit(solution)/shard_map/ppermute | solution.py:228
  22.6 5.8 %collective-permute-done.9.refs_2_ = f32[2,2,64,128]{3,2,1,0:T(8,128)S(1)} collective-permute-done((f32[2,2,64,128]{3,2,1,0:T(8,128)S(1)}, f32[2,2,64,128]{3,2,1,0:T(8,128)S(1)}, u32[]{:S(2)}, u32[]{:S(2)}) %collective-permute-start.9) | collective-permute-done | bytes 131104 | tf_op jit(solution)/shard_map/ppermute | solution.py:228
  28.4 0.0 collective-permute-done.8.refs_1_
  28.4 0.6 %collective-permute-done.11.refs_3_ = f32[2,2,64,128]{3,2,1,0:T(8,128)S(1)} collective-permute-done((f32[2,2,64,128]{3,2,1,0:T(8,128)S(1)}, f32[2,2,64,128]{3,2,1,0:T(8,128)S(1)}, u32[]{:S(2)}, u32[]{:S(2)}) %collective-permute-start.11) | collective-permute-done | bytes 131104 | tf_op jit(solution)/shard_map/ppermute | solution.py:228
  29.0 1.1 %collective-permute-done.13.refs_4_ = f32[2,2,64,128]{3,2,1,0:T(8,128)S(1)} collective-permute-done((f32[2,2,64,128]{3,2,1,0:T(8,128)S(1)}, f32[2,2,64,128]{3,2,1,0:T(8,128)S(1)}, u32[]{:S(2)}, u32[]{:S(2)}) %collective-permute-start.13) | collective-permute-done | bytes 131104 | tf_op jit(solution)/shard_map/ppermute | solution.py:228
  30.0 0.7 %shard_map.57 = f32[2,2,64,128]{3,2,1,0:T(8,128)} custom-call(f32[2,2,64,128]{3,2,1,0:T(8,128)S(1)} %get-tuple-element.33.refs_0_, f32[2,2,64,128]{3,2,1,0:T(8,128)S(1)} %collective-permute-done.8.refs_1_, f32[2,2,64,128]{3,2,1,0:T(8,128)S(1)} %collective-permute-done.9.refs_2_, f32[2,2,64,128]{3,2,1,0:T(8,128)S(1)} %collective-permute-done.11.refs_3_, ...), custom_call_target="tpu_custom_call" | custom-call | tf_op jit(solution)/shard_map/pallas_call | solution.py:275
  (3 shorter events, 0.0 us)
Async XLA Ops:
  0.0 11.3 %copy-start = (f32[2,2,128,64]{2,3,1,0:T(8,128)S(1)}, f32[2,2,128,64]{2,3,1,0:T(8,128)}, u32[]{:S(2)}) copy-start(f32[2,2,128,64]{2,3,1,0:T(8,128)} %param.5) | copy-start | bytes 393220
  0.0 8.4 %collective-permute-start.1 = (f32[2,2,64,128]{3,2,1,0:T(8,128)}, f32[2,2,64,128]{3,2,1,0:T(8,128)S(1)}, u32[]{:S(2)}, u32[]{:S(2)}) collective-permute-start(f32[2,2,64,128]{3,2,1,0:T(8,128)} %bitcast.2), channel_id=1, source_target_pairs={{2,0},{3,1},{0,2},{1,3},{6,4},{7,5},{4,6},{5,7},{10,8},{11,9},{8,1... | collective-permute-start | bytes 393224 | tf_op jit(solution)/shard_map/ppermute | solution.py:225
  2.9 7.8 %collective-permute-start = (f32[2,2,64,128]{3,2,1,0:T(8,128)}, f32[2,2,64,128]{3,2,1,0:T(8,128)S(1)}, u32[]{:S(2)}, u32[]{:S(2)}) collective-permute-start(f32[2,2,64,128]{3,2,1,0:T(8,128)} %bitcast.3), channel_id=1, source_target_pairs={{4,0},{5,1},{6,2},{7,3},{8,4},{9,5},{10,6},{11,7},{12,8},{13,9},{1... | collective-permute-start | bytes 393224 | tf_op jit(solution)/shard_map/ppermute | solution.py:225
  6.5 6.1 %collective-permute-start.3 = (f32[2,2,64,128]{3,2,1,0:T(8,128)}, f32[2,2,64,128]{3,2,1,0:T(8,128)S(1)}, u32[]{:S(2)}, u32[]{:S(2)}) collective-permute-start(f32[2,2,64,128]{3,2,1,0:T(8,128)} %bitcast.4), channel_id=1, source_target_pairs={{6,0},{7,1},{4,2},{5,3},{10,4},{11,5},{8,6},{9,7},{14,8},{15,9},{1... | collective-permute-start | bytes 393224 | tf_op jit(solution)/shard_map/ppermute | solution.py:225
  8.4 4.3 %copy-start.1 = (s32[1,4,2]{1,2,0:T(2,128)S(1)}, s32[1,4,2]{1,2,0:T(2,128)}, u32[]{:S(2)}) copy-start(s32[1,4,2]{1,2,0:T(2,128)} %param.8) | copy-start | bytes 100
  10.7 1.9 %collective-permute-start.4 = (f32[2,2,64,128]{3,2,1,0:T(8,128)S(1)}, f32[2,2,64,128]{3,2,1,0:T(8,128)S(1)}, u32[]{:S(2)}, u32[]{:S(2)}) collective-permute-start(f32[2,2,64,128]{3,2,1,0:T(8,128)S(1)} %collective-permute-done.refs_6_), channel_id=1, source_target_pairs={{0,1},{1,0},{2,3},{3,2},{4,5},{5,4},{6,7},{7,6},{8,9},{9,8},{10,11... | collective-permute-start | bytes 393224 | tf_op jit(solution)/shard_map/ppermute | solution.py:214
  10.7 1.9 %collective-permute-start.5 = (f32[2,2,64,128]{3,2,1,0:T(8,128)S(1)}, f32[2,2,64,128]{3,2,1,0:T(8,128)S(1)}, u32[]{:S(2)}, u32[]{:S(2)}) collective-permute-start(f32[2,2,64,128]{3,2,1,0:T(8,128)S(1)} %collective-permute-done.1.refs_8_), channel_id=1, source_target_pairs={{0,1},{1,0},{2,3},{3,2},{4,5},{5,4},{6,7},{7,6},{8,9},{9,8},{10,11... | collective-permute-start | bytes 393224 | tf_op jit(solution)/shard_map/ppermute | solution.py:214
  11.3 1.5 %collective-permute-start.2 = (f32[2,2,64,128]{3,2,1,0:T(8,128)S(1)}, f32[2,2,64,128]{3,2,1,0:T(8,128)S(1)}, u32[]{:S(2)}, u32[]{:S(2)}) collective-permute-start(f32[2,2,64,128]{3,2,1,0:T(8,128)S(1)} %bitcast.5), channel_id=1, source_target_pairs={{0,1},{1,0},{2,3},{3,2},{4,5},{5,4},{6,7},{7,6},{8,9},{9,8},{10,11... | collective-permute-start | bytes 393224 | tf_op jit(solution)/shard_map/ppermute | solution.py:214
  12.6 1.4 %collective-permute-start.6 = (f32[2,2,64,128]{3,2,1,0:T(8,128)S(1)}, f32[2,2,64,128]{3,2,1,0:T(8,128)S(1)}, u32[]{:S(2)}, u32[]{:S(2)}) collective-permute-start(f32[2,2,64,128]{3,2,1,0:T(8,128)S(1)} %collective-permute-done.3.refs_10_), channel_id=1, source_target_pairs={{0,1},{1,0},{2,3},{3,2},{4,5},{5,4},{6,7},{7,6},{8,9},{9,8},{10,11... | collective-permute-start | bytes 393224 | tf_op jit(solution)/shard_map/ppermute | solution.py:214
  17.8 1.4 %collective-permute-start.7 = (f32[2,2,64,128]{3,2,1,0:T(8,128)S(1)}, f32[2,2,64,128]{3,2,1,0:T(8,128)S(1)}, u32[]{:S(2)}, u32[]{:S(2)}) collective-permute-start(f32[2,2,64,128]{3,2,1,0:T(8,128)S(1)} %get-tuple-element.35), channel_id=1, source_target_pairs={{0,1},{1,0},{2,3},{3,2},{4,5},{5,4},{6,7},{7,6},{8,9},{9,8},{10,11... | collective-permute-start | bytes 393224 | tf_op jit(solution)/shard_map/ppermute | solution.py:214
  18.1 2.1 %collective-permute-start.10 = (f32[2,2,64,128]{3,2,1,0:T(8,128)S(1)}, f32[2,2,64,128]{3,2,1,0:T(8,128)S(1)}, u32[]{:S(2)}, u32[]{:S(2)}) collective-permute-start(f32[2,2,64,128]{3,2,1,0:T(8,128)S(1)} %get-tuple-element.40), channel_id=1, source_target_pairs={{0,1},{1,0},{2,3},{3,2},{4,5},{5,4},{6,7},{7,6},{8,9},{9,8},{10,11... | collective-permute-start | bytes 393224 | tf_op jit(solution)/shard_map/ppermute | solution.py:214
  18.4 2.5 %collective-permute-start.12 = (f32[2,2,64,128]{3,2,1,0:T(8,128)S(1)}, f32[2,2,64,128]{3,2,1,0:T(8,128)S(1)}, u32[]{:S(2)}, u32[]{:S(2)}) collective-permute-start(f32[2,2,64,128]{3,2,1,0:T(8,128)S(1)} %get-tuple-element.42), channel_id=1, source_target_pairs={{0,1},{1,0},{2,3},{3,2},{4,5},{5,4},{6,7},{7,6},{8,9},{9,8},{10,11... | collective-permute-start | bytes 393224 | tf_op jit(solution)/shard_map/ppermute | solution.py:214
  19.3 9.1 %collective-permute-start.9 = (f32[2,2,64,128]{3,2,1,0:T(8,128)S(1)}, f32[2,2,64,128]{3,2,1,0:T(8,128)S(1)}, u32[]{:S(2)}, u32[]{:S(2)}) collective-permute-start(f32[2,2,64,128]{3,2,1,0:T(8,128)S(1)} %add.9), channel_id=1, source_target_pairs={{0,6},{1,7},{2,4},{3,5},{4,10},{5,11},{6,8},{7,9},{8,14},{9,15},{1... | collective-permute-start | bytes 393224 | tf_op jit(solution)/shard_map/ppermute | solution.py:228
  20.1 8.2 %collective-permute-start.8 = (f32[2,2,64,128]{3,2,1,0:T(8,128)S(1)}, f32[2,2,64,128]{3,2,1,0:T(8,128)S(1)}, u32[]{:S(2)}, u32[]{:S(2)}) collective-permute-start(f32[2,2,64,128]{3,2,1,0:T(8,128)S(1)} %get-tuple-element.36), channel_id=1, source_target_pairs={{0,1},{1,0},{2,3},{3,2},{4,5},{5,4},{6,7},{7,6},{8,9},{9,8},{10,11... | collective-permute-start | bytes 393224 | tf_op jit(solution)/shard_map/ppermute | solution.py:214
  20.2 8.8 %collective-permute-start.11 = (f32[2,2,64,128]{3,2,1,0:T(8,128)S(1)}, f32[2,2,64,128]{3,2,1,0:T(8,128)S(1)}, u32[]{:S(2)}, u32[]{:S(2)}) collective-permute-start(f32[2,2,64,128]{3,2,1,0:T(8,128)S(1)} %add.10), channel_id=1, source_target_pairs={{0,2},{1,3},{2,0},{3,1},{4,6},{5,7},{6,4},{7,5},{8,10},{9,11},{10,... | collective-permute-start | bytes 393224 | tf_op jit(solution)/shard_map/ppermute | solution.py:228
  21.0 9.1 %collective-permute-start.13 = (f32[2,2,64,128]{3,2,1,0:T(8,128)S(1)}, f32[2,2,64,128]{3,2,1,0:T(8,128)S(1)}, u32[]{:S(2)}, u32[]{:S(2)}) collective-permute-start(f32[2,2,64,128]{3,2,1,0:T(8,128)S(1)} %add.11), channel_id=1, source_target_pairs={{0,4},{1,5},{2,6},{3,7},{4,8},{5,9},{6,10},{7,11},{8,12},{9,13},{1... | collective-permute-start | bytes 393224 | tf_op jit(solution)/shard_map/ppermute | solution.py:228

commit v6 on v5

--- a/solution.py
+++ b/solution.py
@@ -55,16 +55,16 @@
 
 
 def transform(pairs, right_ref, left_ref, window):
-    halves = [times_right(jnp.concatenate(pair, axis=1), right_ref) for pair in pairs]
-    out = []
+    halves = []
     for at in range(0, len(pairs), PAIRED):
-        group = halves[at : at + PAIRED]
-        rows = [jnp.concatenate([half[:, c * window : (c + 1) * window] for half in group], axis=1) for c in range(2)]
+        group = pairs[at : at + PAIRED]
+        rows = [jnp.concatenate([pair[c] for pair in group], axis=1) for c in range(2)]
         whole = times_left(left_ref, jnp.concatenate(rows, axis=0))
         for n in range(len(group)):
             columns = slice(n * window, (n + 1) * window)
-            out.append((whole[:window, columns], whole[window:, columns]))
-    return out
+            halves.append(jnp.concatenate([whole[:window, columns], whole[window:, columns]], axis=1))
+    outs = [times_right(half, right_ref) for half in halves]
+    return [(out[:, :window], out[:, window:]) for out in outs]
 
 
 def travel_order(ring):
@@ -246,11 +246,12 @@
         compiler_params=PARAMS,
         cost_estimate=cost(1, 1),
     )(*(pltpu.with_memory_space_constraint(value, pltpu.HBM) for value in (probe, intensity, table)))
-    arrived = [tile] + [fetch(tile, *step) for step in steps[1:]]
-    early = [at for at, step in enumerate(steps) if at and not all(step)]
-    late = [at for at, step in enumerate(steps) if all(step)]
-    *values, probe_t = lax.optimization_barrier((*(arrived[at] for at in early), probe_t))
-    arrived = {0: tile, **dict(zip(early, values)), **{at: arrived[at] for at in late}}
+    early = [at for at, step in enumerate(steps) if all(step)]
+    late = [at for at, step in enumerate(steps) if at and not all(step)]
+    arrived = {at: fetch(tile, *steps[at]) for at in early + late}
+    values, probe_t = lax.optimization_barrier(([arrived[at] for at in early], probe_t))
+    arrived[0] = tile
+    arrived.update(zip(early, values))
     swapped = {at: swap(arrived[at]) for at in [0] + early}
     values = lax.optimization_barrier(([arrived[at] for at in late], [swapped[at] for at in early]))
     arrived.update(zip(late, values[0]))
@@ -267,7 +268,7 @@
         cost_estimate=cost(4 * dft_flops, 8 << 20),
     )(positions, probe_t, intensity_t, table, *gathered)
     keep, send = outputs[: len(steps)], outputs[len(steps) :]
-    order = late + early[::-1]
+    order = early + late
     other = {at: swap(send[at]) for at in order}
     own, other[order[0]] = lax.optimization_barrier((send[0], other[order[0]]))
     terms = [give(keep[at] + other[at], *steps[at]) for at in order]

time: 30.9 us -> 30.6 us (level)
  starting transfers between devices: 11.5 us -> 12.6 us
  waiting for transfers between devices: 13 us -> 11.9 us
    ppermute x3, waiting for transfers between devices: 3.7 us -> 2.95 us  [fetch(): lax.ppermute(value, ('region', 'probe'), [(b, a) for a, b in route(step,...]
    ppermute x8, starting transfers between devices: 1.27 us -> 1.98 us  [swap(): return lax.ppermute(value, 'probe', [(i, i ^ 1) for i in range(devices)])]
    ppermute x8, waiting for transfers between devices: 1.91 us -> 1.42 us  [swap(): return lax.ppermute(value, 'probe', [(i, i ^ 1) for i in range(devices)])]
    ppermute x3, starting transfers between devices: 3.29 us -> 3.65 us  [give(): return lax.ppermute(value, ('region', 'probe'), route(step, band))]
  transfers between devices with their start and end apart: 14 -> 14, of which waited for: 7 -> 8; matrix products, arithmetic and copies ran while one was open for 0% -> 0% of each run, Pallas kernels for 5% -> 5%
where the time goes in v6:
time: 30.6 us; the launch traced here: 30.5 us
  starting transfers between devices  12.6 us (41%)
  waiting for transfers between devices  11.9 us (39%)
  Pallas kernels  5.82 us (19%)
    ppermute x3, waiting for transfers between devices, give(): return lax.ppermute(value, ('region', 'probe'), route(step, band))  7.51 us
    ppermute x3, starting transfers between devices, fetch(): lax.ppermute(value, ('region', 'probe'), [(b, a) for a, b in route(step,...  6.96 us
    pallas_call x1, Pallas kernels, body(): pl.pallas_call(lambda *refs: main_kernel(ring, window, *refs), out_shape=...  3.72 us
    ppermute x3, starting transfers between devices, give(): return lax.ppermute(value, ('region', 'probe'), route(step, band))  3.65 us
    ppermute x3, waiting for transfers between devices, fetch(): lax.ppermute(value, ('region', 'probe'), [(b, a) for a, b in route(step,...  2.95 us
    ppermute x8, starting transfers between devices, swap(): return lax.ppermute(value, 'probe', [(i, i ^ 1) for i in range(devices)])  1.98 us
    ppermute x8, waiting for transfers between devices, swap(): return lax.ppermute(value, 'probe', [(i, i ^ 1) for i in range(devices)])  1.42 us
    pallas_call x1, Pallas kernels, body(): pl.pallas_call(prepare_kernel, out_shape=[jax.ShapeDtypeStruct(probe.shap...  1.41 us
  transfers between devices with their start and end apart: 14, of which 8 were waited for; matrix products, arithmetic and copies ran while one was open for 0% of the time, Pallas kernels for 5%

profile of v6, /device:TPU:0, one launch (start us, length us, event | category | flops | bytes accessed | tf_op | source)
XLA Modules:
  0.0 30.5 jit_solution(2445819797204685693)
XLA Ops:
  0.0 0.0 copy-start
  0.0 6.0 %collective-permute-start = (f32[2,2,64,128]{3,2,1,0:T(8,128)}, f32[2,2,64,128]{3,2,1,0:T(8,128)S(1)}, u32[]{:S(2)}, u32[]{:S(2)}) collective-permute-start(f32[2,2,64,128]{3,2,1,0:T(8,128)} %bitcast.2), channel_id=1, source_target_pairs={{6,0},{7,1},{4,2},{5,3},{10,4},{11,5},{8,6},{9,7},{14,8},{15,9},{1... | collective-permute-start | bytes 393224 | tf_op jit(solution)/shard_map/ppermute | solution.py:225
  6.0 0.5 %collective-permute-start.3 = (f32[2,2,64,128]{3,2,1,0:T(8,128)}, f32[2,2,64,128]{3,2,1,0:T(8,128)S(1)}, u32[]{:S(2)}, u32[]{:S(2)}) collective-permute-start(f32[2,2,64,128]{3,2,1,0:T(8,128)} %bitcast.3), channel_id=1, source_target_pairs={{2,0},{3,1},{0,2},{1,3},{6,4},{7,5},{4,6},{5,7},{10,8},{11,9},{8,1... | collective-permute-start | bytes 393224 | tf_op jit(solution)/shard_map/ppermute | solution.py:225
  6.5 0.4 %collective-permute-start.2 = (f32[2,2,64,128]{3,2,1,0:T(8,128)}, f32[2,2,64,128]{3,2,1,0:T(8,128)S(1)}, u32[]{:S(2)}, u32[]{:S(2)}) collective-permute-start(f32[2,2,64,128]{3,2,1,0:T(8,128)} %bitcast.4), channel_id=1, source_target_pairs={{4,0},{5,1},{6,2},{7,3},{8,4},{9,5},{10,6},{11,7},{12,8},{13,9},{1... | collective-permute-start | bytes 393224 | tf_op jit(solution)/shard_map/ppermute | solution.py:225
  7.0 1.4 %shard_map.55 = (f32[2,128,128]{2,1,0:T(8,128)S(1)}, f32[4,128,128]{2,1,0:T(8,128)S(1)}, bf16[4,2,256,256]{3,2,1,0:T(8,128)(2,1)S(1)}) custom-call(f32[2,128,128]{2,1,0:T(8,128)} %refs_0_.2, f32[1,4,128,128]{3,2,1,0:T(8,128)} %refs_1_.1, bf16[4,2,256,256]{3,2,1,0:T(8,128)(2,1)} %constant.2.clone.refs_2_), custom_call_target="tpu_custom_call" | custom-call | flops 1 | bytes 1 | tf_op jit(solution)/shard_map/pallas_call | solution.py:232
  8.4 0.0 copy-start.1
  8.4 1.8 %collective-permute-done.refs_10_ = f32[2,2,64,128]{3,2,1,0:T(8,128)S(1)} collective-permute-done((f32[2,2,64,128]{3,2,1,0:T(8,128)}, f32[2,2,64,128]{3,2,1,0:T(8,128)S(1)}, u32[]{:S(2)}, u32[]{:S(2)}) %collective-permute-start) | collective-permute-done | bytes 131104 | tf_op jit(solution)/shard_map/ppermute | solution.py:225
  10.2 0.0 collective-permute-start.4
  10.2 0.0 copy-done
  10.2 0.5 %collective-permute-start.1 = (f32[2,2,64,128]{3,2,1,0:T(8,128)S(1)}, f32[2,2,64,128]{3,2,1,0:T(8,128)S(1)}, u32[]{:S(2)}, u32[]{:S(2)}) collective-permute-start(f32[2,2,64,128]{3,2,1,0:T(8,128)S(1)} %bitcast.5), channel_id=1, source_target_pairs={{0,1},{1,0},{2,3},{3,2},{4,5},{5,4},{6,7},{7,6},{8,9},{9,8},{10,11... | collective-permute-start | bytes 393224 | tf_op jit(solution)/shard_map/ppermute | solution.py:214
  10.7 0.4 %collective-permute-done.3.refs_8_ = f32[2,2,64,128]{3,2,1,0:T(8,128)S(1)} collective-permute-done((f32[2,2,64,128]{3,2,1,0:T(8,128)}, f32[2,2,64,128]{3,2,1,0:T(8,128)S(1)}, u32[]{:S(2)}, u32[]{:S(2)}) %collective-permute-start.3) | collective-permute-done | bytes 131104 | tf_op jit(solution)/shard_map/ppermute | solution.py:225
  11.2 0.7 %collective-permute-done.2.refs_6_ = f32[2,2,64,128]{3,2,1,0:T(8,128)S(1)} collective-permute-done((f32[2,2,64,128]{3,2,1,0:T(8,128)}, f32[2,2,64,128]{3,2,1,0:T(8,128)S(1)}, u32[]{:S(2)}, u32[]{:S(2)}) %collective-permute-start.2) | collective-permute-done | bytes 131104 | tf_op jit(solution)/shard_map/ppermute | solution.py:225
  11.9 0.0 collective-permute-done.4.refs_11_
  11.9 0.0 collective-permute-start.5
  11.9 0.5 %collective-permute-start.6 = (f32[2,2,64,128]{3,2,1,0:T(8,128)S(1)}, f32[2,2,64,128]{3,2,1,0:T(8,128)S(1)}, u32[]{:S(2)}, u32[]{:S(2)}) collective-permute-start(f32[2,2,64,128]{3,2,1,0:T(8,128)S(1)} %collective-permute-done.3.refs_8_), channel_id=1, source_target_pairs={{0,1},{1,0},{2,3},{3,2},{4,5},{5,4},{6,7},{7,6},{8,9},{9,8},{10,11... | collective-permute-start | bytes 393224 | tf_op jit(solution)/shard_map/ppermute | solution.py:214
  12.4 0.0 copy-done.1
  12.4 0.1 copy.6.refs_0_
  12.5 0.0 collective-permute-done.1.refs_5_
  12.5 0.7 %collective-permute-done.5.refs_7_ = f32[2,2,64,128]{3,2,1,0:T(8,128)S(1)} collective-permute-done((f32[2,2,64,128]{3,2,1,0:T(8,128)S(1)}, f32[2,2,64,128]{3,2,1,0:T(8,128)S(1)}, u32[]{:S(2)}, u32[]{:S(2)}) %collective-permute-start.5) | collective-permute-done | bytes 131104 | tf_op jit(solution)/shard_map/ppermute | solution.py:214
  13.2 0.2 collective-permute-done.6.refs_9_
  13.4 3.7 %shard_map.56 = (f32[2,2,64,128]{3,2,1,0:T(8,128)S(1)}, f32[2,2,64,128]{3,2,1,0:T(8,128)S(1)}, f32[2,2,64,128]{3,2,1,0:T(8,128)S(1)}, f32[2,2,64,128]{3,2,1,0:T(...) custom-call(s32[1,4,2]{2,1,0:T(4,128)S(1)} %copy.6.refs_0_, ...), custom_call_target="tpu_custom_call" | custom-call | flops 1610612736 | bytes 8388608 | tf_op jit(solution)/shard_map/pallas_call | solution.py:261
  17.1 0.4 %collective-permute-start.7 = (f32[2,2,64,128]{3,2,1,0:T(8,128)S(1)}, f32[2,2,64,128]{3,2,1,0:T(8,128)S(1)}, u32[]{:S(2)}, u32[]{:S(2)}) collective-permute-start(f32[2,2,64,128]{3,2,1,0:T(8,128)S(1)} %get-tuple-element.33), channel_id=1, source_target_pairs={{0,1},{1,0},{2,3},{3,2},{4,5},{5,4},{6,7},{7,6},{8,9},{9,8},{10,11... | collective-permute-start | bytes 393224 | tf_op jit(solution)/shard_map/ppermute | solution.py:214
  17.6 0.2 collective-permute-start.10
  17.7 0.4 %collective-permute-start.12 = (f32[2,2,64,128]{3,2,1,0:T(8,128)S(1)}, f32[2,2,64,128]{3,2,1,0:T(8,128)S(1)}, u32[]{:S(2)}, u32[]{:S(2)}) collective-permute-start(f32[2,2,64,128]{3,2,1,0:T(8,128)S(1)} %get-tuple-element.40), channel_id=1, source_target_pairs={{0,1},{1,0},{2,3},{3,2},{4,5},{5,4},{6,7},{7,6},{8,9},{9,8},{10,11... | collective-permute-start | bytes 393224 | tf_op jit(solution)/shard_map/ppermute | solution.py:214
  18.1 0.5 %collective-permute-done.7 = f32[2,2,64,128]{3,2,1,0:T(8,128)S(1)} collective-permute-done((f32[2,2,64,128]{3,2,1,0:T(8,128)S(1)}, f32[2,2,64,128]{3,2,1,0:T(8,128)S(1)}, u32[]{:S(2)}, u32[]{:S(2)}) %collective-permute-start.7) | collective-permute-done | bytes 131104 | tf_op jit(solution)/shard_map/ppermute | solution.py:214
  18.6 1.0 %collective-permute-start.9 = (f32[2,2,64,128]{3,2,1,0:T(8,128)S(1)}, f32[2,2,64,128]{3,2,1,0:T(8,128)S(1)}, u32[]{:S(2)}, u32[]{:S(2)}) collective-permute-start(f32[2,2,64,128]{3,2,1,0:T(8,128)S(1)} %add.9), channel_id=1, source_target_pairs={{0,6},{1,7},{2,4},{3,5},{4,10},{5,11},{6,8},{7,9},{8,14},{9,15},{1... | collective-permute-start | bytes 393224 | tf_op jit(solution)/shard_map/ppermute | solution.py:228
  19.6 0.0 collective-permute-start.8
  19.6 0.0 collective-permute-done.10
  19.6 1.6 %collective-permute-start.11 = (f32[2,2,64,128]{3,2,1,0:T(8,128)S(1)}, f32[2,2,64,128]{3,2,1,0:T(8,128)S(1)}, u32[]{:S(2)}, u32[]{:S(2)}) collective-permute-start(f32[2,2,64,128]{3,2,1,0:T(8,128)S(1)} %add.10), channel_id=1, source_target_pairs={{0,4},{1,5},{2,6},{3,7},{4,8},{5,9},{6,10},{7,11},{8,12},{9,13},{1... | collective-permute-start | bytes 393224 | tf_op jit(solution)/shard_map/ppermute | solution.py:228
  21.3 0.0 collective-permute-done.12
  21.3 1.0 %collective-permute-start.13 = (f32[2,2,64,128]{3,2,1,0:T(8,128)S(1)}, f32[2,2,64,128]{3,2,1,0:T(8,128)S(1)}, u32[]{:S(2)}, u32[]{:S(2)}) collective-permute-start(f32[2,2,64,128]{3,2,1,0:T(8,128)S(1)} %add.11), channel_id=1, source_target_pairs={{0,2},{1,3},{2,0},{3,1},{4,6},{5,7},{6,4},{7,5},{8,10},{9,11},{10,... | collective-permute-start | bytes 393224 | tf_op jit(solution)/shard_map/ppermute | solution.py:228
  22.3 5.5 %collective-permute-done.9.refs_2_ = f32[2,2,64,128]{3,2,1,0:T(8,128)S(1)} collective-permute-done((f32[2,2,64,128]{3,2,1,0:T(8,128)S(1)}, f32[2,2,64,128]{3,2,1,0:T(8,128)S(1)}, u32[]{:S(2)}, u32[]{:S(2)}) %collective-permute-start.9) | collective-permute-done | bytes 131104 | tf_op jit(solution)/shard_map/ppermute | solution.py:228
  27.8 0.0 collective-permute-done.8.refs_1_
  27.8 2.0 %collective-permute-done.11.refs_3_ = f32[2,2,64,128]{3,2,1,0:T(8,128)S(1)} collective-permute-done((f32[2,2,64,128]{3,2,1,0:T(8,128)S(1)}, f32[2,2,64,128]{3,2,1,0:T(8,128)S(1)}, u32[]{:S(2)}, u32[]{:S(2)}) %collective-permute-start.11) | collective-permute-done | bytes 131104 | tf_op jit(solution)/shard_map/ppermute | solution.py:228
  29.8 0.0 collective-permute-done.13.refs_4_
  29.8 0.7 %shard_map.57 = f32[2,2,64,128]{3,2,1,0:T(8,128)} custom-call(f32[2,2,64,128]{3,2,1,0:T(8,128)S(1)} %get-tuple-element.31.refs_0_, f32[2,2,64,128]{3,2,1,0:T(8,128)S(1)} %collective-permute-done.8.refs_1_, f32[2,2,64,128]{3,2,1,0:T(8,128)S(1)} %collective-permute-done.9.refs_2_, f32[2,2,64,128]{3,2,1,0:T(8,128)S(1)} %collective-permute-done.11.refs_3_, ...), custom_call_target="tpu_custom_call" | custom-call | tf_op jit(solution)/shard_map/pallas_call | solution.py:276
  (3 shorter events, 0.0 us)
Async XLA Ops:
  0.0 10.2 %copy-start = (f32[2,2,128,64]{2,3,1,0:T(8,128)S(1)}, f32[2,2,128,64]{2,3,1,0:T(8,128)}, u32[]{:S(2)}) copy-start(f32[2,2,128,64]{2,3,1,0:T(8,128)} %param.5) | copy-start | bytes 393220
  0.0 10.2 %collective-permute-start = (f32[2,2,64,128]{3,2,1,0:T(8,128)}, f32[2,2,64,128]{3,2,1,0:T(8,128)S(1)}, u32[]{:S(2)}, u32[]{:S(2)}) collective-permute-start(f32[2,2,64,128]{3,2,1,0:T(8,128)} %bitcast.2), channel_id=1, source_target_pairs={{6,0},{7,1},{4,2},{5,3},{10,4},{11,5},{8,6},{9,7},{14,8},{15,9},{1... | collective-permute-start | bytes 393224 | tf_op jit(solution)/shard_map/ppermute | solution.py:225
  6.0 5.2 %collective-permute-start.3 = (f32[2,2,64,128]{3,2,1,0:T(8,128)}, f32[2,2,64,128]{3,2,1,0:T(8,128)S(1)}, u32[]{:S(2)}, u32[]{:S(2)}) collective-permute-start(f32[2,2,64,128]{3,2,1,0:T(8,128)} %bitcast.3), channel_id=1, source_target_pairs={{2,0},{3,1},{0,2},{1,3},{6,4},{7,5},{4,6},{5,7},{10,8},{11,9},{8,1... | collective-permute-start | bytes 393224 | tf_op jit(solution)/shard_map/ppermute | solution.py:225
  6.5 5.3 %collective-permute-start.2 = (f32[2,2,64,128]{3,2,1,0:T(8,128)}, f32[2,2,64,128]{3,2,1,0:T(8,128)S(1)}, u32[]{:S(2)}, u32[]{:S(2)}) collective-permute-start(f32[2,2,64,128]{3,2,1,0:T(8,128)} %bitcast.4), channel_id=1, source_target_pairs={{4,0},{5,1},{6,2},{7,3},{8,4},{9,5},{10,6},{11,7},{12,8},{13,9},{1... | collective-permute-start | bytes 393224 | tf_op jit(solution)/shard_map/ppermute | solution.py:225
  8.4 4.0 %copy-start.1 = (s32[1,4,2]{1,2,0:T(2,128)S(1)}, s32[1,4,2]{1,2,0:T(2,128)}, u32[]{:S(2)}) copy-start(s32[1,4,2]{1,2,0:T(2,128)} %param.8) | copy-start | bytes 100
  10.2 1.7 %collective-permute-start.4 = (f32[2,2,64,128]{3,2,1,0:T(8,128)S(1)}, f32[2,2,64,128]{3,2,1,0:T(8,128)S(1)}, u32[]{:S(2)}, u32[]{:S(2)}) collective-permute-start(f32[2,2,64,128]{3,2,1,0:T(8,128)S(1)} %collective-permute-done.refs_10_), channel_id=1, source_target_pairs={{0,1},{1,0},{2,3},{3,2},{4,5},{5,4},{6,7},{7,6},{8,9},{9,8},{10,11... | collective-permute-start | bytes 393224 | tf_op jit(solution)/shard_map/ppermute | solution.py:214
  10.2 2.3 %collective-permute-start.1 = (f32[2,2,64,128]{3,2,1,0:T(8,128)S(1)}, f32[2,2,64,128]{3,2,1,0:T(8,128)S(1)}, u32[]{:S(2)}, u32[]{:S(2)}) collective-permute-start(f32[2,2,64,128]{3,2,1,0:T(8,128)S(1)} %bitcast.5), channel_id=1, source_target_pairs={{0,1},{1,0},{2,3},{3,2},{4,5},{5,4},{6,7},{7,6},{8,9},{9,8},{10,11... | collective-permute-start | bytes 393224 | tf_op jit(solution)/shard_map/ppermute | solution.py:214
  11.9 1.3 %collective-permute-start.5 = (f32[2,2,64,128]{3,2,1,0:T(8,128)S(1)}, f32[2,2,64,128]{3,2,1,0:T(8,128)S(1)}, u32[]{:S(2)}, u32[]{:S(2)}) collective-permute-start(f32[2,2,64,128]{3,2,1,0:T(8,128)S(1)} %collective-permute-done.2.refs_6_), channel_id=1, source_target_pairs={{0,1},{1,0},{2,3},{3,2},{4,5},{5,4},{6,7},{7,6},{8,9},{9,8},{10,11... | collective-permute-start | bytes 393224 | tf_op jit(solution)/shard_map/ppermute | solution.py:214
  11.9 1.5 %collective-permute-start.6 = (f32[2,2,64,128]{3,2,1,0:T(8,128)S(1)}, f32[2,2,64,128]{3,2,1,0:T(8,128)S(1)}, u32[]{:S(2)}, u32[]{:S(2)}) collective-permute-start(f32[2,2,64,128]{3,2,1,0:T(8,128)S(1)} %collective-permute-done.3.refs_8_), channel_id=1, source_target_pairs={{0,1},{1,0},{2,3},{3,2},{4,5},{5,4},{6,7},{7,6},{8,9},{9,8},{10,11... | collective-permute-start | bytes 393224 | tf_op jit(solution)/shard_map/ppermute | solution.py:214
  17.1 1.4 %collective-permute-start.7 = (f32[2,2,64,128]{3,2,1,0:T(8,128)S(1)}, f32[2,2,64,128]{3,2,1,0:T(8,128)S(1)}, u32[]{:S(2)}, u32[]{:S(2)}) collective-permute-start(f32[2,2,64,128]{3,2,1,0:T(8,128)S(1)} %get-tuple-element.33), channel_id=1, source_target_pairs={{0,1},{1,0},{2,3},{3,2},{4,5},{5,4},{6,7},{7,6},{8,9},{9,8},{10,11... | collective-permute-start | bytes 393224 | tf_op jit(solution)/shard_map/ppermute | solution.py:214
  17.6 2.1 %collective-permute-start.10 = (f32[2,2,64,128]{3,2,1,0:T(8,128)S(1)}, f32[2,2,64,128]{3,2,1,0:T(8,128)S(1)}, u32[]{:S(2)}, u32[]{:S(2)}) collective-permute-start(f32[2,2,64,128]{3,2,1,0:T(8,128)S(1)} %get-tuple-element.38), channel_id=1, source_target_pairs={{0,1},{1,0},{2,3},{3,2},{4,5},{5,4},{6,7},{7,6},{8,9},{9,8},{10,11... | collective-permute-start | bytes 393224 | tf_op jit(solution)/shard_map/ppermute | solution.py:214
  17.7 3.6 %collective-permute-start.12 = (f32[2,2,64,128]{3,2,1,0:T(8,128)S(1)}, f32[2,2,64,128]{3,2,1,0:T(8,128)S(1)}, u32[]{:S(2)}, u32[]{:S(2)}) collective-permute-start(f32[2,2,64,128]{3,2,1,0:T(8,128)S(1)} %get-tuple-element.40), channel_id=1, source_target_pairs={{0,1},{1,0},{2,3},{3,2},{4,5},{5,4},{6,7},{7,6},{8,9},{9,8},{10,11... | collective-permute-start | bytes 393224 | tf_op jit(solution)/shard_map/ppermute | solution.py:214
  18.6 9.2 %collective-permute-start.9 = (f32[2,2,64,128]{3,2,1,0:T(8,128)S(1)}, f32[2,2,64,128]{3,2,1,0:T(8,128)S(1)}, u32[]{:S(2)}, u32[]{:S(2)}) collective-permute-start(f32[2,2,64,128]{3,2,1,0:T(8,128)S(1)} %add.9), channel_id=1, source_target_pairs={{0,6},{1,7},{2,4},{3,5},{4,10},{5,11},{6,8},{7,9},{8,14},{9,15},{1... | collective-permute-start | bytes 393224 | tf_op jit(solution)/shard_map/ppermute | solution.py:228
  19.6 8.2 %collective-permute-start.8 = (f32[2,2,64,128]{3,2,1,0:T(8,128)S(1)}, f32[2,2,64,128]{3,2,1,0:T(8,128)S(1)}, u32[]{:S(2)}, u32[]{:S(2)}) collective-permute-start(f32[2,2,64,128]{3,2,1,0:T(8,128)S(1)} %get-tuple-element.34), channel_id=1, source_target_pairs={{0,1},{1,0},{2,3},{3,2},{4,5},{5,4},{6,7},{7,6},{8,9},{9,8},{10,11... | collective-permute-start | bytes 393224 | tf_op jit(solution)/shard_map/ppermute | solution.py:214
  19.6 10.2 %collective-permute-start.11 = (f32[2,2,64,128]{3,2,1,0:T(8,128)S(1)}, f32[2,2,64,128]{3,2,1,0:T(8,128)S(1)}, u32[]{:S(2)}, u32[]{:S(2)}) collective-permute-start(f32[2,2,64,128]{3,2,1,0:T(8,128)S(1)} %add.10), channel_id=1, source_target_pairs={{0,4},{1,5},{2,6},{3,7},{4,8},{5,9},{6,10},{7,11},{8,12},{9,13},{1... | collective-permute-start | bytes 393224 | tf_op jit(solution)/shard_map/ppermute | solution.py:228
  21.3 8.5 %collective-permute-start.13 = (f32[2,2,64,128]{3,2,1,0:T(8,128)S(1)}, f32[2,2,64,128]{3,2,1,0:T(8,128)S(1)}, u32[]{:S(2)}, u32[]{:S(2)}) collective-permute-start(f32[2,2,64,128]{3,2,1,0:T(8,128)S(1)} %add.11), channel_id=1, source_target_pairs={{0,2},{1,3},{2,0},{3,1},{4,6},{5,7},{6,4},{7,5},{8,10},{9,11},{10,... | collective-permute-start | bytes 393224 | tf_op jit(solution)/shard_map/ppermute | solution.py:228

commit v7 on v6

--- a/solution.py
+++ b/solution.py
@@ -143,7 +143,8 @@
 def main_kernel(ring, window, position_ref, probe_ref, intensity_ref, table_ref, *rest):
     direct_ref, inverse_ref, forth_ref, back_ref = (table_ref.at[i] for i in range(4))
     unit_refs, rest = rest[: 4 * ring], rest[4 * ring :]
-    keep_refs, send_refs, (field_ref, wave_ref, total_ref, first_total_ref) = rest[: 2 * ring], rest[2 * ring : -4], rest[-4:]
+    keep_refs, send_refs, scratch = rest[: 2 * ring], rest[2 * ring : -5], rest[-5:]
+    field_ref, wave_ref, patch_ref, total_ref, first_total_ref = scratch
     count = position_ref.shape[1]
     assemble(unit_refs, field_ref, ring, window)
     total_ref[...] = jnp.zeros_like(total_ref)
@@ -153,10 +154,12 @@
     for n in range(count):
         re, im = cut(field_ref, 0, position_ref, n, window)
         exits.append((probe_re * re - probe_im * im, probe_re * im + probe_im * re))
+    for n in range(count):
+        patch_ref[n, 0], patch_ref[n, 1] = cut(field_ref, 1, position_ref, n, window)
     waves = transform(exits, forth_ref, back_ref, window)
     exits = []
     for n in range(count):
-        re, im = cut(field_ref, 1, position_ref, n, window)
+        re, im = patch_ref[n, 0], patch_ref[n, 1]
         w_re, w_im = waves[n]
         wave_ref[n, 0] = w_re
         wave_ref[n, 1] = w_im
@@ -168,7 +171,7 @@
     carried, gradients = [], []
     for n, (b_re, b_im) in enumerate(transform(scaled, inverse_ref, direct_ref, window)):
         w_re, w_im = wave_ref[n, 0], wave_ref[n, 1]
-        p_re, p_im = cut(field_ref, 1, position_ref, n, window)
+        p_re, p_im = patch_ref[n, 0], patch_ref[n, 1]
         carried.append((p_re * b_re + p_im * b_im, p_re * b_im - p_im * b_re))
         deposit(total_ref, position_ref, n, (w_re * b_re + w_im * b_im, w_re * b_im - w_im * b_re), window)
     hand_out(total_ref, 1, keep_refs, send_refs, ring, window)
@@ -263,12 +266,12 @@
         out_shape=[unit] * (2 * len(steps)),
         in_specs=[SMEM] + [VMEM] * (3 + 4 * ring),
         out_specs=[VMEM] * (2 * len(steps)),
-        scratch_shapes=[field, wave_scratch, total, total],
+        scratch_shapes=[field, wave_scratch, wave_scratch, total, total],
         compiler_params=PARAMS,
         cost_estimate=cost(4 * dft_flops, 8 << 20),
     )(positions, probe_t, intensity_t, table, *gathered)
     keep, send = outputs[: len(steps)], outputs[len(steps) :]
-    order = early + late
+    order = early + late[::-1]
     other = {at: swap(send[at]) for at in order}
     own, other[order[0]] = lax.optimization_barrier((send[0], other[order[0]]))
     terms = [give(keep[at] + other[at], *steps[at]) for at in order]

time: 30.6 us -> 30.6 us (level)
  transfers between devices with their start and end apart: 14 -> 14, of which waited for: 8 -> 9; matrix products, arithmetic and copies ran while one was open for 0% -> 0% of each run, Pallas kernels for 5% -> 5%
where the time goes in v7:
time: 30.6 us; the launch traced here: 30.4 us
  starting transfers between devices  12.6 us (41%)
  waiting for transfers between devices  11.9 us (39%)
  Pallas kernels  5.78 us (19%)
    ppermute x3, waiting for transfers between devices, give(): return lax.ppermute(value, ('region', 'probe'), route(step, band))  7.48 us
    ppermute x3, starting transfers between devices, fetch(): lax.ppermute(value, ('region', 'probe'), [(b, a) for a, b in route(step,...  6.96 us
    pallas_call x1, Pallas kernels, body(): pl.pallas_call(lambda *refs: main_kernel(ring, window, *refs), out_shape=...  3.69 us
    ppermute x3, starting transfers between devices, give(): return lax.ppermute(value, ('region', 'probe'), route(step, band))  3.62 us
    ppermute x3, waiting for transfers between devices, fetch(): lax.ppermute(value, ('region', 'probe'), [(b, a) for a, b in route(step,...  2.95 us
    ppermute x8, starting transfers between devices, swap(): return lax.ppermute(value, 'probe', [(i, i ^ 1) for i in range(devices)])  2.01 us
    ppermute x8, waiting for transfers between devices, swap(): return lax.ppermute(value, 'probe', [(i, i ^ 1) for i in range(devices)])  1.42 us
    pallas_call x1, Pallas kernels, body(): pl.pallas_call(prepare_kernel, out_shape=[jax.ShapeDtypeStruct(probe.shap...  1.41 us
  transfers between devices with their start and end apart: 14, of which 9 were waited for; matrix products, arithmetic and copies ran while one was open for 0% of the time, Pallas kernels for 5%

profile of v7, /device:TPU:0, one launch (start us, length us, event | category | flops | bytes accessed | tf_op | source)
XLA Modules:
  0.0 30.4 jit_solution(4406835230999679956)
XLA Ops:
  0.0 0.0 copy-start
  0.0 6.0 %collective-permute-start = (f32[2,2,64,128]{3,2,1,0:T(8,128)}, f32[2,2,64,128]{3,2,1,0:T(8,128)S(1)}, u32[]{:S(2)}, u32[]{:S(2)}) collective-permute-start(f32[2,2,64,128]{3,2,1,0:T(8,128)} %bitcast.2), channel_id=1, source_target_pairs={{6,0},{7,1},{4,2},{5,3},{10,4},{11,5},{8,6},{9,7},{14,8},{15,9},{1... | collective-permute-start | bytes 393224 | tf_op jit(solution)/shard_map/ppermute | solution.py:228
  6.0 0.5 %collective-permute-start.3 = (f32[2,2,64,128]{3,2,1,0:T(8,128)}, f32[2,2,64,128]{3,2,1,0:T(8,128)S(1)}, u32[]{:S(2)}, u32[]{:S(2)}) collective-permute-start(f32[2,2,64,128]{3,2,1,0:T(8,128)} %bitcast.3), channel_id=1, source_target_pairs={{2,0},{3,1},{0,2},{1,3},{6,4},{7,5},{4,6},{5,7},{10,8},{11,9},{8,1... | collective-permute-start | bytes 393224 | tf_op jit(solution)/shard_map/ppermute | solution.py:228
  6.5 0.4 %collective-permute-start.2 = (f32[2,2,64,128]{3,2,1,0:T(8,128)}, f32[2,2,64,128]{3,2,1,0:T(8,128)S(1)}, u32[]{:S(2)}, u32[]{:S(2)}) collective-permute-start(f32[2,2,64,128]{3,2,1,0:T(8,128)} %bitcast.4), channel_id=1, source_target_pairs={{4,0},{5,1},{6,2},{7,3},{8,4},{9,5},{10,6},{11,7},{12,8},{13,9},{1... | collective-permute-start | bytes 393224 | tf_op jit(solution)/shard_map/ppermute | solution.py:228
  7.0 1.4 %shard_map.55 = (f32[2,128,128]{2,1,0:T(8,128)S(1)}, f32[4,128,128]{2,1,0:T(8,128)S(1)}, bf16[4,2,256,256]{3,2,1,0:T(8,128)(2,1)S(1)}) custom-call(f32[2,128,128]{2,1,0:T(8,128)} %refs_0_.2, f32[1,4,128,128]{3,2,1,0:T(8,128)} %refs_1_.1, bf16[4,2,256,256]{3,2,1,0:T(8,128)(2,1)} %constant.2.clone.refs_2_), custom_call_target="tpu_custom_call" | custom-call | flops 1 | bytes 1 | tf_op jit(solution)/shard_map/pallas_call | solution.py:235
  8.4 0.0 copy-start.1
  8.4 1.8 %collective-permute-done.refs_10_ = f32[2,2,64,128]{3,2,1,0:T(8,128)S(1)} collective-permute-done((f32[2,2,64,128]{3,2,1,0:T(8,128)}, f32[2,2,64,128]{3,2,1,0:T(8,128)S(1)}, u32[]{:S(2)}, u32[]{:S(2)}) %collective-permute-start) | collective-permute-done | bytes 131104 | tf_op jit(solution)/shard_map/ppermute | solution.py:228
  10.2 0.0 collective-permute-start.4
  10.2 0.0 copy-done
  10.2 0.5 %collective-permute-start.1 = (f32[2,2,64,128]{3,2,1,0:T(8,128)S(1)}, f32[2,2,64,128]{3,2,1,0:T(8,128)S(1)}, u32[]{:S(2)}, u32[]{:S(2)}) collective-permute-start(f32[2,2,64,128]{3,2,1,0:T(8,128)S(1)} %bitcast.5), channel_id=1, source_target_pairs={{0,1},{1,0},{2,3},{3,2},{4,5},{5,4},{6,7},{7,6},{8,9},{9,8},{10,11... | collective-permute-start | bytes 393224 | tf_op jit(solution)/shard_map/ppermute | solution.py:217
  10.7 0.4 %collective-permute-done.3.refs_8_ = f32[2,2,64,128]{3,2,1,0:T(8,128)S(1)} collective-permute-done((f32[2,2,64,128]{3,2,1,0:T(8,128)}, f32[2,2,64,128]{3,2,1,0:T(8,128)S(1)}, u32[]{:S(2)}, u32[]{:S(2)}) %collective-permute-start.3) | collective-permute-done | bytes 131104 | tf_op jit(solution)/shard_map/ppermute | solution.py:228
  11.2 0.7 %collective-permute-done.2.refs_6_ = f32[2,2,64,128]{3,2,1,0:T(8,128)S(1)} collective-permute-done((f32[2,2,64,128]{3,2,1,0:T(8,128)}, f32[2,2,64,128]{3,2,1,0:T(8,128)S(1)}, u32[]{:S(2)}, u32[]{:S(2)}) %collective-permute-start.2) | collective-permute-done | bytes 131104 | tf_op jit(solution)/shard_map/ppermute | solution.py:228
  11.9 0.0 collective-permute-done.4.refs_11_
  11.9 0.0 collective-permute-start.5
  11.9 0.5 %collective-permute-start.6 = (f32[2,2,64,128]{3,2,1,0:T(8,128)S(1)}, f32[2,2,64,128]{3,2,1,0:T(8,128)S(1)}, u32[]{:S(2)}, u32[]{:S(2)}) collective-permute-start(f32[2,2,64,128]{3,2,1,0:T(8,128)S(1)} %collective-permute-done.3.refs_8_), channel_id=1, source_target_pairs={{0,1},{1,0},{2,3},{3,2},{4,5},{5,4},{6,7},{7,6},{8,9},{9,8},{10,11... | collective-permute-start | bytes 393224 | tf_op jit(solution)/shard_map/ppermute | solution.py:217
  12.4 0.0 copy-done.1
  12.4 0.1 copy.6.refs_0_
  12.5 0.0 collective-permute-done.1.refs_5_
  12.5 0.7 %collective-permute-done.5.refs_7_ = f32[2,2,64,128]{3,2,1,0:T(8,128)S(1)} collective-permute-done((f32[2,2,64,128]{3,2,1,0:T(8,128)S(1)}, f32[2,2,64,128]{3,2,1,0:T(8,128)S(1)}, u32[]{:S(2)}, u32[]{:S(2)}) %collective-permute-start.5) | collective-permute-done | bytes 131104 | tf_op jit(solution)/shard_map/ppermute | solution.py:217
  13.2 0.2 collective-permute-done.6.refs_9_
  13.4 3.7 %shard_map.56 = (f32[2,2,64,128]{3,2,1,0:T(8,128)S(1)}, f32[2,2,64,128]{3,2,1,0:T(8,128)S(1)}, f32[2,2,64,128]{3,2,1,0:T(8,128)S(1)}, f32[2,2,64,128]{3,2,1,0:T(...) custom-call(s32[1,4,2]{2,1,0:T(4,128)S(1)} %copy.6.refs_0_, ...), custom_call_target="tpu_custom_call" | custom-call | flops 1610612736 | bytes 8388608 | tf_op jit(solution)/shard_map/pallas_call | solution.py:264
  17.1 0.4 %collective-permute-start.7 = (f32[2,2,64,128]{3,2,1,0:T(8,128)S(1)}, f32[2,2,64,128]{3,2,1,0:T(8,128)S(1)}, u32[]{:S(2)}, u32[]{:S(2)}) collective-permute-start(f32[2,2,64,128]{3,2,1,0:T(8,128)S(1)} %get-tuple-element.33), channel_id=1, source_target_pairs={{0,1},{1,0},{2,3},{3,2},{4,5},{5,4},{6,7},{7,6},{8,9},{9,8},{10,11... | collective-permute-start | bytes 393224 | tf_op jit(solution)/shard_map/ppermute | solution.py:217
  17.5 0.2 collective-permute-start.10
  17.7 0.4 %collective-permute-start.12 = (f32[2,2,64,128]{3,2,1,0:T(8,128)S(1)}, f32[2,2,64,128]{3,2,1,0:T(8,128)S(1)}, u32[]{:S(2)}, u32[]{:S(2)}) collective-permute-start(f32[2,2,64,128]{3,2,1,0:T(8,128)S(1)} %get-tuple-element.40), channel_id=1, source_target_pairs={{0,1},{1,0},{2,3},{3,2},{4,5},{5,4},{6,7},{7,6},{8,9},{9,8},{10,11... | collective-permute-start | bytes 393224 | tf_op jit(solution)/shard_map/ppermute | solution.py:217
  18.0 0.5 %collective-permute-done.7 = f32[2,2,64,128]{3,2,1,0:T(8,128)S(1)} collective-permute-done((f32[2,2,64,128]{3,2,1,0:T(8,128)S(1)}, f32[2,2,64,128]{3,2,1,0:T(8,128)S(1)}, u32[]{:S(2)}, u32[]{:S(2)}) %collective-permute-start.7) | collective-permute-done | bytes 131104 | tf_op jit(solution)/shard_map/ppermute | solution.py:217
  18.5 1.0 %collective-permute-start.9 = (f32[2,2,64,128]{3,2,1,0:T(8,128)S(1)}, f32[2,2,64,128]{3,2,1,0:T(8,128)S(1)}, u32[]{:S(2)}, u32[]{:S(2)}) collective-permute-start(f32[2,2,64,128]{3,2,1,0:T(8,128)S(1)} %add.9), channel_id=1, source_target_pairs={{0,6},{1,7},{2,4},{3,5},{4,10},{5,11},{6,8},{7,9},{8,14},{9,15},{1... | collective-permute-start | bytes 393224 | tf_op jit(solution)/shard_map/ppermute | solution.py:231
  19.5 0.1 collective-permute-start.8
  19.6 0.0 collective-permute-done.10
  19.6 1.0 %collective-permute-start.11 = (f32[2,2,64,128]{3,2,1,0:T(8,128)S(1)}, f32[2,2,64,128]{3,2,1,0:T(8,128)S(1)}, u32[]{:S(2)}, u32[]{:S(2)}) collective-permute-start(f32[2,2,64,128]{3,2,1,0:T(8,128)S(1)} %add.10), channel_id=1, source_target_pairs={{0,2},{1,3},{2,0},{3,1},{4,6},{5,7},{6,4},{7,5},{8,10},{9,11},{10,... | collective-permute-start | bytes 393224 | tf_op jit(solution)/shard_map/ppermute | solution.py:231
  20.6 0.0 collective-permute-done.12
  20.6 1.6 %collective-permute-start.13 = (f32[2,2,64,128]{3,2,1,0:T(8,128)S(1)}, f32[2,2,64,128]{3,2,1,0:T(8,128)S(1)}, u32[]{:S(2)}, u32[]{:S(2)}) collective-permute-start(f32[2,2,64,128]{3,2,1,0:T(8,128)S(1)} %add.11), channel_id=1, source_target_pairs={{0,4},{1,5},{2,6},{3,7},{4,8},{5,9},{6,10},{7,11},{8,12},{9,13},{1... | collective-permute-start | bytes 393224 | tf_op jit(solution)/shard_map/ppermute | solution.py:231
  22.3 5.5 %collective-permute-done.9.refs_2_ = f32[2,2,64,128]{3,2,1,0:T(8,128)S(1)} collective-permute-done((f32[2,2,64,128]{3,2,1,0:T(8,128)S(1)}, f32[2,2,64,128]{3,2,1,0:T(8,128)S(1)}, u32[]{:S(2)}, u32[]{:S(2)}) %collective-permute-start.9) | collective-permute-done | bytes 131104 | tf_op jit(solution)/shard_map/ppermute | solution.py:231
  27.7 0.0 collective-permute-done.8.refs_1_
  27.7 0.6 %collective-permute-done.11.refs_3_ = f32[2,2,64,128]{3,2,1,0:T(8,128)S(1)} collective-permute-done((f32[2,2,64,128]{3,2,1,0:T(8,128)S(1)}, f32[2,2,64,128]{3,2,1,0:T(8,128)S(1)}, u32[]{:S(2)}, u32[]{:S(2)}) %collective-permute-start.11) | collective-permute-done | bytes 131104 | tf_op jit(solution)/shard_map/ppermute | solution.py:231
  28.4 1.4 %collective-permute-done.13.refs_4_ = f32[2,2,64,128]{3,2,1,0:T(8,128)S(1)} collective-permute-done((f32[2,2,64,128]{3,2,1,0:T(8,128)S(1)}, f32[2,2,64,128]{3,2,1,0:T(8,128)S(1)}, u32[]{:S(2)}, u32[]{:S(2)}) %collective-permute-start.13) | collective-permute-done | bytes 131104 | tf_op jit(solution)/shard_map/ppermute | solution.py:231
  29.7 0.7 %shard_map.57 = f32[2,2,64,128]{3,2,1,0:T(8,128)} custom-call(f32[2,2,64,128]{3,2,1,0:T(8,128)S(1)} %get-tuple-element.31.refs_0_, f32[2,2,64,128]{3,2,1,0:T(8,128)S(1)} %collective-permute-done.8.refs_1_, f32[2,2,64,128]{3,2,1,0:T(8,128)S(1)} %collective-permute-done.9.refs_2_, f32[2,2,64,128]{3,2,1,0:T(8,128)S(1)} %collective-permute-done.11.refs_3_, ...), custom_call_target="tpu_custom_call" | custom-call | tf_op jit(solution)/shard_map/pallas_call | solution.py:279
  (3 shorter events, 0.0 us)
Async XLA Ops:
  0.0 10.2 %copy-start = (f32[2,2,128,64]{2,3,1,0:T(8,128)S(1)}, f32[2,2,128,64]{2,3,1,0:T(8,128)}, u32[]{:S(2)}) copy-start(f32[2,2,128,64]{2,3,1,0:T(8,128)} %param.5) | copy-start | bytes 393220
  0.0 10.2 %collective-permute-start = (f32[2,2,64,128]{3,2,1,0:T(8,128)}, f32[2,2,64,128]{3,2,1,0:T(8,128)S(1)}, u32[]{:S(2)}, u32[]{:S(2)}) collective-permute-start(f32[2,2,64,128]{3,2,1,0:T(8,128)} %bitcast.2), channel_id=1, source_target_pairs={{6,0},{7,1},{4,2},{5,3},{10,4},{11,5},{8,6},{9,7},{14,8},{15,9},{1... | collective-permute-start | bytes 393224 | tf_op jit(solution)/shard_map/ppermute | solution.py:228
  6.0 5.2 %collective-permute-start.3 = (f32[2,2,64,128]{3,2,1,0:T(8,128)}, f32[2,2,64,128]{3,2,1,0:T(8,128)S(1)}, u32[]{:S(2)}, u32[]{:S(2)}) collective-permute-start(f32[2,2,64,128]{3,2,1,0:T(8,128)} %bitcast.3), channel_id=1, source_target_pairs={{2,0},{3,1},{0,2},{1,3},{6,4},{7,5},{4,6},{5,7},{10,8},{11,9},{8,1... | collective-permute-start | bytes 393224 | tf_op jit(solution)/shard_map/ppermute | solution.py:228
  6.5 5.3 %collective-permute-start.2 = (f32[2,2,64,128]{3,2,1,0:T(8,128)}, f32[2,2,64,128]{3,2,1,0:T(8,128)S(1)}, u32[]{:S(2)}, u32[]{:S(2)}) collective-permute-start(f32[2,2,64,128]{3,2,1,0:T(8,128)} %bitcast.4), channel_id=1, source_target_pairs={{4,0},{5,1},{6,2},{7,3},{8,4},{9,5},{10,6},{11,7},{12,8},{13,9},{1... | collective-permute-start | bytes 393224 | tf_op jit(solution)/shard_map/ppermute | solution.py:228
  8.4 4.0 %copy-start.1 = (s32[1,4,2]{1,2,0:T(2,128)S(1)}, s32[1,4,2]{1,2,0:T(2,128)}, u32[]{:S(2)}) copy-start(s32[1,4,2]{1,2,0:T(2,128)} %param.8) | copy-start | bytes 100
  10.2 1.7 %collective-permute-start.4 = (f32[2,2,64,128]{3,2,1,0:T(8,128)S(1)}, f32[2,2,64,128]{3,2,1,0:T(8,128)S(1)}, u32[]{:S(2)}, u32[]{:S(2)}) collective-permute-start(f32[2,2,64,128]{3,2,1,0:T(8,128)S(1)} %collective-permute-done.refs_10_), channel_id=1, source_target_pairs={{0,1},{1,0},{2,3},{3,2},{4,5},{5,4},{6,7},{7,6},{8,9},{9,8},{10,11... | collective-permute-start | bytes 393224 | tf_op jit(solution)/shard_map/ppermute | solution.py:217
  10.2 2.3 %collective-permute-start.1 = (f32[2,2,64,128]{3,2,1,0:T(8,128)S(1)}, f32[2,2,64,128]{3,2,1,0:T(8,128)S(1)}, u32[]{:S(2)}, u32[]{:S(2)}) collective-permute-start(f32[2,2,64,128]{3,2,1,0:T(8,128)S(1)} %bitcast.5), channel_id=1, source_target_pairs={{0,1},{1,0},{2,3},{3,2},{4,5},{5,4},{6,7},{7,6},{8,9},{9,8},{10,11... | collective-permute-start | bytes 393224 | tf_op jit(solution)/shard_map/ppermute | solution.py:217
  11.9 1.3 %collective-permute-start.5 = (f32[2,2,64,128]{3,2,1,0:T(8,128)S(1)}, f32[2,2,64,128]{3,2,1,0:T(8,128)S(1)}, u32[]{:S(2)}, u32[]{:S(2)}) collective-permute-start(f32[2,2,64,128]{3,2,1,0:T(8,128)S(1)} %collective-permute-done.2.refs_6_), channel_id=1, source_target_pairs={{0,1},{1,0},{2,3},{3,2},{4,5},{5,4},{6,7},{7,6},{8,9},{9,8},{10,11... | collective-permute-start | bytes 393224 | tf_op jit(solution)/shard_map/ppermute | solution.py:217
  11.9 1.5 %collective-permute-start.6 = (f32[2,2,64,128]{3,2,1,0:T(8,128)S(1)}, f32[2,2,64,128]{3,2,1,0:T(8,128)S(1)}, u32[]{:S(2)}, u32[]{:S(2)}) collective-permute-start(f32[2,2,64,128]{3,2,1,0:T(8,128)S(1)} %collective-permute-done.3.refs_8_), channel_id=1, source_target_pairs={{0,1},{1,0},{2,3},{3,2},{4,5},{5,4},{6,7},{7,6},{8,9},{9,8},{10,11... | collective-permute-start | bytes 393224 | tf_op jit(solution)/shard_map/ppermute | solution.py:217
  17.1 1.4 %collective-permute-start.7 = (f32[2,2,64,128]{3,2,1,0:T(8,128)S(1)}, f32[2,2,64,128]{3,2,1,0:T(8,128)S(1)}, u32[]{:S(2)}, u32[]{:S(2)}) collective-permute-start(f32[2,2,64,128]{3,2,1,0:T(8,128)S(1)} %get-tuple-element.33), channel_id=1, source_target_pairs={{0,1},{1,0},{2,3},{3,2},{4,5},{5,4},{6,7},{7,6},{8,9},{9,8},{10,11... | collective-permute-start | bytes 393224 | tf_op jit(solution)/shard_map/ppermute | solution.py:217
  17.5 2.1 %collective-permute-start.10 = (f32[2,2,64,128]{3,2,1,0:T(8,128)S(1)}, f32[2,2,64,128]{3,2,1,0:T(8,128)S(1)}, u32[]{:S(2)}, u32[]{:S(2)}) collective-permute-start(f32[2,2,64,128]{3,2,1,0:T(8,128)S(1)} %get-tuple-element.38), channel_id=1, source_target_pairs={{0,1},{1,0},{2,3},{3,2},{4,5},{5,4},{6,7},{7,6},{8,9},{9,8},{10,11... | collective-permute-start | bytes 393224 | tf_op jit(solution)/shard_map/ppermute | solution.py:217
  17.7 2.9 %collective-permute-start.12 = (f32[2,2,64,128]{3,2,1,0:T(8,128)S(1)}, f32[2,2,64,128]{3,2,1,0:T(8,128)S(1)}, u32[]{:S(2)}, u32[]{:S(2)}) collective-permute-start(f32[2,2,64,128]{3,2,1,0:T(8,128)S(1)} %get-tuple-element.40), channel_id=1, source_target_pairs={{0,1},{1,0},{2,3},{3,2},{4,5},{5,4},{6,7},{7,6},{8,9},{9,8},{10,11... | collective-permute-start | bytes 393224 | tf_op jit(solution)/shard_map/ppermute | solution.py:217
  18.5 9.2 %collective-permute-start.9 = (f32[2,2,64,128]{3,2,1,0:T(8,128)S(1)}, f32[2,2,64,128]{3,2,1,0:T(8,128)S(1)}, u32[]{:S(2)}, u32[]{:S(2)}) collective-permute-start(f32[2,2,64,128]{3,2,1,0:T(8,128)S(1)} %add.9), channel_id=1, source_target_pairs={{0,6},{1,7},{2,4},{3,5},{4,10},{5,11},{6,8},{7,9},{8,14},{9,15},{1... | collective-permute-start | bytes 393224 | tf_op jit(solution)/shard_map/ppermute | solution.py:231
  19.5 8.2 %collective-permute-start.8 = (f32[2,2,64,128]{3,2,1,0:T(8,128)S(1)}, f32[2,2,64,128]{3,2,1,0:T(8,128)S(1)}, u32[]{:S(2)}, u32[]{:S(2)}) collective-permute-start(f32[2,2,64,128]{3,2,1,0:T(8,128)S(1)} %get-tuple-element.34), channel_id=1, source_target_pairs={{0,1},{1,0},{2,3},{3,2},{4,5},{5,4},{6,7},{7,6},{8,9},{9,8},{10,11... | collective-permute-start | bytes 393224 | tf_op jit(solution)/shard_map/ppermute | solution.py:217
  19.6 8.7 %collective-permute-start.11 = (f32[2,2,64,128]{3,2,1,0:T(8,128)S(1)}, f32[2,2,64,128]{3,2,1,0:T(8,128)S(1)}, u32[]{:S(2)}, u32[]{:S(2)}) collective-permute-start(f32[2,2,64,128]{3,2,1,0:T(8,128)S(1)} %add.10), channel_id=1, source_target_pairs={{0,2},{1,3},{2,0},{3,1},{4,6},{5,7},{6,4},{7,5},{8,10},{9,11},{10,... | collective-permute-start | bytes 393224 | tf_op jit(solution)/shard_map/ppermute | solution.py:231
  20.6 9.1 %collective-permute-start.13 = (f32[2,2,64,128]{3,2,1,0:T(8,128)S(1)}, f32[2,2,64,128]{3,2,1,0:T(8,128)S(1)}, u32[]{:S(2)}, u32[]{:S(2)}) collective-permute-start(f32[2,2,64,128]{3,2,1,0:T(8,128)S(1)} %add.11), channel_id=1, source_target_pairs={{0,4},{1,5},{2,6},{3,7},{4,8},{5,9},{6,10},{7,11},{8,12},{9,13},{1... | collective-permute-start | bytes 393224 | tf_op jit(solution)/shard_map/ppermute | solution.py:231

commit v8 on v6

--- a/solution.py
+++ b/solution.py
@@ -49,9 +49,9 @@
 
 def times_left(table_ref, values):
     high, low = split(values)
-    table = jnp.concatenate([table_ref[0], table_ref[0], table_ref[1]], axis=1)
-    stacked = jnp.concatenate([high, low, high], axis=0)
-    return jnp.dot(table, stacked, preferred_element_type=jnp.float32)
+    rows = values.shape[0]
+    both = jnp.dot(jnp.concatenate([table_ref[0], table_ref[1]], axis=0), high, preferred_element_type=jnp.float32)
+    return both[:rows] + both[rows:] + jnp.dot(table_ref[0], low, preferred_element_type=jnp.float32)
 
 
 def transform(pairs, right_ref, left_ref, window):
@@ -179,10 +179,17 @@
 
 
 def sum_kernel(scale, *refs):
-    total = refs[0][...]
-    for ref in refs[1:-1]:
-        total += ref[...]
-    refs[-1][...] = total * scale
+    inputs, (out_ref, total_ref, sems) = refs[:-3], refs[-3:]
+    copies = []
+    for layer in range(out_ref.shape[0]):
+        total = inputs[0][layer]
+        for ref in inputs[1:]:
+            total += ref[layer]
+        total_ref[layer] = total * scale
+        copies.append(pltpu.make_async_copy(total_ref.at[layer], out_ref.at[layer], sems.at[layer]))
+        copies[-1].start()
+    for copy in copies:
+        copy.wait()
 
 
 VMEM = pl.BlockSpec(memory_space=pltpu.VMEM)
@@ -277,7 +284,8 @@
         lambda *refs: sum_kernel(1.0 / (count * devices), *refs),
         out_shape=unit,
         in_specs=[VMEM] * (len(steps) + 1),
-        out_specs=VMEM,
+        out_specs=HBM,
+        scratch_shapes=[pltpu.VMEM(unit.shape, jnp.float32), pltpu.SemaphoreType.DMA((layers,))],
         compiler_params=PARAMS,
     )(keep[0], other_own, *terms)
     return jnp.swapaxes(gradient, 2, 3)

time: 30.6 us -> 30.6 us (level)
  no operation moved by 1% of the time
where the time goes in v8:
time: 30.6 us; the launch traced here: 30.5 us
  starting transfers between devices  12.6 us (41%)
  waiting for transfers between devices  11.9 us (39%)
  Pallas kernels  5.83 us (19%)
    ppermute x3, waiting for transfers between devices, give(): return lax.ppermute(value, ('region', 'probe'), route(step, band))  7.5 us
    ppermute x3, starting transfers between devices, fetch(): lax.ppermute(value, ('region', 'probe'), [(b, a) for a, b in route(step,...  6.96 us
    pallas_call x1, Pallas kernels, body(): pl.pallas_call(lambda *refs: main_kernel(ring, window, *refs), out_shape=...  3.73 us
    ppermute x3, starting transfers between devices, give(): return lax.ppermute(value, ('region', 'probe'), route(step, band))  3.62 us
    ppermute x3, waiting for transfers between devices, fetch(): lax.ppermute(value, ('region', 'probe'), [(b, a) for a, b in route(step,...  2.95 us
    ppermute x8, starting transfers between devices, swap(): return lax.ppermute(value, 'probe', [(i, i ^ 1) for i in range(devices)])  1.98 us
    ppermute x8, waiting for transfers between devices, swap(): return lax.ppermute(value, 'probe', [(i, i ^ 1) for i in range(devices)])  1.43 us
    pallas_call x1, Pallas kernels, body(): pl.pallas_call(prepare_kernel, out_shape=[jax.ShapeDtypeStruct(probe.shap...  1.41 us
  transfers between devices with their start and end apart: 14, of which 8 were waited for; matrix products, arithmetic and copies ran while one was open for 0% of the time, Pallas kernels for 5%

profile of v8, /device:TPU:0, one launch (start us, length us, event | category | flops | bytes accessed | tf_op | source)
XLA Modules:
  0.0 30.5 jit_solution(15738887459357701055)
XLA Ops:
  0.0 0.0 copy-start
  0.0 6.0 %collective-permute-start = (f32[2,2,64,128]{3,2,1,0:T(8,128)}, f32[2,2,64,128]{3,2,1,0:T(8,128)S(1)}, u32[]{:S(2)}, u32[]{:S(2)}) collective-permute-start(f32[2,2,64,128]{3,2,1,0:T(8,128)} %bitcast.2), channel_id=1, source_target_pairs={{6,0},{7,1},{4,2},{5,3},{10,4},{11,5},{8,6},{9,7},{14,8},{15,9},{1... | collective-permute-start | bytes 393224 | tf_op jit(solution)/shard_map/ppermute | solution.py:232
  6.0 0.5 %collective-permute-start.3 = (f32[2,2,64,128]{3,2,1,0:T(8,128)}, f32[2,2,64,128]{3,2,1,0:T(8,128)S(1)}, u32[]{:S(2)}, u32[]{:S(2)}) collective-permute-start(f32[2,2,64,128]{3,2,1,0:T(8,128)} %bitcast.3), channel_id=1, source_target_pairs={{2,0},{3,1},{0,2},{1,3},{6,4},{7,5},{4,6},{5,7},{10,8},{11,9},{8,1... | collective-permute-start | bytes 393224 | tf_op jit(solution)/shard_map/ppermute | solution.py:232
  6.5 0.4 %collective-permute-start.2 = (f32[2,2,64,128]{3,2,1,0:T(8,128)}, f32[2,2,64,128]{3,2,1,0:T(8,128)S(1)}, u32[]{:S(2)}, u32[]{:S(2)}) collective-permute-start(f32[2,2,64,128]{3,2,1,0:T(8,128)} %bitcast.4), channel_id=1, source_target_pairs={{4,0},{5,1},{6,2},{7,3},{8,4},{9,5},{10,6},{11,7},{12,8},{13,9},{1... | collective-permute-start | bytes 393224 | tf_op jit(solution)/shard_map/ppermute | solution.py:232
  7.0 1.4 %shard_map.55 = (f32[2,128,128]{2,1,0:T(8,128)S(1)}, f32[4,128,128]{2,1,0:T(8,128)S(1)}, bf16[4,2,256,256]{3,2,1,0:T(8,128)(2,1)S(1)}) custom-call(f32[2,128,128]{2,1,0:T(8,128)} %refs_0_.2, f32[1,4,128,128]{3,2,1,0:T(8,128)} %refs_1_.1, bf16[4,2,256,256]{3,2,1,0:T(8,128)(2,1)} %constant.2.clone.refs_2_), custom_call_target="tpu_custom_call" | custom-call | flops 1 | bytes 1 | tf_op jit(solution)/shard_map/pallas_call | solution.py:239
  8.4 0.0 copy-start.1
  8.4 1.8 %collective-permute-done.refs_10_ = f32[2,2,64,128]{3,2,1,0:T(8,128)S(1)} collective-permute-done((f32[2,2,64,128]{3,2,1,0:T(8,128)}, f32[2,2,64,128]{3,2,1,0:T(8,128)S(1)}, u32[]{:S(2)}, u32[]{:S(2)}) %collective-permute-start) | collective-permute-done | bytes 131104 | tf_op jit(solution)/shard_map/ppermute | solution.py:232
  10.2 0.0 collective-permute-start.4
  10.2 0.0 copy-done
  10.2 0.5 %collective-permute-start.1 = (f32[2,2,64,128]{3,2,1,0:T(8,128)S(1)}, f32[2,2,64,128]{3,2,1,0:T(8,128)S(1)}, u32[]{:S(2)}, u32[]{:S(2)}) collective-permute-start(f32[2,2,64,128]{3,2,1,0:T(8,128)S(1)} %bitcast.5), channel_id=1, source_target_pairs={{0,1},{1,0},{2,3},{3,2},{4,5},{5,4},{6,7},{7,6},{8,9},{9,8},{10,11... | collective-permute-start | bytes 393224 | tf_op jit(solution)/shard_map/ppermute | solution.py:221
  10.7 0.4 %collective-permute-done.3.refs_8_ = f32[2,2,64,128]{3,2,1,0:T(8,128)S(1)} collective-permute-done((f32[2,2,64,128]{3,2,1,0:T(8,128)}, f32[2,2,64,128]{3,2,1,0:T(8,128)S(1)}, u32[]{:S(2)}, u32[]{:S(2)}) %collective-permute-start.3) | collective-permute-done | bytes 131104 | tf_op jit(solution)/shard_map/ppermute | solution.py:232
  11.2 0.7 %collective-permute-done.2.refs_6_ = f32[2,2,64,128]{3,2,1,0:T(8,128)S(1)} collective-permute-done((f32[2,2,64,128]{3,2,1,0:T(8,128)}, f32[2,2,64,128]{3,2,1,0:T(8,128)S(1)}, u32[]{:S(2)}, u32[]{:S(2)}) %collective-permute-start.2) | collective-permute-done | bytes 131104 | tf_op jit(solution)/shard_map/ppermute | solution.py:232
  11.9 0.0 collective-permute-done.4.refs_11_
  11.9 0.0 collective-permute-start.5
  11.9 0.5 %collective-permute-start.6 = (f32[2,2,64,128]{3,2,1,0:T(8,128)S(1)}, f32[2,2,64,128]{3,2,1,0:T(8,128)S(1)}, u32[]{:S(2)}, u32[]{:S(2)}) collective-permute-start(f32[2,2,64,128]{3,2,1,0:T(8,128)S(1)} %collective-permute-done.3.refs_8_), channel_id=1, source_target_pairs={{0,1},{1,0},{2,3},{3,2},{4,5},{5,4},{6,7},{7,6},{8,9},{9,8},{10,11... | collective-permute-start | bytes 393224 | tf_op jit(solution)/shard_map/ppermute | solution.py:221
  12.4 0.0 copy-done.1
  12.4 0.1 copy.6.refs_0_
  12.5 0.0 collective-permute-done.1.refs_5_
  12.5 0.7 %collective-permute-done.5.refs_7_ = f32[2,2,64,128]{3,2,1,0:T(8,128)S(1)} collective-permute-done((f32[2,2,64,128]{3,2,1,0:T(8,128)S(1)}, f32[2,2,64,128]{3,2,1,0:T(8,128)S(1)}, u32[]{:S(2)}, u32[]{:S(2)}) %collective-permute-start.5) | collective-permute-done | bytes 131104 | tf_op jit(solution)/shard_map/ppermute | solution.py:221
  13.2 0.2 collective-permute-done.6.refs_9_
  13.4 3.7 %shard_map.56 = (f32[2,2,64,128]{3,2,1,0:T(8,128)S(1)}, f32[2,2,64,128]{3,2,1,0:T(8,128)S(1)}, f32[2,2,64,128]{3,2,1,0:T(8,128)S(1)}, f32[2,2,64,128]{3,2,1,0:T(...) custom-call(s32[1,4,2]{2,1,0:T(4,128)S(1)} %copy.6.refs_0_, ...), custom_call_target="tpu_custom_call" | custom-call | flops 1610612736 | bytes 8388608 | tf_op jit(solution)/shard_map/pallas_call | solution.py:268
  17.1 0.4 %collective-permute-start.7 = (f32[2,2,64,128]{3,2,1,0:T(8,128)S(1)}, f32[2,2,64,128]{3,2,1,0:T(8,128)S(1)}, u32[]{:S(2)}, u32[]{:S(2)}) collective-permute-start(f32[2,2,64,128]{3,2,1,0:T(8,128)S(1)} %get-tuple-element.33), channel_id=1, source_target_pairs={{0,1},{1,0},{2,3},{3,2},{4,5},{5,4},{6,7},{7,6},{8,9},{9,8},{10,11... | collective-permute-start | bytes 393224 | tf_op jit(solution)/shard_map/ppermute | solution.py:221
  17.5 0.2 collective-permute-start.10
  17.7 0.3 %collective-permute-start.12 = (f32[2,2,64,128]{3,2,1,0:T(8,128)S(1)}, f32[2,2,64,128]{3,2,1,0:T(8,128)S(1)}, u32[]{:S(2)}, u32[]{:S(2)}) collective-permute-start(f32[2,2,64,128]{3,2,1,0:T(8,128)S(1)} %get-tuple-element.40), channel_id=1, source_target_pairs={{0,1},{1,0},{2,3},{3,2},{4,5},{5,4},{6,7},{7,6},{8,9},{9,8},{10,11... | collective-permute-start | bytes 393224 | tf_op jit(solution)/shard_map/ppermute | solution.py:221
  18.1 0.5 %collective-permute-done.7 = f32[2,2,64,128]{3,2,1,0:T(8,128)S(1)} collective-permute-done((f32[2,2,64,128]{3,2,1,0:T(8,128)S(1)}, f32[2,2,64,128]{3,2,1,0:T(8,128)S(1)}, u32[]{:S(2)}, u32[]{:S(2)}) %collective-permute-start.7) | collective-permute-done | bytes 131104 | tf_op jit(solution)/shard_map/ppermute | solution.py:221
  18.6 1.0 %collective-permute-start.9 = (f32[2,2,64,128]{3,2,1,0:T(8,128)S(1)}, f32[2,2,64,128]{3,2,1,0:T(8,128)S(1)}, u32[]{:S(2)}, u32[]{:S(2)}) collective-permute-start(f32[2,2,64,128]{3,2,1,0:T(8,128)S(1)} %add.9), channel_id=1, source_target_pairs={{0,6},{1,7},{2,4},{3,5},{4,10},{5,11},{6,8},{7,9},{8,14},{9,15},{1... | collective-permute-start | bytes 393224 | tf_op jit(solution)/shard_map/ppermute | solution.py:235
  19.6 0.0 collective-permute-start.8
  19.6 0.0 collective-permute-done.10
  19.6 1.6 %collective-permute-start.11 = (f32[2,2,64,128]{3,2,1,0:T(8,128)S(1)}, f32[2,2,64,128]{3,2,1,0:T(8,128)S(1)}, u32[]{:S(2)}, u32[]{:S(2)}) collective-permute-start(f32[2,2,64,128]{3,2,1,0:T(8,128)S(1)} %add.10), channel_id=1, source_target_pairs={{0,4},{1,5},{2,6},{3,7},{4,8},{5,9},{6,10},{7,11},{8,12},{9,13},{1... | collective-permute-start | bytes 393224 | tf_op jit(solution)/shard_map/ppermute | solution.py:235
  21.3 0.0 collective-permute-done.12
  21.3 1.0 %collective-permute-start.13 = (f32[2,2,64,128]{3,2,1,0:T(8,128)S(1)}, f32[2,2,64,128]{3,2,1,0:T(8,128)S(1)}, u32[]{:S(2)}, u32[]{:S(2)}) collective-permute-start(f32[2,2,64,128]{3,2,1,0:T(8,128)S(1)} %add.11), channel_id=1, source_target_pairs={{0,2},{1,3},{2,0},{3,1},{4,6},{5,7},{6,4},{7,5},{8,10},{9,11},{10,... | collective-permute-start | bytes 393224 | tf_op jit(solution)/shard_map/ppermute | solution.py:235
  22.3 5.5 %collective-permute-done.9.refs_2_ = f32[2,2,64,128]{3,2,1,0:T(8,128)S(1)} collective-permute-done((f32[2,2,64,128]{3,2,1,0:T(8,128)S(1)}, f32[2,2,64,128]{3,2,1,0:T(8,128)S(1)}, u32[]{:S(2)}, u32[]{:S(2)}) %collective-permute-start.9) | collective-permute-done | bytes 131104 | tf_op jit(solution)/shard_map/ppermute | solution.py:235
  27.7 0.0 collective-permute-done.8.refs_1_
  27.7 2.0 %collective-permute-done.11.refs_3_ = f32[2,2,64,128]{3,2,1,0:T(8,128)S(1)} collective-permute-done((f32[2,2,64,128]{3,2,1,0:T(8,128)S(1)}, f32[2,2,64,128]{3,2,1,0:T(8,128)S(1)}, u32[]{:S(2)}, u32[]{:S(2)}) %collective-permute-start.11) | collective-permute-done | bytes 131104 | tf_op jit(solution)/shard_map/ppermute | solution.py:235
  29.8 0.0 collective-permute-done.13.refs_4_
  29.8 0.7 %shard_map.57 = f32[2,2,64,128]{3,2,1,0:T(8,128)} custom-call(f32[2,2,64,128]{3,2,1,0:T(8,128)S(1)} %get-tuple-element.31.refs_0_, f32[2,2,64,128]{3,2,1,0:T(8,128)S(1)} %collective-permute-done.8.refs_1_, f32[2,2,64,128]{3,2,1,0:T(8,128)S(1)} %collective-permute-done.9.refs_2_, f32[2,2,64,128]{3,2,1,0:T(8,128)S(1)} %collective-permute-done.11.refs_3_, ...), custom_call_target="tpu_custom_call" | custom-call | tf_op jit(solution)/shard_map/pallas_call | solution.py:283
  (3 shorter events, 0.0 us)
Async XLA Ops:
  0.0 10.2 %copy-start = (f32[2,2,128,64]{2,3,1,0:T(8,128)S(1)}, f32[2,2,128,64]{2,3,1,0:T(8,128)}, u32[]{:S(2)}) copy-start(f32[2,2,128,64]{2,3,1,0:T(8,128)} %param.5) | copy-start | bytes 393220
  0.0 10.2 %collective-permute-start = (f32[2,2,64,128]{3,2,1,0:T(8,128)}, f32[2,2,64,128]{3,2,1,0:T(8,128)S(1)}, u32[]{:S(2)}, u32[]{:S(2)}) collective-permute-start(f32[2,2,64,128]{3,2,1,0:T(8,128)} %bitcast.2), channel_id=1, source_target_pairs={{6,0},{7,1},{4,2},{5,3},{10,4},{11,5},{8,6},{9,7},{14,8},{15,9},{1... | collective-permute-start | bytes 393224 | tf_op jit(solution)/shard_map/ppermute | solution.py:232
  6.0 5.2 %collective-permute-start.3 = (f32[2,2,64,128]{3,2,1,0:T(8,128)}, f32[2,2,64,128]{3,2,1,0:T(8,128)S(1)}, u32[]{:S(2)}, u32[]{:S(2)}) collective-permute-start(f32[2,2,64,128]{3,2,1,0:T(8,128)} %bitcast.3), channel_id=1, source_target_pairs={{2,0},{3,1},{0,2},{1,3},{6,4},{7,5},{4,6},{5,7},{10,8},{11,9},{8,1... | collective-permute-start | bytes 393224 | tf_op jit(solution)/shard_map/ppermute | solution.py:232
  6.5 5.3 %collective-permute-start.2 = (f32[2,2,64,128]{3,2,1,0:T(8,128)}, f32[2,2,64,128]{3,2,1,0:T(8,128)S(1)}, u32[]{:S(2)}, u32[]{:S(2)}) collective-permute-start(f32[2,2,64,128]{3,2,1,0:T(8,128)} %bitcast.4), channel_id=1, source_target_pairs={{4,0},{5,1},{6,2},{7,3},{8,4},{9,5},{10,6},{11,7},{12,8},{13,9},{1... | collective-permute-start | bytes 393224 | tf_op jit(solution)/shard_map/ppermute | solution.py:232
  8.4 4.0 %copy-start.1 = (s32[1,4,2]{1,2,0:T(2,128)S(1)}, s32[1,4,2]{1,2,0:T(2,128)}, u32[]{:S(2)}) copy-start(s32[1,4,2]{1,2,0:T(2,128)} %param.8) | copy-start | bytes 100
  10.2 1.7 %collective-permute-start.4 = (f32[2,2,64,128]{3,2,1,0:T(8,128)S(1)}, f32[2,2,64,128]{3,2,1,0:T(8,128)S(1)}, u32[]{:S(2)}, u32[]{:S(2)}) collective-permute-start(f32[2,2,64,128]{3,2,1,0:T(8,128)S(1)} %collective-permute-done.refs_10_), channel_id=1, source_target_pairs={{0,1},{1,0},{2,3},{3,2},{4,5},{5,4},{6,7},{7,6},{8,9},{9,8},{10,11... | collective-permute-start | bytes 393224 | tf_op jit(solution)/shard_map/ppermute | solution.py:221
  10.2 2.3 %collective-permute-start.1 = (f32[2,2,64,128]{3,2,1,0:T(8,128)S(1)}, f32[2,2,64,128]{3,2,1,0:T(8,128)S(1)}, u32[]{:S(2)}, u32[]{:S(2)}) collective-permute-start(f32[2,2,64,128]{3,2,1,0:T(8,128)S(1)} %bitcast.5), channel_id=1, source_target_pairs={{0,1},{1,0},{2,3},{3,2},{4,5},{5,4},{6,7},{7,6},{8,9},{9,8},{10,11... | collective-permute-start | bytes 393224 | tf_op jit(solution)/shard_map/ppermute | solution.py:221
  11.9 1.3 %collective-permute-start.5 = (f32[2,2,64,128]{3,2,1,0:T(8,128)S(1)}, f32[2,2,64,128]{3,2,1,0:T(8,128)S(1)}, u32[]{:S(2)}, u32[]{:S(2)}) collective-permute-start(f32[2,2,64,128]{3,2,1,0:T(8,128)S(1)} %collective-permute-done.2.refs_6_), channel_id=1, source_target_pairs={{0,1},{1,0},{2,3},{3,2},{4,5},{5,4},{6,7},{7,6},{8,9},{9,8},{10,11... | collective-permute-start | bytes 393224 | tf_op jit(solution)/shard_map/ppermute | solution.py:221
  11.9 1.5 %collective-permute-start.6 = (f32[2,2,64,128]{3,2,1,0:T(8,128)S(1)}, f32[2,2,64,128]{3,2,1,0:T(8,128)S(1)}, u32[]{:S(2)}, u32[]{:S(2)}) collective-permute-start(f32[2,2,64,128]{3,2,1,0:T(8,128)S(1)} %collective-permute-done.3.refs_8_), channel_id=1, source_target_pairs={{0,1},{1,0},{2,3},{3,2},{4,5},{5,4},{6,7},{7,6},{8,9},{9,8},{10,11... | collective-permute-start | bytes 393224 | tf_op jit(solution)/shard_map/ppermute | solution.py:221
  17.1 1.4 %collective-permute-start.7 = (f32[2,2,64,128]{3,2,1,0:T(8,128)S(1)}, f32[2,2,64,128]{3,2,1,0:T(8,128)S(1)}, u32[]{:S(2)}, u32[]{:S(2)}) collective-permute-start(f32[2,2,64,128]{3,2,1,0:T(8,128)S(1)} %get-tuple-element.33), channel_id=1, source_target_pairs={{0,1},{1,0},{2,3},{3,2},{4,5},{5,4},{6,7},{7,6},{8,9},{9,8},{10,11... | collective-permute-start | bytes 393224 | tf_op jit(solution)/shard_map/ppermute | solution.py:221
  17.5 2.1 %collective-permute-start.10 = (f32[2,2,64,128]{3,2,1,0:T(8,128)S(1)}, f32[2,2,64,128]{3,2,1,0:T(8,128)S(1)}, u32[]{:S(2)}, u32[]{:S(2)}) collective-permute-start(f32[2,2,64,128]{3,2,1,0:T(8,128)S(1)} %get-tuple-element.38), channel_id=1, source_target_pairs={{0,1},{1,0},{2,3},{3,2},{4,5},{5,4},{6,7},{7,6},{8,9},{9,8},{10,11... | collective-permute-start | bytes 393224 | tf_op jit(solution)/shard_map/ppermute | solution.py:221
  17.7 3.5 %collective-permute-start.12 = (f32[2,2,64,128]{3,2,1,0:T(8,128)S(1)}, f32[2,2,64,128]{3,2,1,0:T(8,128)S(1)}, u32[]{:S(2)}, u32[]{:S(2)}) collective-permute-start(f32[2,2,64,128]{3,2,1,0:T(8,128)S(1)} %get-tuple-element.40), channel_id=1, source_target_pairs={{0,1},{1,0},{2,3},{3,2},{4,5},{5,4},{6,7},{7,6},{8,9},{9,8},{10,11... | collective-permute-start | bytes 393224 | tf_op jit(solution)/shard_map/ppermute | solution.py:221
  18.6 9.2 %collective-permute-start.9 = (f32[2,2,64,128]{3,2,1,0:T(8,128)S(1)}, f32[2,2,64,128]{3,2,1,0:T(8,128)S(1)}, u32[]{:S(2)}, u32[]{:S(2)}) collective-permute-start(f32[2,2,64,128]{3,2,1,0:T(8,128)S(1)} %add.9), channel_id=1, source_target_pairs={{0,6},{1,7},{2,4},{3,5},{4,10},{5,11},{6,8},{7,9},{8,14},{9,15},{1... | collective-permute-start | bytes 393224 | tf_op jit(solution)/shard_map/ppermute | solution.py:235
  19.6 8.2 %collective-permute-start.8 = (f32[2,2,64,128]{3,2,1,0:T(8,128)S(1)}, f32[2,2,64,128]{3,2,1,0:T(8,128)S(1)}, u32[]{:S(2)}, u32[]{:S(2)}) collective-permute-start(f32[2,2,64,128]{3,2,1,0:T(8,128)S(1)} %get-tuple-element.34), channel_id=1, source_target_pairs={{0,1},{1,0},{2,3},{3,2},{4,5},{5,4},{6,7},{7,6},{8,9},{9,8},{10,11... | collective-permute-start | bytes 393224 | tf_op jit(solution)/shard_map/ppermute | solution.py:221
  19.6 10.1 %collective-permute-start.11 = (f32[2,2,64,128]{3,2,1,0:T(8,128)S(1)}, f32[2,2,64,128]{3,2,1,0:T(8,128)S(1)}, u32[]{:S(2)}, u32[]{:S(2)}) collective-permute-start(f32[2,2,64,128]{3,2,1,0:T(8,128)S(1)} %add.10), channel_id=1, source_target_pairs={{0,4},{1,5},{2,6},{3,7},{4,8},{5,9},{6,10},{7,11},{8,12},{9,13},{1... | collective-permute-start | bytes 393224 | tf_op jit(solution)/shard_map/ppermute | solution.py:235
  21.3 8.5 %collective-permute-start.13 = (f32[2,2,64,128]{3,2,1,0:T(8,128)S(1)}, f32[2,2,64,128]{3,2,1,0:T(8,128)S(1)}, u32[]{:S(2)}, u32[]{:S(2)}) collective-permute-start(f32[2,2,64,128]{3,2,1,0:T(8,128)S(1)} %add.11), channel_id=1, source_target_pairs={{0,2},{1,3},{2,0},{3,1},{4,6},{5,7},{6,4},{7,5},{8,10},{9,11},{10,... | collective-permute-start | bytes 393224 | tf_op jit(solution)/shard_map/ppermute | solution.py:235

commit v9 on v8

--- a/solution.py
+++ b/solution.py
@@ -10,7 +10,7 @@
 from jax.sharding import PartitionSpec as P
 
 CORES = 2
-PAIRED = 2
+PAIRED = 4
 HALF = 64
 
 
@@ -275,7 +275,7 @@
         cost_estimate=cost(4 * dft_flops, 8 << 20),
     )(positions, probe_t, intensity_t, table, *gathered)
     keep, send = outputs[: len(steps)], outputs[len(steps) :]
-    order = early + late
+    order = early + late[::-1]
     other = {at: swap(send[at]) for at in order}
     own, other[order[0]] = lax.optimization_barrier((send[0], other[order[0]]))
     terms = [give(keep[at] + other[at], *steps[at]) for at in order]

time: 30.6 us -> 30.6 us (level)
  transfers between devices with their start and end apart: 14 -> 14, of which waited for: 8 -> 9; matrix products, arithmetic and copies ran while one was open for 0% -> 0% of each run, Pallas kernels for 5% -> 5%
where the time goes in v9:
time: 30.6 us; the launch traced here: 30.5 us
  starting transfers between devices  12.6 us (41%)
  waiting for transfers between devices  11.9 us (39%)
  Pallas kernels  5.83 us (19%)
    ppermute x3, waiting for transfers between devices, give(): return lax.ppermute(value, ('region', 'probe'), route(step, band))  7.49 us
    ppermute x3, starting transfers between devices, fetch(): lax.ppermute(value, ('region', 'probe'), [(b, a) for a, b in route(step,...  6.96 us
    pallas_call x1, Pallas kernels, body(): pl.pallas_call(lambda *refs: main_kernel(ring, window, *refs), out_shape=...  3.74 us
    ppermute x3, starting transfers between devices, give(): return lax.ppermute(value, ('region', 'probe'), route(step, band))  3.59 us
    ppermute x3, waiting for transfers between devices, fetch(): lax.ppermute(value, ('region', 'probe'), [(b, a) for a, b in route(step,...  2.95 us
    ppermute x8, starting transfers between devices, swap(): return lax.ppermute(value, 'probe', [(i, i ^ 1) for i in range(devices)])  2.02 us
    ppermute x8, waiting for transfers between devices, swap(): return lax.ppermute(value, 'probe', [(i, i ^ 1) for i in range(devices)])  1.42 us
    pallas_call x1, Pallas kernels, body(): pl.pallas_call(prepare_kernel, out_shape=[jax.ShapeDtypeStruct(probe.shap...  1.41 us
  transfers between devices with their start and end apart: 14, of which 9 were waited for; matrix products, arithmetic and copies ran while one was open for 0% of the time, Pallas kernels for 5%

profile of v9, /device:TPU:0, one launch (start us, length us, event | category | flops | bytes accessed | tf_op | source)
XLA Modules:
  0.0 30.5 jit_solution(4552998748650541739)
XLA Ops:
  0.0 0.0 copy-start
  0.0 6.0 %collective-permute-start = (f32[2,2,64,128]{3,2,1,0:T(8,128)}, f32[2,2,64,128]{3,2,1,0:T(8,128)S(1)}, u32[]{:S(2)}, u32[]{:S(2)}) collective-permute-start(f32[2,2,64,128]{3,2,1,0:T(8,128)} %bitcast.2), channel_id=1, source_target_pairs={{6,0},{7,1},{4,2},{5,3},{10,4},{11,5},{8,6},{9,7},{14,8},{15,9},{1... | collective-permute-start | bytes 393224 | tf_op jit(solution)/shard_map/ppermute | solution.py:232
  6.0 0.5 %collective-permute-start.3 = (f32[2,2,64,128]{3,2,1,0:T(8,128)}, f32[2,2,64,128]{3,2,1,0:T(8,128)S(1)}, u32[]{:S(2)}, u32[]{:S(2)}) collective-permute-start(f32[2,2,64,128]{3,2,1,0:T(8,128)} %bitcast.3), channel_id=1, source_target_pairs={{2,0},{3,1},{0,2},{1,3},{6,4},{7,5},{4,6},{5,7},{10,8},{11,9},{8,1... | collective-permute-start | bytes 393224 | tf_op jit(solution)/shard_map/ppermute | solution.py:232
  6.5 0.4 %collective-permute-start.2 = (f32[2,2,64,128]{3,2,1,0:T(8,128)}, f32[2,2,64,128]{3,2,1,0:T(8,128)S(1)}, u32[]{:S(2)}, u32[]{:S(2)}) collective-permute-start(f32[2,2,64,128]{3,2,1,0:T(8,128)} %bitcast.4), channel_id=1, source_target_pairs={{4,0},{5,1},{6,2},{7,3},{8,4},{9,5},{10,6},{11,7},{12,8},{13,9},{1... | collective-permute-start | bytes 393224 | tf_op jit(solution)/shard_map/ppermute | solution.py:232
  7.0 1.4 %shard_map.55 = (f32[2,128,128]{2,1,0:T(8,128)S(1)}, f32[4,128,128]{2,1,0:T(8,128)S(1)}, bf16[4,2,256,256]{3,2,1,0:T(8,128)(2,1)S(1)}) custom-call(f32[2,128,128]{2,1,0:T(8,128)} %refs_0_.2, f32[1,4,128,128]{3,2,1,0:T(8,128)} %refs_1_.1, bf16[4,2,256,256]{3,2,1,0:T(8,128)(2,1)} %constant.2.clone.refs_2_), custom_call_target="tpu_custom_call" | custom-call | flops 1 | bytes 1 | tf_op jit(solution)/shard_map/pallas_call | solution.py:239
  8.4 0.0 copy-start.1
  8.4 1.8 %collective-permute-done.refs_10_ = f32[2,2,64,128]{3,2,1,0:T(8,128)S(1)} collective-permute-done((f32[2,2,64,128]{3,2,1,0:T(8,128)}, f32[2,2,64,128]{3,2,1,0:T(8,128)S(1)}, u32[]{:S(2)}, u32[]{:S(2)}) %collective-permute-start) | collective-permute-done | bytes 131104 | tf_op jit(solution)/shard_map/ppermute | solution.py:232
  10.2 0.0 collective-permute-start.4
  10.2 0.0 copy-done
  10.2 0.5 %collective-permute-start.1 = (f32[2,2,64,128]{3,2,1,0:T(8,128)S(1)}, f32[2,2,64,128]{3,2,1,0:T(8,128)S(1)}, u32[]{:S(2)}, u32[]{:S(2)}) collective-permute-start(f32[2,2,64,128]{3,2,1,0:T(8,128)S(1)} %bitcast.5), channel_id=1, source_target_pairs={{0,1},{1,0},{2,3},{3,2},{4,5},{5,4},{6,7},{7,6},{8,9},{9,8},{10,11... | collective-permute-start | bytes 393224 | tf_op jit(solution)/shard_map/ppermute | solution.py:221
  10.7 0.4 %collective-permute-done.3.refs_8_ = f32[2,2,64,128]{3,2,1,0:T(8,128)S(1)} collective-permute-done((f32[2,2,64,128]{3,2,1,0:T(8,128)}, f32[2,2,64,128]{3,2,1,0:T(8,128)S(1)}, u32[]{:S(2)}, u32[]{:S(2)}) %collective-permute-start.3) | collective-permute-done | bytes 131104 | tf_op jit(solution)/shard_map/ppermute | solution.py:232
  11.2 0.7 %collective-permute-done.2.refs_6_ = f32[2,2,64,128]{3,2,1,0:T(8,128)S(1)} collective-permute-done((f32[2,2,64,128]{3,2,1,0:T(8,128)}, f32[2,2,64,128]{3,2,1,0:T(8,128)S(1)}, u32[]{:S(2)}, u32[]{:S(2)}) %collective-permute-start.2) | collective-permute-done | bytes 131104 | tf_op jit(solution)/shard_map/ppermute | solution.py:232
  11.9 0.0 collective-permute-done.4.refs_11_
  11.9 0.0 collective-permute-start.5
  11.9 0.5 %collective-permute-start.6 = (f32[2,2,64,128]{3,2,1,0:T(8,128)S(1)}, f32[2,2,64,128]{3,2,1,0:T(8,128)S(1)}, u32[]{:S(2)}, u32[]{:S(2)}) collective-permute-start(f32[2,2,64,128]{3,2,1,0:T(8,128)S(1)} %collective-permute-done.3.refs_8_), channel_id=1, source_target_pairs={{0,1},{1,0},{2,3},{3,2},{4,5},{5,4},{6,7},{7,6},{8,9},{9,8},{10,11... | collective-permute-start | bytes 393224 | tf_op jit(solution)/shard_map/ppermute | solution.py:221
  12.4 0.0 copy-done.1
  12.4 0.1 copy.6.refs_0_
  12.5 0.0 collective-permute-done.1.refs_5_
  12.5 0.7 %collective-permute-done.5.refs_7_ = f32[2,2,64,128]{3,2,1,0:T(8,128)S(1)} collective-permute-done((f32[2,2,64,128]{3,2,1,0:T(8,128)S(1)}, f32[2,2,64,128]{3,2,1,0:T(8,128)S(1)}, u32[]{:S(2)}, u32[]{:S(2)}) %collective-permute-start.5) | collective-permute-done | bytes 131104 | tf_op jit(solution)/shard_map/ppermute | solution.py:221
  13.2 0.2 collective-permute-done.6.refs_9_
  13.4 3.7 %shard_map.56 = (f32[2,2,64,128]{3,2,1,0:T(8,128)S(1)}, f32[2,2,64,128]{3,2,1,0:T(8,128)S(1)}, f32[2,2,64,128]{3,2,1,0:T(8,128)S(1)}, f32[2,2,64,128]{3,2,1,0:T(...) custom-call(s32[1,4,2]{2,1,0:T(4,128)S(1)} %copy.6.refs_0_, ...), custom_call_target="tpu_custom_call" | custom-call | flops 1610612736 | bytes 8388608 | tf_op jit(solution)/shard_map/pallas_call | solution.py:268
  17.1 0.4 %collective-permute-start.7 = (f32[2,2,64,128]{3,2,1,0:T(8,128)S(1)}, f32[2,2,64,128]{3,2,1,0:T(8,128)S(1)}, u32[]{:S(2)}, u32[]{:S(2)}) collective-permute-start(f32[2,2,64,128]{3,2,1,0:T(8,128)S(1)} %get-tuple-element.33), channel_id=1, source_target_pairs={{0,1},{1,0},{2,3},{3,2},{4,5},{5,4},{6,7},{7,6},{8,9},{9,8},{10,11... | collective-permute-start | bytes 393224 | tf_op jit(solution)/shard_map/ppermute | solution.py:221
  17.6 0.2 collective-permute-start.10
  17.7 0.4 %collective-permute-start.12 = (f32[2,2,64,128]{3,2,1,0:T(8,128)S(1)}, f32[2,2,64,128]{3,2,1,0:T(8,128)S(1)}, u32[]{:S(2)}, u32[]{:S(2)}) collective-permute-start(f32[2,2,64,128]{3,2,1,0:T(8,128)S(1)} %get-tuple-element.40), channel_id=1, source_target_pairs={{0,1},{1,0},{2,3},{3,2},{4,5},{5,4},{6,7},{7,6},{8,9},{9,8},{10,11... | collective-permute-start | bytes 393224 | tf_op jit(solution)/shard_map/ppermute | solution.py:221
  18.1 0.5 %collective-permute-done.7 = f32[2,2,64,128]{3,2,1,0:T(8,128)S(1)} collective-permute-done((f32[2,2,64,128]{3,2,1,0:T(8,128)S(1)}, f32[2,2,64,128]{3,2,1,0:T(8,128)S(1)}, u32[]{:S(2)}, u32[]{:S(2)}) %collective-permute-start.7) | collective-permute-done | bytes 131104 | tf_op jit(solution)/shard_map/ppermute | solution.py:221
  18.6 1.0 %collective-permute-start.9 = (f32[2,2,64,128]{3,2,1,0:T(8,128)S(1)}, f32[2,2,64,128]{3,2,1,0:T(8,128)S(1)}, u32[]{:S(2)}, u32[]{:S(2)}) collective-permute-start(f32[2,2,64,128]{3,2,1,0:T(8,128)S(1)} %add.9), channel_id=1, source_target_pairs={{0,6},{1,7},{2,4},{3,5},{4,10},{5,11},{6,8},{7,9},{8,14},{9,15},{1... | collective-permute-start | bytes 393224 | tf_op jit(solution)/shard_map/ppermute | solution.py:235
  19.6 0.1 collective-permute-start.8
  19.6 0.0 collective-permute-done.10
  19.7 1.0 %collective-permute-start.11 = (f32[2,2,64,128]{3,2,1,0:T(8,128)S(1)}, f32[2,2,64,128]{3,2,1,0:T(8,128)S(1)}, u32[]{:S(2)}, u32[]{:S(2)}) collective-permute-start(f32[2,2,64,128]{3,2,1,0:T(8,128)S(1)} %add.10), channel_id=1, source_target_pairs={{0,2},{1,3},{2,0},{3,1},{4,6},{5,7},{6,4},{7,5},{8,10},{9,11},{10,... | collective-permute-start | bytes 393224 | tf_op jit(solution)/shard_map/ppermute | solution.py:235
  20.6 0.0 collective-permute-done.12
  20.7 1.6 %collective-permute-start.13 = (f32[2,2,64,128]{3,2,1,0:T(8,128)S(1)}, f32[2,2,64,128]{3,2,1,0:T(8,128)S(1)}, u32[]{:S(2)}, u32[]{:S(2)}) collective-permute-start(f32[2,2,64,128]{3,2,1,0:T(8,128)S(1)} %add.11), channel_id=1, source_target_pairs={{0,4},{1,5},{2,6},{3,7},{4,8},{5,9},{6,10},{7,11},{8,12},{9,13},{1... | collective-permute-start | bytes 393224 | tf_op jit(solution)/shard_map/ppermute | solution.py:235
  22.3 5.4 %collective-permute-done.9.refs_2_ = f32[2,2,64,128]{3,2,1,0:T(8,128)S(1)} collective-permute-done((f32[2,2,64,128]{3,2,1,0:T(8,128)S(1)}, f32[2,2,64,128]{3,2,1,0:T(8,128)S(1)}, u32[]{:S(2)}, u32[]{:S(2)}) %collective-permute-start.9) | collective-permute-done | bytes 131104 | tf_op jit(solution)/shard_map/ppermute | solution.py:235
  27.7 0.0 collective-permute-done.8.refs_1_
  27.7 0.6 %collective-permute-done.11.refs_3_ = f32[2,2,64,128]{3,2,1,0:T(8,128)S(1)} collective-permute-done((f32[2,2,64,128]{3,2,1,0:T(8,128)S(1)}, f32[2,2,64,128]{3,2,1,0:T(8,128)S(1)}, u32[]{:S(2)}, u32[]{:S(2)}) %collective-permute-start.11) | collective-permute-done | bytes 131104 | tf_op jit(solution)/shard_map/ppermute | solution.py:235
  28.4 1.4 %collective-permute-done.13.refs_4_ = f32[2,2,64,128]{3,2,1,0:T(8,128)S(1)} collective-permute-done((f32[2,2,64,128]{3,2,1,0:T(8,128)S(1)}, f32[2,2,64,128]{3,2,1,0:T(8,128)S(1)}, u32[]{:S(2)}, u32[]{:S(2)}) %collective-permute-start.13) | collective-permute-done | bytes 131104 | tf_op jit(solution)/shard_map/ppermute | solution.py:235
  29.8 0.7 %shard_map.57 = f32[2,2,64,128]{3,2,1,0:T(8,128)} custom-call(f32[2,2,64,128]{3,2,1,0:T(8,128)S(1)} %get-tuple-element.31.refs_0_, f32[2,2,64,128]{3,2,1,0:T(8,128)S(1)} %collective-permute-done.8.refs_1_, f32[2,2,64,128]{3,2,1,0:T(8,128)S(1)} %collective-permute-done.9.refs_2_, f32[2,2,64,128]{3,2,1,0:T(8,128)S(1)} %collective-permute-done.11.refs_3_, ...), custom_call_target="tpu_custom_call" | custom-call | tf_op jit(solution)/shard_map/pallas_call | solution.py:283
  (3 shorter events, 0.0 us)
Async XLA Ops:
  0.0 10.2 %copy-start = (f32[2,2,128,64]{2,3,1,0:T(8,128)S(1)}, f32[2,2,128,64]{2,3,1,0:T(8,128)}, u32[]{:S(2)}) copy-start(f32[2,2,128,64]{2,3,1,0:T(8,128)} %param.5) | copy-start | bytes 393220
  0.0 10.2 %collective-permute-start = (f32[2,2,64,128]{3,2,1,0:T(8,128)}, f32[2,2,64,128]{3,2,1,0:T(8,128)S(1)}, u32[]{:S(2)}, u32[]{:S(2)}) collective-permute-start(f32[2,2,64,128]{3,2,1,0:T(8,128)} %bitcast.2), channel_id=1, source_target_pairs={{6,0},{7,1},{4,2},{5,3},{10,4},{11,5},{8,6},{9,7},{14,8},{15,9},{1... | collective-permute-start | bytes 393224 | tf_op jit(solution)/shard_map/ppermute | solution.py:232
  6.0 5.2 %collective-permute-start.3 = (f32[2,2,64,128]{3,2,1,0:T(8,128)}, f32[2,2,64,128]{3,2,1,0:T(8,128)S(1)}, u32[]{:S(2)}, u32[]{:S(2)}) collective-permute-start(f32[2,2,64,128]{3,2,1,0:T(8,128)} %bitcast.3), channel_id=1, source_target_pairs={{2,0},{3,1},{0,2},{1,3},{6,4},{7,5},{4,6},{5,7},{10,8},{11,9},{8,1... | collective-permute-start | bytes 393224 | tf_op jit(solution)/shard_map/ppermute | solution.py:232
  6.5 5.3 %collective-permute-start.2 = (f32[2,2,64,128]{3,2,1,0:T(8,128)}, f32[2,2,64,128]{3,2,1,0:T(8,128)S(1)}, u32[]{:S(2)}, u32[]{:S(2)}) collective-permute-start(f32[2,2,64,128]{3,2,1,0:T(8,128)} %bitcast.4), channel_id=1, source_target_pairs={{4,0},{5,1},{6,2},{7,3},{8,4},{9,5},{10,6},{11,7},{12,8},{13,9},{1... | collective-permute-start | bytes 393224 | tf_op jit(solution)/shard_map/ppermute | solution.py:232
  8.4 4.0 %copy-start.1 = (s32[1,4,2]{1,2,0:T(2,128)S(1)}, s32[1,4,2]{1,2,0:T(2,128)}, u32[]{:S(2)}) copy-start(s32[1,4,2]{1,2,0:T(2,128)} %param.8) | copy-start | bytes 100
  10.2 1.7 %collective-permute-start.4 = (f32[2,2,64,128]{3,2,1,0:T(8,128)S(1)}, f32[2,2,64,128]{3,2,1,0:T(8,128)S(1)}, u32[]{:S(2)}, u32[]{:S(2)}) collective-permute-start(f32[2,2,64,128]{3,2,1,0:T(8,128)S(1)} %collective-permute-done.refs_10_), channel_id=1, source_target_pairs={{0,1},{1,0},{2,3},{3,2},{4,5},{5,4},{6,7},{7,6},{8,9},{9,8},{10,11... | collective-permute-start | bytes 393224 | tf_op jit(solution)/shard_map/ppermute | solution.py:221
  10.2 2.3 %collective-permute-start.1 = (f32[2,2,64,128]{3,2,1,0:T(8,128)S(1)}, f32[2,2,64,128]{3,2,1,0:T(8,128)S(1)}, u32[]{:S(2)}, u32[]{:S(2)}) collective-permute-start(f32[2,2,64,128]{3,2,1,0:T(8,128)S(1)} %bitcast.5), channel_id=1, source_target_pairs={{0,1},{1,0},{2,3},{3,2},{4,5},{5,4},{6,7},{7,6},{8,9},{9,8},{10,11... | collective-permute-start | bytes 393224 | tf_op jit(solution)/shard_map/ppermute | solution.py:221
  11.9 1.3 %collective-permute-start.5 = (f32[2,2,64,128]{3,2,1,0:T(8,128)S(1)}, f32[2,2,64,128]{3,2,1,0:T(8,128)S(1)}, u32[]{:S(2)}, u32[]{:S(2)}) collective-permute-start(f32[2,2,64,128]{3,2,1,0:T(8,128)S(1)} %collective-permute-done.2.refs_6_), channel_id=1, source_target_pairs={{0,1},{1,0},{2,3},{3,2},{4,5},{5,4},{6,7},{7,6},{8,9},{9,8},{10,11... | collective-permute-start | bytes 393224 | tf_op jit(solution)/shard_map/ppermute | solution.py:221
  11.9 1.5 %collective-permute-start.6 = (f32[2,2,64,128]{3,2,1,0:T(8,128)S(1)}, f32[2,2,64,128]{3,2,1,0:T(8,128)S(1)}, u32[]{:S(2)}, u32[]{:S(2)}) collective-permute-start(f32[2,2,64,128]{3,2,1,0:T(8,128)S(1)} %collective-permute-done.3.refs_8_), channel_id=1, source_target_pairs={{0,1},{1,0},{2,3},{3,2},{4,5},{5,4},{6,7},{7,6},{8,9},{9,8},{10,11... | collective-permute-start | bytes 393224 | tf_op jit(solution)/shard_map/ppermute | solution.py:221
  17.1 1.4 %collective-permute-start.7 = (f32[2,2,64,128]{3,2,1,0:T(8,128)S(1)}, f32[2,2,64,128]{3,2,1,0:T(8,128)S(1)}, u32[]{:S(2)}, u32[]{:S(2)}) collective-permute-start(f32[2,2,64,128]{3,2,1,0:T(8,128)S(1)} %get-tuple-element.33), channel_id=1, source_target_pairs={{0,1},{1,0},{2,3},{3,2},{4,5},{5,4},{6,7},{7,6},{8,9},{9,8},{10,11... | collective-permute-start | bytes 393224 | tf_op jit(solution)/shard_map/ppermute | solution.py:221
  17.6 2.1 %collective-permute-start.10 = (f32[2,2,64,128]{3,2,1,0:T(8,128)S(1)}, f32[2,2,64,128]{3,2,1,0:T(8,128)S(1)}, u32[]{:S(2)}, u32[]{:S(2)}) collective-permute-start(f32[2,2,64,128]{3,2,1,0:T(8,128)S(1)} %get-tuple-element.38), channel_id=1, source_target_pairs={{0,1},{1,0},{2,3},{3,2},{4,5},{5,4},{6,7},{7,6},{8,9},{9,8},{10,11... | collective-permute-start | bytes 393224 | tf_op jit(solution)/shard_map/ppermute | solution.py:221
  17.7 2.9 %collective-permute-start.12 = (f32[2,2,64,128]{3,2,1,0:T(8,128)S(1)}, f32[2,2,64,128]{3,2,1,0:T(8,128)S(1)}, u32[]{:S(2)}, u32[]{:S(2)}) collective-permute-start(f32[2,2,64,128]{3,2,1,0:T(8,128)S(1)} %get-tuple-element.40), channel_id=1, source_target_pairs={{0,1},{1,0},{2,3},{3,2},{4,5},{5,4},{6,7},{7,6},{8,9},{9,8},{10,11... | collective-permute-start | bytes 393224 | tf_op jit(solution)/shard_map/ppermute | solution.py:221
  18.6 9.2 %collective-permute-start.9 = (f32[2,2,64,128]{3,2,1,0:T(8,128)S(1)}, f32[2,2,64,128]{3,2,1,0:T(8,128)S(1)}, u32[]{:S(2)}, u32[]{:S(2)}) collective-permute-start(f32[2,2,64,128]{3,2,1,0:T(8,128)S(1)} %add.9), channel_id=1, source_target_pairs={{0,6},{1,7},{2,4},{3,5},{4,10},{5,11},{6,8},{7,9},{8,14},{9,15},{1... | collective-permute-start | bytes 393224 | tf_op jit(solution)/shard_map/ppermute | solution.py:235
  19.6 8.2 %collective-permute-start.8 = (f32[2,2,64,128]{3,2,1,0:T(8,128)S(1)}, f32[2,2,64,128]{3,2,1,0:T(8,128)S(1)}, u32[]{:S(2)}, u32[]{:S(2)}) collective-permute-start(f32[2,2,64,128]{3,2,1,0:T(8,128)S(1)} %get-tuple-element.34), channel_id=1, source_target_pairs={{0,1},{1,0},{2,3},{3,2},{4,5},{5,4},{6,7},{7,6},{8,9},{9,8},{10,11... | collective-permute-start | bytes 393224 | tf_op jit(solution)/shard_map/ppermute | solution.py:221
  19.7 8.7 %collective-permute-start.11 = (f32[2,2,64,128]{3,2,1,0:T(8,128)S(1)}, f32[2,2,64,128]{3,2,1,0:T(8,128)S(1)}, u32[]{:S(2)}, u32[]{:S(2)}) collective-permute-start(f32[2,2,64,128]{3,2,1,0:T(8,128)S(1)} %add.10), channel_id=1, source_target_pairs={{0,2},{1,3},{2,0},{3,1},{4,6},{5,7},{6,4},{7,5},{8,10},{9,11},{10,... | collective-permute-start | bytes 393224 | tf_op jit(solution)/shard_map/ppermute | solution.py:235
  20.7 9.1 %collective-permute-start.13 = (f32[2,2,64,128]{3,2,1,0:T(8,128)S(1)}, f32[2,2,64,128]{3,2,1,0:T(8,128)S(1)}, u32[]{:S(2)}, u32[]{:S(2)}) collective-permute-start(f32[2,2,64,128]{3,2,1,0:T(8,128)S(1)} %add.11), channel_id=1, source_target_pairs={{0,4},{1,5},{2,6},{3,7},{4,8},{5,9},{6,10},{7,11},{8,12},{9,13},{1... | collective-permute-start | bytes 393224 | tf_op jit(solution)/shard_map/ppermute | solution.py:235
